TPU v7x, 32 devices: a whole 2x2x4 slice. The times are simulated.
32 devices in a mesh: wide: 8 (over z, y), narrow: 4 (over x, core).
Axes of the slice: x: 2, y: 2, z: 4, core: 2. Of those that a mesh axis runs over, the one named last changes fastest.
Arguments:
- tokens: bfloat16 [32768, 768], P(('wide', 'narrow')), may hold values from -6 to 6
- grad_out: bfloat16 [32768, 768], P(('wide', 'narrow')), may hold values from -6 to 6
- routes: int32 [32768, 1], P(('wide', 'narrow')), may hold values from 0 to 7; in each aligned block of 1024 rows (0 to 1023, 1024 to 2047, ...) at most 256 rows name the same one
- group_counts: int32 [8], replicated, may hold values from 1 to 8, 32 in all
- group_weights: int32 [8], replicated, may hold values from 1 to 4
- norm1_gain: float32 [768], replicated, may hold values from 0.5 to 1.5
- norm1_bias: float32 [768], replicated, may hold values from -1.25 to 1.25
- w_query: bfloat16 [768, 768], replicated, may hold values from -0.4375 to 0.4375
- bias_query: float32 [768], replicated, may hold values from -3 to 3
- w_key: bfloat16 [768, 768], replicated, may hold values from -0.21875 to 0.21875
- w_value: bfloat16 [768, 768], replicated, may hold values from -0.21875 to 0.21875
- bias_value: float32 [768], replicated, may hold values from -1.75 to 1.75
- w_out: bfloat16 [768, 768], replicated, may hold values from -0.875 to 0.875
- bias_out: float32 [768], replicated, may hold values from -1.75 to 1.75
- norm2_gain: float32 [768], replicated, may hold values from 0.5 to 1.5
- norm2_bias: float32 [768], replicated, may hold values from -1.25 to 1.25
- router: bfloat16 [768, 8], replicated, may hold values from -0.21875 to 0.21875
- w_in: bfloat16 [8, 768, 3072], P('wide', None, 'narrow'), may hold values from -0.21875 to 0.21875
- bias_in: bfloat16 [8, 3072], P('wide', 'narrow'), may hold values from -1.75 to 1.75
- w_down: bfloat16 [8, 3072, 768], P('wide', 'narrow'), may hold values from -0.4375 to 0.4375
- bias_down: bfloat16 [8, 768], P('wide'), may hold values from -1.75 to 1.75
Outputs:
- block_out: bfloat16 [32768, 768], P(('wide', 'narrow'))
- balance_loss: float32 [], replicated
- grad_tokens: bfloat16 [32768, 768], P(('wide', 'narrow'))
- grad_norm1_gain: float32 [768], replicated
- grad_norm1_bias: float32 [768], replicated
- grad_w_query: float32 [768, 768], replicated
- grad_bias_query: float32 [768], replicated
- grad_w_key: float32 [768, 768], replicated
- grad_w_value: float32 [768, 768], replicated
- grad_bias_value: float32 [768], replicated
- grad_w_out: float32 [768, 768], replicated
- grad_bias_out: float32 [768], replicated
- grad_norm2_gain: float32 [768], replicated
- grad_norm2_bias: float32 [768], replicated
- grad_router: float32 [768, 8], replicated
- grad_w_in: float32 [8, 768, 3072], P('wide', None, 'narrow')
- grad_bias_in: float32 [8, 3072], P('wide', 'narrow')
- grad_w_down: float32 [8, 3072, 768], P('wide', 'narrow')
- grad_bias_down: float32 [8, 768], P('wide', 'narrow')
Inputs may be any that keep to these rules, and one draw needn't show every extreme that they name: `routes`: among the 1024 tokens of one device at most 256 name the same expert, and in every draw some device has an expert named by exactly 256 of its tokens. The counts add up to 32; group g holds the next group_counts[g] sequences in order.
All inputs are finite; a program needn't handle non-finite values.
Results may differ from a plain program's by a relative error of at most 0.015.
Values may be sent and summed in bfloat16 or wider, within the bound.
No kernel may reach another device: no remote copies, remote signals or barrier semaphores. Data moves between devices by JAX's collectives and lax.ppermute only.
A program may use at most 384 MiB of HBM per device.

v0:
```python
import jax
import jax.numpy as jnp
from jax import lax
from jax.sharding import PartitionSpec as P

HEADS = 12
HEAD_DIM = 64
SEQ_LEN = 1024


EPS = 1e-05
BALANCE = 48.0
NEGATIVE = -1e30


def layer_norm(values, norm_gain, norm_shift):
    centred = values - jnp.mean(values, axis=-1, keepdims=True)
    spread = lax.rsqrt(jnp.mean(centred * centred, axis=-1, keepdims=True) + EPS)
    return centred * spread * norm_gain + norm_shift


def exact_gelu(values):
    return jax.nn.gelu(values, approximate=False)


def masked_scores(query_block, key_heads, first_row):
    scores = (
        jnp.einsum("qhe,khe->hqk", query_block, key_heads, preferred_element_type=jnp.float32)
        * 0.125
    )
    row_ids = first_row + lax.broadcasted_iota(jnp.int32, scores.shape, 1)
    col_ids = lax.broadcasted_iota(jnp.int32, scores.shape, 2)
    return jnp.where(col_ids <= row_ids, scores, NEGATIVE)


def attend_sequence(operands):
    queries, key_heads, values = operands
    length = queries.shape[0]
    block_rows = min(512, length)
    contexts = []
    log_totals = []
    for first_row in range(0, length, block_rows):
        scores = masked_scores(queries[first_row : first_row + block_rows], key_heads, first_row)
        row_peak = jnp.max(scores, axis=-1, keepdims=True)
        exponent = jnp.exp(scores - row_peak)
        row_total = jnp.sum(exponent, axis=-1, keepdims=True)
        weights = (exponent / row_total).astype(jnp.bfloat16)
        contexts.append(
            jnp.einsum("hqk,khe->qhe", weights, values, preferred_element_type=jnp.float32)
        )
        log_totals.append((row_peak + jnp.log(row_total))[:, :, 0])
    return (jnp.concatenate(contexts, 0), jnp.concatenate(log_totals, 1))


def attend_backward(operands):
    queries, key_heads, values, log_totals, grad_context = operands
    length = queries.shape[0]
    block_rows = min(512, length)
    grad_query_parts = []
    grad_keys = jnp.zeros(key_heads.shape, jnp.float32)
    grad_values = jnp.zeros(values.shape, jnp.float32)
    for first_row in range(0, length, block_rows):
        query_block = queries[first_row : first_row + block_rows]
        grad_block = grad_context[first_row : first_row + block_rows]
        scores = masked_scores(query_block, key_heads, first_row)
        soft_probs = jnp.exp(scores - log_totals[:, first_row : first_row + block_rows, None])
        weights = soft_probs.astype(jnp.bfloat16)
        grad_probs = jnp.einsum(
            "qhe,khe->hqk", grad_block, values, preferred_element_type=jnp.float32
        )
        row_inner = jnp.sum(soft_probs * grad_probs, axis=-1, keepdims=True)
        grad_scores = (soft_probs * (grad_probs - row_inner)).astype(jnp.bfloat16)
        grad_query_parts.append(
            jnp.einsum("hqk,khe->qhe", grad_scores, key_heads, preferred_element_type=jnp.float32)
            * 0.125
        )
        grad_keys = (
            grad_keys
            + jnp.einsum(
                "hqk,qhe->khe", grad_scores, query_block, preferred_element_type=jnp.float32
            )
            * 0.125
        )
        grad_values = grad_values + jnp.einsum(
            "hqk,qhe->khe", weights, grad_block, preferred_element_type=jnp.float32
        )
    return (jnp.concatenate(grad_query_parts, 0), grad_keys, grad_values)


def to_rows(blocks, wide_count, local_experts):
    capacity, model_width = (blocks.shape[1], blocks.shape[2])
    shaped = blocks.reshape(wide_count, local_experts, capacity, model_width)
    return shaped.transpose(0, 2, 1, 3).reshape(wide_count * capacity, local_experts, model_width)


def to_blocks(row_sets, wide_count):
    total_rows, local_experts, model_width = row_sets.shape
    capacity = total_rows // wide_count
    shaped = row_sets.reshape(wide_count, capacity, local_experts, model_width)
    return shaped.transpose(0, 2, 1, 3).reshape(wide_count * local_experts, capacity, model_width)


def per_device(
    tokens,
    grad_out,
    routes,
    group_counts,
    group_weights,
    norm1_gain,
    norm1_bias,
    w_query,
    bias_query,
    w_key,
    w_value,
    bias_value,
    w_out,
    bias_out,
    norm2_gain,
    norm2_bias,
    router,
    w_in,
    bias_in,
    w_down,
    bias_down,
):
    tok_rows, model_width = tokens.shape
    seq_dev = tok_rows // SEQ_LEN
    experts = router.shape[1]
    local_experts = w_in.shape[0]
    wide_count = lax.axis_size("wide")
    narrow_count = lax.axis_size("narrow")
    capacity = 2 * tok_rows // experts
    total_tokens = tok_rows * wide_count * narrow_count
    seq_total = seq_dev * wide_count * narrow_count
    group_total = group_counts.shape[0]
    head_shape = (seq_dev, SEQ_LEN, HEADS, HEAD_DIM)
    share_cols = model_width // narrow_count
    device_index = lax.axis_index(("wide", "narrow"))
    seq_ids = device_index * seq_dev + lax.broadcasted_iota(jnp.int32, (tok_rows, 1), 0) // SEQ_LEN
    group_ends = jnp.cumsum(group_counts, dtype=jnp.int32)
    group_starts = group_ends - group_counts
    member = ((seq_ids >= group_starts[None, :]) & (seq_ids < group_ends[None, :])).astype(
        jnp.float32
    )
    factor = (
        group_weights.astype(jnp.float32)
        * seq_total
        / (group_total * group_counts.astype(jnp.float32))
    )
    token_weight = jnp.sum(member * factor[None, :], axis=1, keepdims=True)
    inputs = tokens.astype(jnp.float32)
    normed = layer_norm(inputs, norm1_gain, norm1_bias).astype(jnp.bfloat16)
    queries = (jnp.dot(normed, w_query, preferred_element_type=jnp.float32) + bias_query).astype(
        jnp.bfloat16
    )
    key_heads = jnp.dot(normed, w_key, preferred_element_type=jnp.float32).astype(jnp.bfloat16)
    values = (jnp.dot(normed, w_value, preferred_element_type=jnp.float32) + bias_value).astype(
        jnp.bfloat16
    )
    query_heads = queries.reshape(head_shape)
    key_split = key_heads.reshape(head_shape)
    value_heads = values.reshape(head_shape)
    contexts, log_totals = lax.map(attend_sequence, (query_heads, key_split, value_heads))
    context = contexts.reshape(tok_rows, model_width).astype(jnp.bfloat16)
    hidden = inputs + jnp.dot(context, w_out, preferred_element_type=jnp.float32) + bias_out
    moe_in = layer_norm(hidden, norm2_gain, norm2_bias).astype(jnp.bfloat16)
    logits = jnp.dot(moe_in, router, preferred_element_type=jnp.float32)
    expert_ids = routes[:, 0]
    picked = expert_ids[:, None] == lax.broadcasted_iota(jnp.int32, (1, experts), 1)
    chosen = picked.astype(jnp.float32)
    gate_value = jax.nn.sigmoid(jnp.sum(logits * chosen, axis=1))
    router_probs = jax.nn.softmax(logits, axis=1)
    counted, prob_sums = lax.psum(
        (jnp.sum(chosen, axis=0), jnp.sum(router_probs, axis=0)), ("wide", "narrow")
    )
    fraction = counted / total_tokens
    balance_loss = experts * jnp.sum(fraction * (prob_sums / total_tokens))
    rank_flags = picked.astype(jnp.int32)
    position = jnp.sum(
        (jnp.cumsum(rank_flags, axis=0, dtype=jnp.int32) - rank_flags) * rank_flags, axis=1
    )
    slot_ids = expert_ids * capacity + position
    outgoing = jnp.zeros((experts * capacity, model_width), jnp.bfloat16).at[slot_ids].set(moe_in)
    incoming = lax.all_to_all(
        outgoing.reshape(experts, capacity, model_width),
        "wide",
        split_axis=0,
        concat_axis=0,
        tiled=True,
    )
    expert_rows = to_rows(incoming, wide_count, local_experts)
    gathered = lax.all_gather(expert_rows, "narrow", axis=0, tiled=True)
    pre_act = (
        jnp.einsum("red,edf->ref", gathered, w_in, preferred_element_type=jnp.float32)
        + bias_in.astype(jnp.float32)[None]
    )
    activated = exact_gelu(pre_act).astype(jnp.bfloat16)
    row_piece = activated
    partial_out = lax.psum_scatter(
        jnp.einsum("ref,efd->red", row_piece, w_down, preferred_element_type=jnp.float32).astype(
            jnp.bfloat16
        ),
        "narrow",
        scatter_dimension=0,
        tiled=True,
    ).astype(jnp.float32)
    expert_out = (partial_out + bias_down.astype(jnp.float32)[None]).astype(jnp.bfloat16)
    returned = lax.all_to_all(
        to_blocks(expert_out, wide_count), "wide", split_axis=0, concat_axis=0, tiled=True
    )
    returned_rows = returned.reshape(experts * capacity, model_width)[slot_ids].astype(jnp.float32)
    block_out = (hidden + gate_value[:, None] * returned_rows).astype(jnp.bfloat16)
    upstream = token_weight * grad_out.astype(jnp.float32)
    grad_gate = jnp.sum(upstream * returned_rows, axis=1)
    grad_expert = (upstream * gate_value[:, None]).astype(jnp.bfloat16)
    grad_outgoing = (
        jnp.zeros((experts * capacity, model_width), jnp.bfloat16).at[slot_ids].set(grad_expert)
    )
    grad_incoming = lax.all_to_all(
        grad_outgoing.reshape(experts, capacity, model_width),
        "wide",
        split_axis=0,
        concat_axis=0,
        tiled=True,
    )
    grad_rows = to_rows(grad_incoming, wide_count, local_experts)
    grad_gathered = lax.all_gather(grad_rows, "narrow", axis=0, tiled=True)
    grad_act = jnp.einsum("red,efd->ref", grad_gathered, w_down, preferred_element_type=jnp.float32)
    _, gelu_pull = jax.vjp(exact_gelu, pre_act)
    grad_pre = gelu_pull(grad_act)[0].astype(jnp.bfloat16)
    grad_w_down = jnp.einsum(
        "ref,red->efd", activated, grad_gathered, preferred_element_type=jnp.float32
    )
    down_sums = jnp.sum(grad_gathered, axis=0, dtype=jnp.float32)
    grad_bias_down = lax.dynamic_slice_in_dim(
        down_sums, lax.axis_index("narrow") * share_cols, share_cols, 1
    )
    grad_w_in = jnp.einsum("red,ref->edf", gathered, grad_pre, preferred_element_type=jnp.float32)
    grad_bias_in = jnp.sum(grad_pre, axis=0, dtype=jnp.float32)
    row_piece = grad_pre
    grad_back = lax.psum_scatter(
        jnp.einsum("ref,edf->red", row_piece, w_in, preferred_element_type=jnp.float32),
        "narrow",
        scatter_dimension=0,
        tiled=True,
    ).astype(jnp.bfloat16)
    grad_returned = lax.all_to_all(
        to_blocks(grad_back, wide_count), "wide", split_axis=0, concat_axis=0, tiled=True
    )
    grad_moe_expert = grad_returned.reshape(experts * capacity, model_width)[slot_ids].astype(
        jnp.float32
    )
    balance_grad = BALANCE * experts * fraction
    softmax_grad = router_probs * (
        balance_grad[None, :] - jnp.sum(router_probs * balance_grad[None, :], axis=1, keepdims=True)
    )
    gate_slope = grad_gate * gate_value * (1.0 - gate_value)
    grad_logits = (softmax_grad + chosen * gate_slope[:, None]).astype(jnp.bfloat16)
    grad_router = jnp.einsum("td,te->de", moe_in, grad_logits, preferred_element_type=jnp.float32)
    grad_moe = (
        jnp.einsum("te,de->td", grad_logits, router, preferred_element_type=jnp.float32)
        + grad_moe_expert
    )
    _, second_pull = jax.vjp(layer_norm, hidden, norm2_gain, norm2_bias)
    grad_hidden_norm, grad_norm2_gain, grad_norm2_bias = second_pull(grad_moe)
    grad_hidden = upstream + grad_hidden_norm
    grad_branch = grad_hidden.astype(jnp.bfloat16)
    grad_bias_out = jnp.sum(grad_branch, axis=0, dtype=jnp.float32)
    grad_w_out = jnp.einsum("td,te->de", context, grad_branch, preferred_element_type=jnp.float32)
    grad_context = jnp.einsum(
        "te,de->td", grad_branch, w_out, preferred_element_type=jnp.float32
    ).astype(jnp.bfloat16)
    grad_query_heads, grad_key_heads, grad_value_heads = lax.map(
        attend_backward,
        (query_heads, key_split, value_heads, log_totals, grad_context.reshape(head_shape)),
    )
    grad_queries = grad_query_heads.reshape(tok_rows, model_width).astype(jnp.bfloat16)
    grad_keys = grad_key_heads.reshape(tok_rows, model_width).astype(jnp.bfloat16)
    grad_values = grad_value_heads.reshape(tok_rows, model_width).astype(jnp.bfloat16)
    grad_w_query = jnp.einsum("td,te->de", normed, grad_queries, preferred_element_type=jnp.float32)
    grad_bias_query = jnp.sum(grad_queries, axis=0, dtype=jnp.float32)
    grad_w_key = jnp.einsum("td,te->de", normed, grad_keys, preferred_element_type=jnp.float32)
    grad_w_value = jnp.einsum("td,te->de", normed, grad_values, preferred_element_type=jnp.float32)
    grad_bias_value = jnp.sum(grad_values, axis=0, dtype=jnp.float32)
    grad_normed = jnp.einsum("te,de->td", grad_queries, w_query, preferred_element_type=jnp.float32)
    grad_normed = grad_normed + jnp.einsum(
        "te,de->td", grad_keys, w_key, preferred_element_type=jnp.float32
    )
    grad_normed = grad_normed + jnp.einsum(
        "te,de->td", grad_values, w_value, preferred_element_type=jnp.float32
    )
    _, first_pull = jax.vjp(layer_norm, inputs, norm1_gain, norm1_bias)
    grad_inputs, grad_norm1_gain, grad_norm1_bias = first_pull(grad_normed)
    grad_tokens = (grad_hidden + grad_inputs).astype(jnp.bfloat16)
    summed = lax.psum(
        (
            grad_norm1_gain,
            grad_norm1_bias,
            grad_w_query,
            grad_bias_query,
            grad_w_key,
            grad_w_value,
            grad_bias_value,
            grad_w_out,
            grad_bias_out,
            grad_norm2_gain,
            grad_norm2_bias,
            grad_router,
        ),
        ("wide", "narrow"),
    )
    return (
        block_out,
        balance_loss,
        grad_tokens,
        summed[0],
        summed[1],
        summed[2],
        summed[3],
        summed[4],
        summed[5],
        summed[6],
        summed[7],
        summed[8],
        summed[9],
        summed[10],
        summed[11],
        grad_w_in,
        grad_bias_in,
        grad_w_down,
        grad_bias_down,
    )


def solution(mesh):
    return jax.shard_map(
        per_device,
        mesh=mesh,
        in_specs=(
            P(("wide", "narrow"), None),
            P(("wide", "narrow"), None),
            P(("wide", "narrow"), None),
            P(),
            P(),
            P(),
            P(),
            P(),
            P(),
            P(),
            P(),
            P(),
            P(),
            P(),
            P(),
            P(),
            P(),
            P("wide", None, "narrow"),
            P("wide", "narrow"),
            P("wide", "narrow", None),
            P("wide", None),
        ),
        out_specs=(
            P(("wide", "narrow"), None),
            P(),
            P(("wide", "narrow"), None),
            P(),
            P(),
            P(),
            P(),
            P(),
            P(),
            P(),
            P(),
            P(),
            P(),
            P(),
            P(),
            P("wide", None, "narrow"),
            P("wide", "narrow"),
            P("wide", "narrow", None),
            P("wide", "narrow"),
        ),
        check_vma=False,
    )
```

profile of v0, /device:TPU:0, one launch (start us, length us, event | category | flops | bytes accessed | tf_op | source)
XLA Modules:
  0.0 1468.5 jit_solution(7834594140973677743)
XLA Ops:
  8.1 2.3 reduce-window.18
  12.3 1.7 copy.50
  14.8 3.0 convolution_convert_fusion.2
  19.7 1.6 add_convert_fusion.5
  21.3 10.6 fusion.120
  32.0 11.0 fusion.119
  42.9 11.1 fusion.24
  54.1 10.4 fusion.80
  64.5 10.9 fusion.23
  75.4 10.5 fusion.79
  86.2 1.7 fusion.121
  90.8 1.6 copy.51
  92.5 7.9 scatter_custom_fusion
  100.3 78.1 %all_to_all.20 = bf16[8,256,768]{2,1,0:T(8,128)(2,1)} all-to-all(bf16[8,256,768]{2,1,0:T(8,128)(2,1)} %bitcast.300), channel_id=1, replica_groups=mesh['wide'=8,'narrow'=4] {'wide'}, dimensions={0} | all-to-all | bytes 6291456 | tf_op jit(solution)/shard_map/all_to_all | solution.py:184
  178.5 81.2 %all-gather.3.cloned.1.call-done = bf16[8192,1,768]{2,0,1:T(8,128)(2,1)} async-done(((bf16[2048,1,768]{2,0,1:T(8,128)(2,1)}), bf16[8192,1,768]{2,0,1:T(8,128)(2,1)}) %all-gather.3.cloned.1.call-update) | async-done | bytes 12582928 | tf_op jit(solution)/shard_map/all_gather | solution.py:192
  259.7 18.1 %fusion.40 = f32[8192,768]{1,0:T(8,128)} fusion(bf16[8192,1,768]{2,0,1:T(8,128)(2,1)} %all-gather.3.cloned.1.call-done, bf16[1,768,768]{2,1,0:T(8,128)(2,1)} %param.38), kind=kOutput, calls=%fused_computation.70 | convolution fusion | flops 9663676416 | bytes 38928384 | tf_op jit(solution)/shard_map/red,edf->ref/dot_general | solution.py:194
  277.9 67.5 %fusion.46 = bf16[8192,1,768]{2,0,1:T(8,128)(2,1)} fusion(bf16[1,768,768]{2,1,0:T(8,128)(2,1)S(1)} %copy-done, f32[8192,768]{1,0:T(8,128)} %fusion.40, f32[768]{0:T(1024)S(1)} %convert_reduce_fusion.8), kind=kOutput, calls=%fused_computation.76 | convolution fusion | flops 10085203968 | bytes 38931456 | tf_op jit(solution)/shard_map/ref,efd->red/dot_general | solution.py:200
  346.1 98.5 %reduce-scatter.3.cloned.1.call-done = bf16[2048,1,768]{2,0,1:T(8,128)(2,1)} async-done(((bf16[8192,1,768]{2,0,1:T(8,128)(2,1)}), bf16[2048,1,768]{2,0,1:T(8,128)(2,1)}) %reduce-scatter.3.cloned.1.call-update) | async-done | bytes 3145744 | tf_op jit(solution)/shard_map/reduce_scatter | solution.py:199
  444.6 4.1 add_convert_fusion
  448.7 5.7 all-to-all-start.1
  454.6 90.7 %psum.98 = f32[8]{0:T(128)S(1)} all-reduce(f32[8]{0:T(128)S(1)} %convert_reduce_fusion.6), channel_id=1, replica_groups=mesh['wide'=8,'narrow'=4] {'wide','narrow'}, use_global_device_ids=true, to_apply=%region_15.16 | all-reduce | flops 8 | bytes 64 | tf_op jit(solution)/shard_map/psum | solution.py:173
  545.4 2.6 copy.53
  550.8 8.0 gather_fusion
  558.8 2.6 copy.52
  561.4 3.8 fusion.58
  565.2 1.7 copy.54
  567.0 7.4 scatter_custom_fusion.1
  574.4 74.7 %all_to_all.21 = bf16[8,256,768]{2,1,0:T(8,128)(2,1)} all-to-all(bf16[8,256,768]{2,1,0:T(8,128)(2,1)} %bitcast.299), channel_id=1, replica_groups=mesh['wide'=8,'narrow'=4] {'wide'}, dimensions={0} | all-to-all | bytes 6291456 | tf_op jit(solution)/shard_map/all_to_all | solution.py:219
  649.2 81.0 %all-gather.5.cloned.1.call-done = bf16[8192,1,768]{2,0,1:T(8,128)(2,1)} async-done(((bf16[2048,1,768]{2,0,1:T(8,128)(2,1)}), bf16[8192,1,768]{2,0,1:T(8,128)(2,1)}) %all-gather.5.cloned.1.call-update) | async-done | bytes 12582928 | tf_op jit(solution)/shard_map/all_gather | solution.py:227
  730.2 70.5 %convert_reduce_fusion.1 = (f32[768]{0:T(1024)}, bf16[8192,1,768]{2,0,1:T(8,128)(2,1)}) fusion(f32[768]{0:T(1024)S(1)} %convert_reduce_fusion.8, f32[8192,768]{1,0:T(8,128)} %fusion.40, bf16[1,768,768]{2,1,0:T(8,128)(2,1)S(1)} %copy-done, bf16[8192,1,768]{2,0,1:T(8,128)(2,1)} %all-gather.5.cloned.1.call-done), kind=kOutput, calls=%fused_computation.24 | convolution fusion | flops 10135534592 | bytes 51517440 | tf_op jit(solution)/shard_map/red,efd->ref/dot_general | solution.py:228
  800.7 18.4 %convolution_bitcast_fusion = f32[8192,1,768]{2,0,1:T(8,128)} fusion(bf16[8192,1,768]{2,0,1:T(8,128)(2,1)} %get-tuple-element.126, bf16[1,768,768]{2,1,0:T(8,128)(2,1)S(1)} %copy-done.106), kind=kOutput, calls=%fused_computation.57 | convolution fusion | flops 9663676416 | bytes 38928384 | tf_op jit(solution)/shard_map/ref,edf->red/dot_general | solution.py:242
  822.4 177.5 %reduce-scatter.5.cloned.1.call-done = f32[2048,1,768]{2,0,1:T(8,128)} async-done(((f32[8192,1,768]{2,0,1:T(8,128)}), f32[2048,1,768]{2,0,1:T(8,128)}) %reduce-scatter.5.cloned.1.call-update) | async-done | bytes 6291472 | tf_op jit(solution)/shard_map/reduce_scatter | solution.py:241
  999.9 4.7 convert_element_type.191
  1004.6 5.5 all-to-all-start.3
  1010.2 66.7 %fusion.65 = f32[1,768,768]{2,1,0:T(8,128)} fusion(bf16[8192,1,768]{2,0,1:T(8,128)(2,1)} %all-gather.5.cloned.1.call-done, f32[8192,768]{1,0:T(8,128)} %fusion.40, f32[768]{0:T(1024)S(1)} %convert_reduce_fusion.8), kind=kOutput, calls=%fused_computation.119 | convolution fusion | flops 10078912512 | bytes 40111104 | tf_op jit(solution)/shard_map/ref,red->efd/dot_general | solution.py:231
  1077.5 6.3 convert_reduce_fusion
  1084.5 7.9 gather_fusion.1
  1092.4 2.7 copy.55
  1095.2 4.6 multiply_reduce_fusion.2
  1099.9 2.3 fusion.116
  1104.7 2.8 fusion.124
  1109.1 19.7 %multiply_reduce_fusion.1 = (f32[12,512]{1,0:T(8,128)S(1)}, f32[12,512,1024]{2,1,0:T(8,128)}) fusion(f32[12,512,1024]{2,1,0:T(8,128)} %get-tuple-element.143, f32[12,512]{1,0:T(8,128)S(1)} %copy-done.39, bf16[512,12,64]{0,2,1:T(8,128)(2,1)S(1)} %bitcast.303, bf16[1024,12,64]{0,2,1:T(8,128)(2,1)S(1)} %bitcast.309), kind=kOutput, calls=%fused_computation.29 | convolution fusion | flops 824174592 | bytes 52740096 | tf_op jit(solution)/shard_map/while/body/eval_jaxpr/qhe,khe->hqk/dot_general | solution.py:68
  1128.8 21.7 %multiply_convert_fusion.1 = bf16[12,512,1024]{2,1,0:T(8,128)(2,1)} fusion(f32[12,512,1024]{2,1,0:T(8,128)} %get-tuple-element.152, f32[12,512,1024]{2,1,0:T(8,128)} %get-tuple-element.143, f32[12,512]{1,0:T(8,128)S(1)} %get-tuple-element.151, f32[12,512]{1,0:T(8,128)S(1)} %copy-done.39), kind=kLoop, calls=%fused_computation.28 | loop fusion | flops 25165824 | bytes 62963712 | tf_op jit(solution)/shard_map/while/body/eval_jaxpr/convert_element_type | solution.py:72
  1150.5 9.5 multiply_bitcast_fusion.1
  1160.0 8.6 fusion.123
  1168.5 12.2 fusion.27
  1180.7 19.7 %multiply_reduce_fusion = (f32[12,512]{1,0:T(8,128)S(1)}, f32[12,512,1024]{2,1,0:T(8,128)}) fusion(f32[12,512,1024]{2,1,0:T(8,128)} %get-tuple-element.141, f32[12,512]{1,0:T(8,128)S(1)} %copy-done.40, bf16[512,12,64]{0,2,1:T(8,128)(2,1)S(1)} %bitcast.306, bf16[1024,12,64]{0,2,1:T(8,128)(2,1)S(1)} %bitcast.310), kind=kOutput, calls=%fused_computation.26 | convolution fusion | flops 824174592 | bytes 52740096 | tf_op jit(solution)/shard_map/while/body/eval_jaxpr/qhe,khe->hqk/dot_general | solution.py:68
  1200.4 11.7 convert_reduce_fusion.4
  1212.2 3.0 fusion.104
  1215.2 21.8 %multiply_convert_fusion = bf16[12,512,1024]{2,1,0:T(8,128)(2,1)} fusion(f32[12,512,1024]{2,1,0:T(8,128)} %get-tuple-element.150, f32[12,512,1024]{2,1,0:T(8,128)} %get-tuple-element.141, f32[12,512]{1,0:T(8,128)S(1)} %get-tuple-element.149, f32[12,512]{1,0:T(8,128)S(1)} %copy-done.40), kind=kLoop, calls=%fused_computation.25 | loop fusion | flops 25165824 | bytes 62963712 | tf_op jit(solution)/shard_map/while/body/eval_jaxpr/convert_element_type | solution.py:72
  1237.0 8.7 multiply_bitcast_fusion
  1245.7 6.9 multiply_convert_fusion.2
  1252.9 3.0 fusion.108
  1256.0 3.0 fusion.106
  1259.0 16.6 %fusion.68 = f32[1,768,768]{2,1,0:T(8,128)} fusion(bf16[8192,1,768]{2,0,1:T(8,128)(2,1)} %get-tuple-element.126, bf16[8192,1,768]{2,0,1:T(8,128)(2,1)} %all-gather.3.cloned.1.call-done), kind=kOutput, calls=%fused_computation.120 | convolution fusion | flops 9663676416 | bytes 27525120 | tf_op jit(solution)/shard_map/red,ref->edf/dot_general | solution.py:238
  1275.8 2.9 fusion.125
  1278.7 2.9 fusion.126
  1281.8 1.9 fusion.113
  1286.7 42.4 %all-reduce = (f32[8]{0:T(128)S(1)}, f32[768]{0:T(1024)}, f32[768]{0:T(1024)}, f32[768]{0:T(1024)}, f32[768]{0:T(1024)}, /*index=5*/f32[768]{0:T(1024)}, f32[768]{0:T(1024)}, f32[768]{0:T(1024)}, f32[768,8]{0,1:T(8,128)}) all-reduce(f32[8]{0:T(128)S(1)} %copy-done.105, ...), channel_id=1, replica_groups=mesh['wide'=8,'narrow'=4] {'wide','narrow'}, use_global_device_ids=true, to_apply=%region_19.20 | all-reduce | flops 11528 | bytes 92224 | tf_op jit(solution)/shard_map/psum | solution.py:173
  1329.2 2.6 copy.60
  1331.8 6.1 add_convert_fusion.1
  1337.9 2.6 copy.61
  1341.8 111.0 %all-reduce.4.cloned.1.call-done = (f32[768,768]{1,0:T(8,128)}, f32[768,768]{1,0:T(8,128)}, f32[768,768]{1,0:T(8,128)}, f32[768,768]{1,0:T(8,128)}) async-done(((f32[768,768]{1,0:T(8,128)}, f32[768,768]{1,0:T(8,128)}, f32[768,768]{1,0:T(8,128)}, f32[768,768]{1,0:T(8,128)}), (f32[768,768]{1,0:T(8,128)}, f32[768,768]{1,0:T(8,128)}, f32[768,768]{1,0:T(8,128)}, ...) | async-done | bytes 9437200 | tf_op jit(solution)/shard_map/psum | solution.py:295
  1452.8 3.4 copy.72
  (307 shorter events, 29.2 us)
Async XLA Ops:
  7.2 270.7 %copy-start = (bf16[1,768,768]{2,1,0:T(8,128)(2,1)S(1)}, bf16[1,768,768]{2,1,0:T(8,128)(2,1)}, u32[]{:S(2)}) copy-start(bf16[1,768,768]{2,1,0:T(8,128)(2,1)} %param.40) | copy-start | bytes 3538948
  7.2 7.6 copy-start.72
  7.2 7.6 copy-start.115
  7.2 252.5 %all-gather.3.cloned.1.call-start = ((), (), s32[]{:S(2)}) async-start(), calls=%async_computation.6 | async-start | bytes 15728640 | tf_op jit(solution)/shard_map/all_gather | solution.py:192
  12.3 80.2 %copy-start.94 = (s32[1024,1]{0,1:T(1,128)}, s32[1024,1]{0,1:T(1,128)S(1)}, u32[]{:S(2)}) copy-start(s32[1024,1]{0,1:T(1,128)S(1)} %compare_select_fusion) | copy-start | bytes 12292
  14.0 72.2 %copy-start.2 = (bf16[1024,768]{0,1:T(8,128)(2,1)}, bf16[1024,768]{0,1:T(8,128)(2,1)S(1)}, u32[]{:S(2)}) copy-start(bf16[1024,768]{0,1:T(8,128)(2,1)S(1)} %copy.50) | copy-start | bytes 4718596
  17.8 14.2 copy-start.19
  19.7 12.3 copy-start.22
  21.3 54.1 %copy-start.15 = (bf16[1024,768]{0,1:T(8,128)(2,1)}, bf16[1024,768]{0,1:T(8,128)(2,1)S(1)}, u32[]{:S(2)}) copy-start(bf16[1024,768]{0,1:T(8,128)(2,1)S(1)} %add_convert_fusion.5) | copy-start | bytes 4718596
  31.9 43.5 %copy-start.44 = (f32[12,512]{1,0:T(8,128)}, f32[12,512]{1,0:T(8,128)S(1)}, u32[]{:S(2)}) copy-start(f32[12,512]{1,0:T(8,128)S(1)} %get-tuple-element.142) | copy-start | bytes 73732
  42.9 11.1 copy-start.46
  54.0 10.4 copy-start.48
  75.4 10.5 copy-start.50
  75.4 10.8 copy-start.107
  75.4 10.8 copy-start.114
  90.8 87.6 %copy-start.9 = (bf16[1024,768]{0,1:T(8,128)(2,1)}, bf16[1024,768]{0,1:T(8,128)(2,1)S(1)}, u32[]{:S(2)}) copy-start(bf16[1024,768]{0,1:T(8,128)(2,1)S(1)} %add_convert_fusion.3) | copy-start | bytes 4718596
  92.5 86.0 %copy-start.103 = (bf16[1,768]{1,0:T(2,128)(2,1)S(1)}, bf16[1,768]{1,0:T(2,128)(2,1)}, u32[]{:S(2)}) copy-start(bf16[1,768]{1,0:T(2,128)(2,1)} %param.39) | copy-start | bytes 4612
  178.4 266.1 %reduce-scatter.3.cloned.1.call-start = ((), (), s32[]{:S(2)}) async-start(), calls=%async_computation.7 | async-start | bytes 15728640 | tf_op jit(solution)/shard_map/reduce_scatter | solution.py:199
  346.0 108.4 %copy-start.41 = (s32[1024,1]{0,1:T(1,128)S(1)}, s32[1024,1]{0,1:T(1,128)}, u32[]{:S(2)}) copy-start(s32[1024,1]{0,1:T(1,128)} %param.23) | copy-start | bytes 12292
  346.0 199.2 %copy-start.117 = (s32[8]{0:T(128)S(1)}, s32[8]{0:T(128)}, u32[]{:S(2)}) copy-start(s32[8]{0:T(128)} %param.24) | copy-start | bytes 100
  448.7 99.3 %copy-start.10 = (bf16[1024,768]{0,1:T(8,128)(2,1)S(1)}, bf16[1024,768]{0,1:T(8,128)(2,1)}, u32[]{:S(2)}) copy-start(bf16[1024,768]{0,1:T(8,128)(2,1)} %copy-done.9) | copy-start | bytes 4718596
  448.7 99.3 %copy-start.68 = (bf16[768,8]{0,1:T(8,128)(2,1)S(1)}, bf16[768,8]{0,1:T(8,128)(2,1)}, u32[]{:S(2)}) copy-start(bf16[768,8]{0,1:T(8,128)(2,1)} %param.37) | copy-start | bytes 36868
  448.7 99.7 %copy-start.118 = (s32[8]{0:T(128)S(1)}, s32[8]{0:T(128)}, u32[]{:S(2)}) copy-start(s32[8]{0:T(128)} %param.25) | copy-start | bytes 100
  448.7 101.5 %copy-start.95 = (s32[1024,1]{0,1:T(1,128)S(1)}, s32[1024,1]{0,1:T(1,128)}, u32[]{:S(2)}) copy-start(s32[1024,1]{0,1:T(1,128)} %copy-done.94) | copy-start | bytes 12292
  448.7 102.1 %all-to-all-start.1 = ((bf16[8,256,768]{2,1,0:T(8,128)(2,1)}), bf16[8,256,768]{2,1,0:T(8,128)(2,1)}, u32[]{:S(2)}, u32[]{:S(2)}) async-start(bf16[8,256,768]{2,1,0:T(8,128)(2,1)} %bitcast.301), calls=%async_computation.2 | async-start | bytes 6291456 | tf_op jit(solution)/shard_map/all_to_all | solution.py:208
  454.4 275.8 %all-gather.5.cloned.1.call-start = ((), (), s32[]{:S(2)}) async-start(), calls=%async_computation.8 | async-start | bytes 15728640 | tf_op jit(solution)/shard_map/all_gather | solution.py:227
  545.2 13.6 copy-start.119
  548.5 12.9 copy-start.65
  550.2 8.6 copy-start.90
  550.8 10.6 copy-start.88
  550.8 10.6 copy-start.12
  649.1 350.7 %reduce-scatter.5.cloned.1.call-start = ((), (), s32[]{:S(2)}) async-start(), calls=%async_computation.9 | async-start | bytes 31457280 | tf_op jit(solution)/shard_map/reduce_scatter | solution.py:241
  730.2 70.5 %copy-start.106 = (bf16[1,768,768]{2,1,0:T(8,128)(2,1)S(1)}, bf16[1,768,768]{2,1,0:T(8,128)(2,1)}, u32[]{:S(2)}) copy-start(bf16[1,768,768]{2,1,0:T(8,128)(2,1)} %param.38) | copy-start | bytes 3538948
  821.2 183.4 %copy-start.74 = (f32[1024]{0:T(1024)}, f32[1024]{0:T(1024)S(1)}, u32[]{:S(2)}) copy-start(f32[1024]{0:T(1024)S(1)} %subtract_multiply_fusion) | copy-start | bytes 12292
  1004.6 79.8 %all-to-all-start.3 = ((bf16[8,256,768]{2,1,0:T(8,128)(2,1)}), bf16[8,256,768]{2,1,0:T(8,128)(2,1)}, u32[]{:S(2)}, u32[]{:S(2)}) async-start(bf16[8,256,768]{2,1,0:T(8,128)(2,1)} %bitcast.302), calls=%async_computation.5 | async-start | bytes 6291456 | tf_op jit(solution)/shard_map/all_to_all | solution.py:247
  1010.1 442.7 %all-reduce.4.cloned.1.call-start = ((), (), s32[]{:S(2)}) async-start(), calls=%async_computation.10 | async-start | bytes 18874368 | tf_op jit(solution)/shard_map/psum | solution.py:295
  1010.1 66.7 %copy-start.102 = (f32[768]{0:T(1024)S(1)}, f32[768]{0:T(1024)}, u32[]{:S(2)}) copy-start(f32[768]{0:T(1024)} %get-tuple-element.125) | copy-start | bytes 9220
  1084.4 10.7 copy-start.38
  1084.4 10.7 copy-start.43
  1084.4 10.7 copy-start.55
  1084.4 10.7 copy-start.58
  1084.4 10.7 copy-start.61
  1084.5 10.7 copy-start.64
  1084.5 10.7 copy-start.69
  1084.5 10.7 copy-start.71
  1084.5 10.7 copy-start.75
  1084.5 10.7 copy-start.79
  1084.5 10.7 copy-start.100
  1128.8 21.7 %copy-start.20 = (bf16[1024,768]{0,1:T(8,128)(2,1)S(1)}, bf16[1024,768]{0,1:T(8,128)(2,1)}, u32[]{:S(2)}) copy-start(bf16[1024,768]{0,1:T(8,128)(2,1)} %copy-done.19) | copy-start | bytes 4718596
  1150.5 9.5 copy-start.25
  1160.0 8.6 copy-start.40
  1200.4 11.7 copy-start.3
  1200.4 11.7 copy-start.53
  1200.4 11.8 copy-start.73
  1200.4 11.8 copy-start.77
  1200.4 11.8 copy-start.116
  1215.2 21.8 %copy-start.21 = (bf16[1024,768]{0,1:T(8,128)(2,1)S(1)}, bf16[1024,768]{0,1:T(8,128)(2,1)}, u32[]{:S(2)}) copy-start(bf16[1024,768]{0,1:T(8,128)(2,1)} %copy-done.19) | copy-start | bytes 4718596
  1237.0 8.7 copy-start.8
  1237.0 8.7 copy-start.23
  1259.0 16.8 %copy-start.110 = (bf16[768,768]{1,0:T(8,128)(2,1)S(1)}, bf16[768,768]{1,0:T(8,128)(2,1)}, u32[]{:S(2)}) copy-start(bf16[768,768]{1,0:T(8,128)(2,1)} %param.28) | copy-start | bytes 3538948
  1283.7 48.0 %copy-start.67 = (f32[1024]{0:T(1024)S(1)}, f32[1024]{0:T(1024)}, u32[]{:S(2)}) copy-start(f32[1024]{0:T(1024)} %copy-done.65) | copy-start | bytes 12292
  1283.7 48.0 %copy-start.87 = (f32[1024]{0:T(1024)S(1)}, f32[1024]{0:T(1024)}, u32[]{:S(2)}) copy-start(f32[1024]{0:T(1024)} %copy-done.86) | copy-start | bytes 12292
  1331.8 8.7 copy-start.120
  1452.8 7.6 copy-start.1
  (64 other events, 195.0 us)
Sparse Core Ops, SparseCore 0:
  178.6 81.1 all-gather.2
  345.5 99.0 reduce-scatter.2
  649.2 80.9 all-gather.4
  819.4 180.4 reduce-scatter.4
  1259.1 193.5 all-reduce.3
where the time goes:
time: 1480 us; the launch traced here: 1470 us
  waiting for transfers between devices  549 us (37%)
  matrix products  432 us (29%)
  blocking collectives  286 us (19%)
  other arithmetic  105 us (7%)
  local copies, waits for them, and re-layouts  66.9 us (5%)
  between operations  17.5 us (1%)
    reduce_scatter x1, waiting for transfers between devices, per_device(): lax.psum_scatter(jnp.einsum('ref,edf->red', row_piece, w_in, preferred_el...  177 us
    psum x2, blocking collectives, per_device(): lax.psum((jnp.sum(chosen, axis=0), jnp.sum(router_probs, axis=0)), ('wide...  133 us
    psum x1, waiting for transfers between devices, per_device(): lax.psum((grad_norm1_gain, grad_norm1_bias, grad_w_query, grad_bias_query...  111 us
    reduce_scatter x1, waiting for transfers between devices, per_device(): lax.psum_scatter(jnp.einsum('ref,efd->red', row_piece, w_down, preferred_...  98.5 us
    all_gather x1, waiting for transfers between devices, per_device(): gathered = lax.all_gather(expert_rows, 'narrow', axis=0, tiled=True)  81.2 us
    all_gather x1, waiting for transfers between devices, per_device(): grad_gathered = lax.all_gather(grad_rows, 'narrow', axis=0, tiled=True)  81 us
    all_to_all x1, blocking collectives, per_device(): lax.all_to_all(outgoing.reshape(experts, capacity, model_width), 'wide',...  78.1 us
    all_to_all x1, blocking collectives, per_device(): lax.all_to_all(grad_outgoing.reshape(experts, capacity, model_width), 'wi...  74.7 us
  transfers between devices with their start and end apart: 7, of which 5 were waited for; matrix products, arithmetic and copies ran while one was open for 8% of the time, Pallas kernels for 0%

commit v1 on v0

v1 whole, which is shorter than its diff:
```python
import functools
import jax
import jax.numpy as jnp
from jax import lax
from jax.experimental import pallas as pl
from jax.experimental.pallas import tpu as pltpu
from jax.sharding import PartitionSpec as P

HEADS = 12
HEAD_DIM = 64
SEQ_LEN = 1024
EPS = 1e-05
BALANCE = 48.0
NEGATIVE = -1e30
PAIR = 2 * HEAD_DIM
F32 = jnp.float32
BF16 = jnp.bfloat16
VMEM_LIMIT = 56 * 1024 * 1024
EXTRA = 8
ATTEND_CALLS = 2


def mm(left, right):
    return lax.dot_general(left, right, (((1,), (0,)), ((), ())), preferred_element_type=F32)


def mm_nt(left, right):
    return lax.dot_general(left, right, (((1,), (1,)), ((), ())), preferred_element_type=F32)


def mm_tn(left, right):
    return lax.dot_general(left, right, (((0,), (0,)), ((), ())), preferred_element_type=F32)


def cost(flops, nbytes, trans=0):
    return pl.CostEstimate(flops=int(flops), bytes_accessed=int(nbytes), transcendentals=int(trans))


def params(*semantics):
    return pltpu.CompilerParams(dimension_semantics=semantics, vmem_limit_bytes=VMEM_LIMIT)


def head_mask(block, head):
    lanes = lax.broadcasted_iota(jnp.int32, block.shape, 1)
    return jnp.where(lanes // HEAD_DIM == head, block, jnp.zeros_like(block))


def causal(scores, block):
    keys = scores.shape[0]
    first = lax.broadcasted_iota(jnp.int32, (block, block), 0)
    second = lax.broadcasted_iota(jnp.int32, (block, block), 1)
    last = jnp.where(first <= second, scores[keys - block :], NEGATIVE)
    if keys == block:
        return last
    return jnp.concatenate([scores[: keys - block], last], axis=0)


def attend_kernel(block, q_ref, k_ref, v_ref, context_ref, log_ref):
    rows = q_ref.shape[0]
    keys = k_ref[...]
    values_t = jnp.transpose(v_ref[...])
    for first in range(0, rows, block):
        span = first + block
        query = q_ref[first:span, :]
        parts = []
        for head in range(2):
            scores = causal(mm_nt(keys[:span], head_mask(query, head)), block)
            peak = jnp.max(scores, axis=0, keepdims=True)
            powers = jnp.exp(scores - peak)
            total = jnp.sum(powers, axis=0, keepdims=True)
            out = mm(values_t[head * HEAD_DIM : (head + 1) * HEAD_DIM, :span], powers.astype(BF16))
            parts.append(out / total)
            log_ref[0, head : head + 1, first:span] = peak + jnp.log(total)
        context_ref[first:span, :] = jnp.transpose(jnp.concatenate(parts, axis=0)).astype(BF16)


def attend(queries, keys, values, block=256):
    rows, width = queries.shape
    pairs = width // PAIR
    spec = pl.BlockSpec((rows, PAIR), lambda p: (0, p))
    return pl.pallas_call(
        functools.partial(attend_kernel, block),
        grid=(pairs,),
        in_specs=[spec, spec, spec],
        out_specs=[spec, pl.BlockSpec((1, 2, rows), lambda p: (p, 0, 0))],
        out_shape=[
            jax.ShapeDtypeStruct((rows, width), BF16),
            jax.ShapeDtypeStruct((pairs, 2, rows), F32),
        ],
        compiler_params=params("arbitrary"),
        cost_estimate=cost(4 * rows * rows * width * 2, rows * width * 8, pairs * 2 * rows * rows),
        name="attend",
    )(queries, keys, values)


def attend_back_kernel(block, q_ref, k_ref, v_ref, log_ref, g_ref, normed_ref,
                       dq_ref, dk_ref, dv_ref, packed_ref, sums_ref, dq_acc, dk_acc, dv_acc):
    rows = q_ref.shape[0]
    keys = k_ref[...]
    values = v_ref[...]
    keys_t = jnp.transpose(keys)
    for first in reversed(range(0, rows, block)):
        span = first + block
        query = q_ref[first:span, :]
        grad = g_ref[first:span, :]
        grad_query, probs_both, scores_both, query_both, grad_both = [], [], [], [], []
        for head in range(2):
            query_h = head_mask(query, head)
            grad_h = head_mask(grad, head)
            scores = causal(mm_nt(keys[:span], query_h), block)
            probs = jnp.exp(scores - log_ref[0, head : head + 1, first:span])
            grad_probs = mm_nt(values[:span], grad_h)
            inner = jnp.sum(probs * grad_probs, axis=0, keepdims=True)
            grad_scores = (probs * (grad_probs - inner)).astype(BF16)
            grad_query.append(mm(keys_t[head * HEAD_DIM : (head + 1) * HEAD_DIM, :span], grad_scores))
            probs_both.append(probs.astype(BF16))
            scores_both.append(grad_scores)
            query_both.append(query_h)
            grad_both.append(grad_h)
        dv = mm(jnp.concatenate(probs_both, axis=1), jnp.concatenate(grad_both, axis=0))
        dk = mm(jnp.concatenate(scores_both, axis=1), jnp.concatenate(query_both, axis=0))
        if span == rows:
            dv_acc[...] = dv
            dk_acc[...] = dk
        else:
            dv_acc[:span, :] += dv
            dk_acc[:span, :] += dk
        dq = jnp.transpose(jnp.concatenate(grad_query, axis=0)) * 0.125
        dq_acc[first:span, :] = dq.astype(BF16)
    dq = dq_acc[...]
    dk = dk_acc[...].astype(BF16)
    dv = dv_acc[...].astype(BF16)
    dq_ref[...] = dq
    dk_ref[...] = dk
    dv_ref[...] = dv
    normed = normed_ref[...]
    packed_ref[:, : 2 * PAIR] = mm(normed, jnp.concatenate([dq, dk], axis=1)).astype(BF16)
    packed_ref[:, 2 * PAIR :] = mm(normed, dv).astype(BF16)
    sums_ref[...] = jnp.concatenate(
        [
            jnp.sum(dq.astype(F32), axis=0, keepdims=True),
            jnp.sum(dv.astype(F32), axis=0, keepdims=True),
            jnp.zeros((6, PAIR), F32),
        ],
        axis=0,
    )


def attend_back(queries, keys, values, logs, grad_context, normed_t, start, pairs, block=256):
    rows, width = queries.shape
    spec = pl.BlockSpec((rows, PAIR), lambda p: (0, p + start))
    out_spec = pl.BlockSpec((rows, PAIR), lambda p: (0, p))
    return pl.pallas_call(
        functools.partial(attend_back_kernel, block),
        grid=(pairs,),
        in_specs=[
            spec,
            spec,
            spec,
            pl.BlockSpec((1, 2, rows), lambda p: (p + start, 0, 0)),
            spec,
            pl.BlockSpec((width, rows), lambda p: (0, 0)),
        ],
        out_specs=[
            out_spec,
            out_spec,
            out_spec,
            pl.BlockSpec((width, 3 * PAIR), lambda p: (0, p)),
            pl.BlockSpec((8, PAIR), lambda p: (0, p)),
        ],
        out_shape=[jax.ShapeDtypeStruct((rows, pairs * PAIR), BF16)] * 3
        + [
            jax.ShapeDtypeStruct((width, 3 * pairs * PAIR), BF16),
            jax.ShapeDtypeStruct((8, pairs * PAIR), F32),
        ],
        scratch_shapes=[
            pltpu.VMEM((rows, PAIR), BF16),
            pltpu.VMEM((rows, PAIR), F32),
            pltpu.VMEM((rows, PAIR), F32),
        ],
        compiler_params=params("arbitrary"),
        cost_estimate=cost(rows * PAIR, rows * PAIR),
        name="attend_back",
    )(queries, keys, values, logs, grad_context, normed_t)


def normalise(values):
    centred = values - jnp.mean(values, axis=-1, keepdims=True)
    spread = lax.rsqrt(jnp.mean(centred * centred, axis=-1, keepdims=True) + EPS)
    return centred * spread, spread


def normalise_back(grad, unit, spread, gain):
    scaled = grad * gain
    mean = jnp.mean(scaled, axis=-1, keepdims=True)
    tilt = jnp.mean(scaled * unit, axis=-1, keepdims=True)
    return spread * (scaled - mean - unit * tilt)


def pieces(values):
    high = values.astype(BF16)
    rest = values - high.astype(F32)
    middle = rest.astype(BF16)
    low = (rest - middle.astype(F32)).astype(BF16)
    fill = jnp.zeros((5, values.shape[1]), F32)
    stacked = jnp.concatenate(
        [high.astype(F32), middle.astype(F32), low.astype(F32), fill], axis=0
    )
    return stacked.astype(BF16)


def join(parts):
    return parts[0:1] + parts[1:2] + parts[2:3]


def column(row):
    return jnp.transpose(jnp.broadcast_to(row, (8, row.shape[1])))[:, 0:1]


def gate_row(logits, picked):
    return jax.nn.sigmoid(jnp.sum(jnp.where(picked, logits, 0.0), axis=0, keepdims=True))


def picked_rows(ids, experts):
    return lax.broadcasted_iota(jnp.int32, (experts, ids.shape[1]), 0) == ids


def one_hot_rows(slots, first, count):
    places = lax.broadcasted_iota(jnp.int32, (count, slots.shape[1]), 0) + first
    return (places == slots).astype(F32).astype(BF16)


def one_hot_columns(slots, first, count):
    places = lax.broadcasted_iota(jnp.int32, (slots.shape[0], count), 1) + first
    return (places == slots).astype(F32).astype(BF16)


def route_kernel(experts, capacity, row_ref, col_ref, grad_ref, slots_ref, columns_ref, out_ref, count_row):
    step = pl.program_id(0)
    rows = row_ref.shape[1]
    width = grad_ref.shape[1]
    half = capacity // 2

    @pl.when(step == 0)
    def _():
        first = lax.broadcasted_iota(jnp.int32, (rows, rows), 0)
        second = lax.broadcasted_iota(jnp.int32, (rows, rows), 1)
        ids = row_ref[...]
        picked = picked_rows(ids, experts).astype(F32)
        before = mm(picked.astype(BF16), (first < second).astype(F32).astype(BF16))
        place = jnp.sum(before * picked, axis=0, keepdims=True).astype(jnp.int32)
        slots_ref[...] = ids * capacity + place
        ids = col_ref[...]
        picked = (lax.broadcasted_iota(jnp.int32, (rows, 128), 1) == ids).astype(F32)
        before = mm((second < first).astype(F32).astype(BF16), picked.astype(BF16))
        place = jnp.sum(before * picked, axis=1, keepdims=True).astype(jnp.int32)
        late = experts * half + ids * (half + EXTRA) + place - half
        columns_ref[:, 0:1] = jnp.where(place < half, ids * half + place, late)
        columns_ref[:, 1:2] = ids * capacity + place
        count_row[...] = jnp.zeros_like(count_row)
        count_row[0:1, 0:128] = jnp.sum(picked, axis=0, keepdims=True)

    chosen = one_hot_rows(slots_ref[...], step * capacity, capacity)
    out_ref[0, :capacity, :] = mm(chosen, grad_ref[...]).astype(BF16)
    out_ref[0, capacity:, :] = count_row[...].astype(BF16)


def route(routes, grad_out, experts, capacity):
    rows, width = grad_out.shape
    whole = lambda e: (0, 0)
    return pl.pallas_call(
        functools.partial(route_kernel, experts, capacity),
        grid=(experts,),
        in_specs=[
            pl.BlockSpec((1, rows), whole),
            pl.BlockSpec((rows, 1), whole),
            pl.BlockSpec((rows, width), whole),
        ],
        out_specs=[
            pl.BlockSpec((1, rows), whole),
            pl.BlockSpec((rows, 2), whole),
            pl.BlockSpec((1, capacity + EXTRA, width), lambda e: (e, 0, 0)),
        ],
        out_shape=[
            jax.ShapeDtypeStruct((1, rows), jnp.int32),
            jax.ShapeDtypeStruct((rows, 2), jnp.int32),
            jax.ShapeDtypeStruct((experts, capacity + EXTRA, width), BF16),
        ],
        scratch_shapes=[pltpu.VMEM((EXTRA, width), F32)],
        compiler_params=params("arbitrary"),
        cost_estimate=cost(2 * experts * capacity * rows * width, 6 * rows * width),
        name="route",
    )(routes.reshape(1, rows), routes, grad_out)


def project_kernel(tokens_ref, gain_ref, shift_ref, wq_ref, bq_ref, wk_ref, wv_ref, bv_ref,
                   normed_ref, q_ref, k_ref, v_ref):
    unit, _ = normalise(tokens_ref[...].astype(F32))
    normed = (unit * gain_ref[...] + shift_ref[...]).astype(BF16)
    normed_ref[...] = jnp.transpose(normed)
    q_ref[...] = ((mm(normed, wq_ref[...]) + bq_ref[...]) * 0.125).astype(BF16)
    k_ref[...] = mm(normed, wk_ref[...]).astype(BF16)
    v_ref[...] = (mm(normed, wv_ref[...]) + bv_ref[...]).astype(BF16)


def project(tokens, gain, shift, w_query, bias_query, w_key, w_value, bias_value, tile=256):
    rows, width = tokens.shape
    row_spec = pl.BlockSpec((tile, width), lambda t: (t, 0))
    vector = pl.BlockSpec((1, width), lambda t: (0, 0))
    square = pl.BlockSpec((width, width), lambda t: (0, 0))
    return pl.pallas_call(
        project_kernel,
        grid=(rows // tile,),
        in_specs=[row_spec, vector, vector, square, vector, square, square, vector],
        out_specs=[pl.BlockSpec((width, tile), lambda t: (0, t))] + [row_spec] * 3,
        out_shape=[jax.ShapeDtypeStruct((width, rows), BF16)]
        + [jax.ShapeDtypeStruct((rows, width), BF16)] * 3,
        compiler_params=params("arbitrary"),
        cost_estimate=cost(6 * rows * width * width, 10 * rows * width + 6 * width * width),
        name="project",
    )(tokens, gain, shift, w_query, bias_query, w_key, w_value, bias_value)


def settle_kernel(context_ref, tokens_ref, w_out_ref, bias_ref, gain_ref, shift_ref, router_ref,
                  hidden_ref, moe_ref, logits_ref):
    hidden = tokens_ref[...].astype(F32) + mm(context_ref[...], w_out_ref[...]) + bias_ref[...]
    unit, _ = normalise(hidden)
    moe_in = (unit * gain_ref[...] + shift_ref[...]).astype(BF16)
    hidden_ref[...] = hidden
    moe_ref[...] = moe_in
    logits_ref[...] = mm_nt(router_ref[...], moe_in)


def settle(context, tokens, w_out, bias_out, gain, shift, router_rows, tile=256):
    rows, width = tokens.shape
    experts = router_rows.shape[0]
    row_spec = pl.BlockSpec((tile, width), lambda t: (t, 0))
    vector = pl.BlockSpec((1, width), lambda t: (0, 0))
    return pl.pallas_call(
        settle_kernel,
        grid=(rows // tile,),
        in_specs=[
            row_spec,
            row_spec,
            pl.BlockSpec((width, width), lambda t: (0, 0)),
            vector,
            vector,
            vector,
            pl.BlockSpec((experts, width), lambda t: (0, 0)),
        ],
        out_specs=[row_spec, row_spec, pl.BlockSpec((experts, tile), lambda t: (0, t))],
        out_shape=[
            jax.ShapeDtypeStruct((rows, width), F32),
            jax.ShapeDtypeStruct((rows, width), BF16),
            jax.ShapeDtypeStruct((experts, rows), F32),
        ],
        compiler_params=params("arbitrary"),
        cost_estimate=cost(2 * rows * width * width, 10 * rows * width + 2 * width * width),
        name="settle",
    )(context, tokens, w_out, bias_out, gain, shift, router_rows)


def dispatch_kernel(weight_ref, slots_ref, ids_ref, logits_ref, moe_ref, first_ref, second_ref, parts):
    step = pl.program_id(0)
    experts = logits_ref.shape[0]
    half = first_ref.shape[1]

    @pl.when(step == 0)
    def _():
        gate = gate_row(logits_ref[...], picked_rows(ids_ref[...], experts))
        parts[...] = pieces(gate * weight_ref[0, 0])

    chosen = one_hot_rows(slots_ref[...], step * 2 * half, 2 * half)
    rows = mm(chosen, moe_ref[...]).astype(BF16)
    first_ref[0] = rows[:half]
    second_ref[0, :half, :] = rows[half:]
    second_ref[0, half:, :] = jnp.zeros((EXTRA, rows.shape[1]), BF16)
    second_ref[0, half:, 0 : 2 * half] = mm_nt(parts[...], chosen).astype(BF16)


def dispatch(weight, slots, ids, logits, moe_in, capacity):
    rows, width = moe_in.shape
    experts = logits.shape[0]
    half = capacity // 2
    whole = lambda e: (0, 0)
    return pl.pallas_call(
        dispatch_kernel,
        grid=(experts,),
        in_specs=[
            pl.BlockSpec(memory_space=pltpu.SMEM),
            pl.BlockSpec((1, rows), whole),
            pl.BlockSpec((1, rows), whole),
            pl.BlockSpec((experts, rows), whole),
            pl.BlockSpec((rows, width), whole),
        ],
        out_specs=[
            pl.BlockSpec((1, half, width), lambda e: (e, 0, 0)),
            pl.BlockSpec((1, half + EXTRA, width), lambda e: (e, 0, 0)),
        ],
        out_shape=[
            jax.ShapeDtypeStruct((experts, half, width), BF16),
            jax.ShapeDtypeStruct((experts, half + EXTRA, width), BF16),
        ],
        scratch_shapes=[pltpu.VMEM((8, rows), BF16)],
        compiler_params=params("arbitrary"),
        cost_estimate=cost(2 * experts * capacity * rows * width, 6 * rows * width),
        name="dispatch",
    )(weight, slots, ids, logits, moe_in)


def row_sum(values):
    ones = jnp.ones((8, values.shape[1]), BF16)
    high = values.astype(BF16)
    rest = values - high.astype(F32)
    middle = rest.astype(BF16)
    low = (rest - middle.astype(F32)).astype(BF16)
    return (mm_nt(ones, high) + mm_nt(ones, middle) + mm_nt(ones, low))[0:1]


def expert_kernel(steps, chunk, *refs):
    if chunk == 0:
        (x_ref, g_ref, w_in_ref, b_in_ref, w_down_ref, b_down_ref,
         act_ref, up_ref, out_ref, back_ref, dot_ref, back_acc, dot_acc, out_acc) = refs
    else:
        (x_ref, g_ref, w_in_ref, b_in_ref, w_down_ref, b_down_ref, _, _, _, earlier_ref,
         act_ref, up_ref, out_ref, back_ref, back_acc, dot_acc, out_acc) = refs
    part = pl.program_id(0)
    tile = pl.program_id(1)
    group, half, width = x_ref.shape
    rows = group * half
    x = x_ref[...].reshape(rows, width)
    g = g_ref[...].reshape(rows, width)
    w_in = w_in_ref[0]
    pre = mm(x, w_in) + b_in_ref[0].astype(F32)
    grad_act = mm_nt(g, w_down_ref[0])
    below = 0.5 + 0.5 * lax.erf(pre * 0.7071067811865476)
    act = pre * below
    slope = below + pre * (0.3989422804014327 * jnp.exp(-0.5 * pre * pre))
    up = (grad_act * slope).astype(BF16)
    rounded = act.astype(BF16)
    act_ref[0, 0] = rounded
    up_ref[0, 0] = up
    out = mm(rounded, w_down_ref[0])
    product = act * grad_act
    lanes = min(128, product.shape[1])
    folded = product[:, :lanes]
    for lane in range(lanes, product.shape[1], lanes):
        folded = folded + product[:, lane : lane + lanes]
    where = pl.ds(pl.multiple_of(tile * rows, rows), rows)
    back = mm_nt(up, w_in)

    @pl.when(part == 0)
    def _():
        biased = g.astype(F32) * b_down_ref[...].astype(F32)
        total = folded
        for lane in range(0, biased.shape[1], lanes):
            total = total + biased[:, lane : lane + lanes]
        back_acc[where, :] = back
        out_acc[where, :] = out + b_down_ref[...].astype(F32)
        dot_acc[where, :] = total

    @pl.when(part > 0)
    def _():
        back_acc[where, :] += back
        out_acc[where, :] += out
        dot_acc[where, :] += folded

    @pl.when(part == steps - 1)
    def _():
        out_ref[...] = out_acc[where, :].astype(BF16).reshape(group, half, width)
        back_ref[:, :half, :] = back_acc[where, :].astype(BF16).reshape(group, half, width)
        dots = dot_acc[where, :]
        for index in range(group):
            own = pieces(row_sum(dots[index * half : (index + 1) * half, :])).astype(F32)
            if chunk == 0:
                dot_ref[index] = own.astype(BF16)
            else:
                before = earlier_ref[index].astype(F32)
                extra = jnp.concatenate([own[0:3], before[0:3], own[6:8]], axis=0)
                back_ref[index, half:, :] = jnp.zeros((EXTRA, width), BF16)
                back_ref[index, half:, 0:half] = extra.astype(BF16)


def expert(x, g, w_in, b_in, w_down, b_down, chunk, earlier=()):
    sources, width = x.shape[0], x.shape[2]
    half = (g.shape[1] - EXTRA) // 2
    rows = sources * half
    parts, _, hidden = w_in.shape
    group = max(1, 256 // half)
    tile = group * half
    tiles = sources // group
    last = parts - 1
    late = lambda p, t: jnp.where(p == last, t, 0)
    wide_spec = pl.BlockSpec((1, 1, tile, hidden), lambda p, t: (p, chunk, t, 0))
    wide_shape = jax.ShapeDtypeStruct((parts, 2, rows, hidden), BF16)
    dot_shape = jax.ShapeDtypeStruct((sources, 8, half), BF16)
    dot_spec = pl.BlockSpec((group, 8, half), lambda p, t: (late(p, t), 0, 0))
    back_rows = half + EXTRA * chunk
    return pl.pallas_call(
        functools.partial(expert_kernel, parts, chunk),
        grid=(parts, tiles),
        in_specs=[
            pl.BlockSpec((group, half, width), lambda p, t: (t, 0, 0)),
            pl.BlockSpec((group, half, width), lambda p, t: (t, chunk, 0)),
            pl.BlockSpec((1, width, hidden), lambda p, t: (p, 0, 0)),
            pl.BlockSpec((1, 1, hidden), lambda p, t: (p, 0, 0)),
            pl.BlockSpec((1, hidden, width), lambda p, t: (p, 0, 0)),
            pl.BlockSpec((1, width), lambda p, t: (0, 0)),
        ]
        + ([pl.BlockSpec(memory_space=pl.ANY)] * 3 + [dot_spec] if chunk else []),
        out_specs=[
            wide_spec,
            wide_spec,
            pl.BlockSpec((group, half, width), lambda p, t: (late(p, t), chunk, 0)),
            pl.BlockSpec((group, back_rows, width), lambda p, t: (late(p, t), 0, 0)),
        ]
        + ([] if chunk else [dot_spec]),
        out_shape=[
            wide_shape,
            wide_shape,
            jax.ShapeDtypeStruct((sources, 2 * half, width), BF16),
            jax.ShapeDtypeStruct((sources, back_rows, width), BF16),
        ]
        + ([] if chunk else [dot_shape]),
        scratch_shapes=[
            pltpu.VMEM((rows, width), F32),
            pltpu.VMEM((rows, min(128, hidden)), F32),
            pltpu.VMEM((rows, width), F32),
        ],
        input_output_aliases={6: 0, 7: 1, 8: 2} if chunk else {},
        compiler_params=params("arbitrary", "arbitrary"),
        cost_estimate=cost(
            6 * rows * width * hidden * parts, rows * hidden * parts * 4, 2 * rows * hidden * parts
        ),
        name="expert",
    )(x, g, w_in, b_in, w_down, b_down, *earlier)


def weight_kernel(parts, x0_ref, x1_ref, g_ref, act_ref, up_ref, scale_ref,
                  grad_ref, down_acc, in_acc, bias_acc, bias_down_acc, flipped):
    part = pl.program_id(0)
    chunk = pl.program_id(1)
    sources, half, width = x0_ref.shape
    rows = sources * half
    hidden = act_ref.shape[3]
    scale = scale_ref[0]
    split = pieces(scale)
    g = g_ref[...].reshape(rows, width)

    def flip(values):
        return (jnp.transpose(values).astype(F32) * scale).astype(BF16)

    @pl.when((part == 0) & (chunk == 0))
    def _():
        flipped[0] = flip(x0_ref[...].reshape(rows, width))

    @pl.when((part == 0) & (chunk == 1))
    def _():
        flipped[1] = flip(x1_ref[...].reshape(rows, width))

    act = act_ref[0, 0]
    up = up_ref[0, 0]
    down = mm(flip(act), g)
    into = mm(flipped[chunk], up)
    bias_in = join(mm(split, up))

    @pl.when(chunk == 0)
    def _():
        down_acc[...] = down
        in_acc[...] = into
        bias_acc[...] = bias_in

    @pl.when(chunk == 1)
    def _():
        grad_ref[0, width : width + hidden, :] = (down_acc[...] + down).astype(BF16)
        grad_ref[0, :width, 0:hidden] = (in_acc[...] + into).astype(BF16)

    @pl.when(part == 0)
    def _():
        bias_down = join(mm(split, g))
        bias_down_acc[...] = jnp.where(chunk == 0, bias_down, bias_down_acc[...] + bias_down)

    @pl.when(chunk == 1)
    def _():
        first = width + hidden
        grad_ref[0, first:, :] = jnp.zeros((EXTRA, width), BF16)
        grad_ref[0, first : first + 1, 0:hidden] = (bias_acc[...] + bias_in).astype(BF16)
        grad_ref[0, first + 1 : first + 2, :] = bias_down_acc[...].astype(BF16)


def weight_grads(x0, x1, g, act, up, scale):
    sources, half, width = x0.shape
    parts, _, rows, hidden = act.shape
    wide_spec = pl.BlockSpec((1, 1, rows, hidden), lambda p, t: (p, t, 0, 0))
    return pl.pallas_call(
        functools.partial(weight_kernel, parts),
        grid=(parts, 2),
        in_specs=[
            pl.BlockSpec((sources, half, width), lambda p, t: (0, 0, 0)),
            pl.BlockSpec((sources, half, width), lambda p, t: (0, 0, 0)),
            pl.BlockSpec((sources, half, width), lambda p, t: (0, t, 0)),
            wide_spec,
            wide_spec,
            pl.BlockSpec((1, 1, rows), lambda p, t: (t, 0, 0)),
        ],
        out_specs=pl.BlockSpec((1, width + hidden + EXTRA, width), lambda p, t: (p, 0, 0)),
        out_shape=jax.ShapeDtypeStruct((parts, width + hidden + EXTRA, width), BF16),
        scratch_shapes=[
            pltpu.VMEM((hidden, width), F32),
            pltpu.VMEM((width, hidden), F32),
            pltpu.VMEM((1, hidden), F32),
            pltpu.VMEM((1, width), F32),
            pltpu.VMEM((2, width, rows), BF16),
        ],
        compiler_params=params("arbitrary", "arbitrary"),
        cost_estimate=cost(12 * rows * width * hidden * parts, rows * hidden * parts * 8),
        name="weight_grads",
    )(x0, x1, g, act, up, scale)


def combine_kernel(weight_ref, back0_ref, back1_ref, dots0_ref, dots1_ref, columns_ref, ids_ref, logits_ref, pull_ref,
                   hidden_ref, grad_ref, context_ref, moe_ref, w_out_ref, router_ref, gain_ref,
                   hid_grad_ref, con_grad_ref, out_grad_ref, sums_ref, router_grad_ref, probs_ref, out_acc):
    step = pl.program_id(0)
    experts = logits_ref.shape[0]
    count0 = back0_ref.shape[0]
    count1 = back1_ref.shape[0]
    weight = weight_ref[0, 0]
    columns = columns_ref[:, 0:1]
    chosen0 = one_hot_columns(columns, 0, count0)
    chosen1 = one_hot_columns(columns, count0, count1)
    rows = mm(chosen0, back0_ref[...]) + mm(chosen1, back1_ref[...])
    dots = join(mm_nt(dots0_ref[...], chosen0)) + join(mm_nt(dots1_ref[...], chosen1))
    logits = logits_ref[...]
    picked = picked_rows(ids_ref[...], experts)
    gate = gate_row(logits, picked)
    powers = jnp.exp(logits - jnp.max(logits, axis=0, keepdims=True))
    probs = powers / jnp.sum(powers, axis=0, keepdims=True)
    pull = pull_ref[...]
    slope = dots * weight * gate * (1.0 - gate)
    logit_grad = probs * (pull - jnp.sum(probs * pull, axis=0, keepdims=True))
    logit_grad = (logit_grad + jnp.where(picked, slope, 0.0)).astype(BF16)
    moe_grad = mm_tn(logit_grad, router_ref[...]) + rows * column(gate * weight)
    unit, spread = normalise(hidden_ref[...])
    hid_grad = weight * grad_ref[...].astype(F32) + normalise_back(
        moe_grad, unit, spread, gain_ref[...]
    )
    branch = hid_grad.astype(BF16)
    hid_grad_ref[...] = hid_grad
    con_grad_ref[...] = mm_nt(branch, w_out_ref[...]).astype(BF16)
    out_grad = mm_tn(context_ref[...], branch)
    router_grad = mm(logit_grad, moe_ref[...])
    prob_sum = jnp.sum(probs, axis=1, keepdims=True)
    sums = jnp.concatenate(
        [
            jnp.sum(moe_grad * unit, axis=0, keepdims=True),
            jnp.sum(moe_grad, axis=0, keepdims=True),
            jnp.sum(branch.astype(F32), axis=0, keepdims=True),
            jnp.zeros((5, unit.shape[1]), F32),
        ],
        axis=0,
    )

    @pl.when(step == 0)
    def _():
        out_acc[...] = out_grad
        router_grad_ref[...] = router_grad
        probs_ref[...] = prob_sum
        sums_ref[...] = sums

    @pl.when(step > 0)
    def _():
        out_acc[...] += out_grad
        router_grad_ref[...] += router_grad
        probs_ref[...] += prob_sum
        sums_ref[...] += sums

    @pl.when(step == pl.num_programs(0) - 1)
    def _():
        out_grad_ref[...] = out_acc[...].astype(BF16)


def combine(weight, back0, back1, dots0, dots1, columns, ids, logits, pull, hidden, grad_out, context, moe_in,
            w_out, router_rows, gain, tile=256):
    rows, width = hidden.shape
    experts = logits.shape[0]
    count = back0.shape[0]
    count1 = back1.shape[0]
    whole = lambda t: (0, 0)
    row_spec = pl.BlockSpec((tile, width), lambda t: (t, 0))
    square = pl.BlockSpec((width, width), whole)
    return pl.pallas_call(
        combine_kernel,
        grid=(rows // tile,),
        in_specs=[
            pl.BlockSpec(memory_space=pltpu.SMEM),
            pl.BlockSpec((count, width), whole),
            pl.BlockSpec((count1, width), whole),
            pl.BlockSpec((8, count), whole),
            pl.BlockSpec((8, count1), whole),
            pl.BlockSpec((tile, 2), lambda t: (t, 0)),
            pl.BlockSpec((1, tile), lambda t: (0, t)),
            pl.BlockSpec((experts, tile), lambda t: (0, t)),
            pl.BlockSpec((experts, 1), whole),
            row_spec,
            row_spec,
            row_spec,
            row_spec,
            square,
            pl.BlockSpec((experts, width), whole),
            pl.BlockSpec((1, width), whole),
        ],
        out_specs=[
            row_spec,
            row_spec,
            square,
            pl.BlockSpec((8, width), whole),
            pl.BlockSpec((experts, width), whole),
            pl.BlockSpec((experts, 1), whole),
        ],
        out_shape=[
            jax.ShapeDtypeStruct((rows, width), F32),
            jax.ShapeDtypeStruct((rows, width), BF16),
            jax.ShapeDtypeStruct((width, width), BF16),
            jax.ShapeDtypeStruct((8, width), F32),
            jax.ShapeDtypeStruct((experts, width), F32),
            jax.ShapeDtypeStruct((experts, 1), F32),
        ],
        scratch_shapes=[pltpu.VMEM((width, width), F32)],
        compiler_params=params("arbitrary"),
        cost_estimate=cost(rows * width, rows * width),
        name="combine",
    )(weight, back0, back1, dots0, dots1, columns, ids, logits, pull, hidden, grad_out, context, moe_in, w_out,
      router_rows, gain)


def close_kernel(count, *refs):
    grads = refs[: 3 * count]
    (tokens_ref, hid_grad_ref, gain_ref, wq_ref, wk_ref, wv_ref, tok_grad_ref, sums_ref) = refs[3 * count :]
    step = pl.program_id(0)
    width = tokens_ref.shape[1]
    norm_grad = None
    for index, weights in enumerate((wq_ref, wk_ref, wv_ref)):
        parts = [grads[3 * part + index][...] for part in range(count)]
        term = mm_nt(jnp.concatenate(parts, axis=1), weights[...])
        norm_grad = term if norm_grad is None else norm_grad + term
    unit, spread = normalise(tokens_ref[...].astype(F32))
    tok_grad = hid_grad_ref[...] + normalise_back(norm_grad, unit, spread, gain_ref[...])
    tok_grad_ref[...] = tok_grad.astype(BF16)
    sums = jnp.concatenate(
        [
            jnp.sum(norm_grad * unit, axis=0, keepdims=True),
            jnp.sum(norm_grad, axis=0, keepdims=True),
            jnp.zeros((6, width), F32),
        ],
        axis=0,
    )

    @pl.when(step == 0)
    def _():
        sums_ref[...] = sums

    @pl.when(step > 0)
    def _():
        sums_ref[...] += sums


def close(grads, tokens, hid_grad, gain, w_query, w_key, w_value, tile=256):
    rows, width = tokens.shape
    whole = lambda t: (0, 0)
    row_spec = pl.BlockSpec((tile, width), lambda t: (t, 0))
    square = pl.BlockSpec((width, width), whole)
    flat = [item for triple in grads for item in triple]
    return pl.pallas_call(
        functools.partial(close_kernel, len(grads)),
        grid=(rows // tile,),
        in_specs=[pl.BlockSpec((tile, item.shape[1]), lambda t: (t, 0)) for item in flat]
        + [row_spec, row_spec, pl.BlockSpec((1, width), whole), square, square, square],
        out_specs=[row_spec, pl.BlockSpec((8, width), whole)],
        out_shape=[
            jax.ShapeDtypeStruct((rows, width), BF16),
            jax.ShapeDtypeStruct((8, width), F32),
        ],
        compiler_params=params("arbitrary"),
        cost_estimate=cost(6 * rows * width * width, 16 * rows * width + 6 * width * width),
        name="close",
    )(*flat, tokens, hid_grad, gain, w_query, w_key, w_value)


def block_out_kernel(back_ref, columns_ref, ids_ref, logits_ref, hidden_ref, out_ref):
    chosen = one_hot_columns(columns_ref[:, 1:2], 0, back_ref.shape[0])
    rows = mm(chosen, back_ref[...])
    gate = gate_row(logits_ref[...], picked_rows(ids_ref[...], logits_ref.shape[0]))
    out_ref[...] = (hidden_ref[...] + column(gate) * rows).astype(BF16)


def block_output(back, columns, ids, logits, hidden, tile=256):
    rows, width = hidden.shape
    experts = logits.shape[0]
    count = back.shape[0]
    row_spec = pl.BlockSpec((tile, width), lambda t: (t, 0))
    return pl.pallas_call(
        block_out_kernel,
        grid=(rows // tile,),
        in_specs=[
            pl.BlockSpec((count, width), lambda t: (0, 0)),
            pl.BlockSpec((tile, 2), lambda t: (t, 0)),
            pl.BlockSpec((1, tile), lambda t: (0, t)),
            pl.BlockSpec((experts, tile), lambda t: (0, t)),
            row_spec,
        ],
        out_specs=row_spec,
        out_shape=jax.ShapeDtypeStruct((rows, width), BF16),
        compiler_params=params("arbitrary"),
        cost_estimate=cost(2 * rows * width * count, 6 * rows * width + 2 * count * width),
        name="block_output",
    )(back, columns, ids, logits, hidden)


def unpack_kernel(early_ref, late_ref, out_ref, *refs):
    width = out_ref.shape[1]
    out_ref[...] = early_ref[:, :width].astype(F32)
    place = 0
    for ref, first in ((early_ref, width), (late_ref, 0)):
        for base in range(first, ref.shape[1], 3 * PAIR):
            for index in range(3):
                lanes = ref[:, base + index * PAIR : base + (index + 1) * PAIR]
                refs[index][:, place : place + PAIR] = lanes.astype(F32)
            place += PAIR


def unpack(early, late, tile=256):
    rows = early.shape[0]
    width = (early.shape[1] + late.shape[1]) // 4
    spec = pl.BlockSpec((tile, width), lambda t: (t, 0))
    return pl.pallas_call(
        unpack_kernel,
        grid=(rows // tile,),
        in_specs=[
            pl.BlockSpec((tile, early.shape[1]), lambda t: (t, 0)),
            pl.BlockSpec((tile, late.shape[1]), lambda t: (t, 0)),
        ],
        out_specs=[spec] * 4,
        out_shape=[jax.ShapeDtypeStruct((rows, width), F32)] * 4,
        compiler_params=params("arbitrary"),
        cost_estimate=cost(rows * width, 24 * rows * width),
        name="unpack",
    )(early, late)


def swap(blocks, axis):
    return lax.all_to_all(blocks, axis, split_axis=0, concat_axis=0, tiled=True)


def after(value, *others):
    return lax.optimization_barrier((value,) + others)[0]


def trade(value, axis, bit):
    count = lax.axis_size(axis)
    return lax.ppermute(value, axis, [(place, place ^ bit) for place in range(count)])


def bits(axis):
    count, bit = lax.axis_size(axis), 1
    while bit < count:
        yield bit
        bit *= 2


def narrow_sum(value):
    for bit in bits("narrow"):
        value = value + trade(value, "narrow", bit)
    return value


def is_upper(axis, bit):
    return (lax.axis_index(axis) // bit) % 2


def halve(value, axis, bit):
    upper = is_upper(axis, bit)
    halves = value.reshape((2, value.shape[0] // 2) + value.shape[1:])
    mine = lax.dynamic_index_in_dim(halves, upper, 0, keepdims=False)
    other = lax.dynamic_index_in_dim(halves, 1 - upper, 0, keepdims=False)
    return (mine.astype(F32) + trade(other, axis, bit).astype(F32)).astype(value.dtype)


def rejoin(value, axis, bit):
    got = trade(value, axis, bit)
    upper = is_upper(axis, bit) == 1
    low = jnp.concatenate([value, got], axis=0)
    return jnp.where(upper, jnp.concatenate([got, value], axis=0), low)


def spread_out(value, axis):
    count = lax.axis_size(axis)
    copies = jnp.broadcast_to(value[None], (count,) + value.shape)
    return swap(copies, axis)


def narrow_part(value):
    for bit in bits("narrow"):
        value = halve(value, "narrow", bit)
    return value


def wide_part(value):
    width = value.shape[1]
    count = lax.axis_size("wide")
    parts = swap(value.reshape(count, -1, width), "wide")
    return jnp.sum(parts.astype(F32), axis=0).astype(value.dtype)


def wide_whole(value):
    return spread_out(value, "wide").reshape(-1, value.shape[1])


def narrow_whole(value):
    for bit in reversed(list(bits("narrow"))):
        value = rejoin(value, "narrow", bit)
    return value


def small_sum(value):
    for axis in ("narrow", "wide"):
        for bit in bits(axis):
            value = value + trade(value, axis, bit)
    return value


def per_device(
    tokens,
    grad_out,
    routes,
    group_counts,
    group_weights,
    norm1_gain,
    norm1_bias,
    w_query,
    bias_query,
    w_key,
    w_value,
    bias_value,
    w_out,
    bias_out,
    norm2_gain,
    norm2_bias,
    router,
    w_in,
    bias_in,
    w_down,
    bias_down,
):
    rows, width = tokens.shape
    experts = router.shape[1]
    assert rows == SEQ_LEN and w_in.shape[0] == 1
    hidden_cols = w_in.shape[2]
    wide_count = lax.axis_size("wide")
    narrow_count = lax.axis_size("narrow")
    devices = wide_count * narrow_count
    capacity = 2 * rows // experts
    half = capacity // 2
    total_tokens = rows * devices
    row = lambda vector: vector.reshape(1, -1)

    sequence = lax.axis_index(("wide", "narrow"))
    group_ends = jnp.cumsum(group_counts, dtype=jnp.int32)
    member = ((sequence >= group_ends - group_counts) & (sequence < group_ends)).astype(F32)
    factor = group_weights.astype(F32) * devices / (group_counts.shape[0] * group_counts.astype(F32))
    weight = jnp.sum(member * factor).reshape(1, 1)
    ids = routes.reshape(1, rows)
    router_rows = jnp.transpose(router)

    slots, columns, grad_outgoing = route(routes, grad_out, experts, capacity)
    grad_rows = swap(grad_outgoing, "wide")
    gathered_in = lax.all_gather(w_in[0], "narrow", axis=0)
    gathered_down = lax.all_gather(w_down[0], "narrow", axis=0)

    normed_t, queries, keys, values = project(
        tokens, row(norm1_gain), row(norm1_bias), w_query, row(bias_query), w_key, w_value, row(bias_value)
    )
    context, logs = attend(queries, keys, values)
    hidden, moe_in, logits = settle(
        context, tokens, w_out, row(bias_out), row(norm2_gain), row(norm2_bias), router_rows
    )
    first, second = dispatch(weight, slots, ids, logits, moe_in, capacity)
    gathered_bias = lax.all_gather(after(bias_in, first), "narrow", axis=0)
    x0 = swap(after(first, grad_rows), "wide")
    counted = jnp.sum(grad_rows[:, capacity, :experts].astype(F32), axis=0)
    fraction = narrow_sum(counted) / total_tokens
    x1 = swap(after(second, x0), "wide")
    act, up, out, back0, dots = expert(
        x0, grad_rows, gathered_in, gathered_bias, gathered_down, bias_down, 0
    )
    back0 = swap(after(back0, x1), "wide")
    act, up, expert_out, back1 = expert(
        x1, grad_rows, gathered_in, gathered_bias, gathered_down, bias_down, 1, (act, up, out, dots)
    )
    back1 = arrived = swap(after(back1, back0), "wide")
    scale = jnp.sum(x1[:, half : half + 3, :capacity].astype(F32), axis=1)
    scale = jnp.transpose(scale.reshape(wide_count, 2, half), (1, 0, 2)).reshape(2, 1, wide_count * half)
    expert_grad = weight_grads(after(x0, back0), x1, grad_rows, act, up, scale)
    expert_grad = lax.psum_scatter(after(expert_grad, arrived), "narrow", scatter_dimension=0).astype(F32)
    share = width // narrow_count
    grad_w_in = expert_grad[:width, :hidden_cols]
    grad_w_down = expert_grad[width : width + hidden_cols]
    grad_bias_in = expert_grad[width + hidden_cols : width + hidden_cols + 1, :hidden_cols]
    grad_bias_down = lax.dynamic_slice_in_dim(
        expert_grad[width + hidden_cols + 1 : width + hidden_cols + 2],
        lax.axis_index("narrow") * share,
        share,
        1,
    )
    back1 = after(back1, expert_grad)
    returned = swap(after(expert_out, arrived), "wide")

    extras = jnp.transpose(back1[:, half:, :half], (1, 0, 2))
    dots1 = jnp.pad(extras, ((0, 0), (0, 0), (0, EXTRA))).reshape(EXTRA, experts * (half + EXTRA))
    dots0 = jnp.concatenate([extras[3:], extras[:3]], axis=0).reshape(EXTRA, experts * half)
    pull = (BALANCE * experts * fraction).reshape(experts, 1)
    hid_grad, con_grad, out_grad, sums, router_grad, prob_sums = combine(
        weight,
        back0.reshape(experts * half, width),
        back1.reshape(experts * (half + EXTRA), width),
        dots0,
        dots1,
        columns,
        ids,
        logits,
        pull,
        hidden,
        grad_out,
        context,
        moe_in,
        w_out,
        router_rows,
        row(norm2_gain),
    )
    pairs = width // PAIR
    span = pairs // ATTEND_CALLS
    grads, bias_sums = [], []
    packed = [narrow_part(out_grad)]
    for call in range(ATTEND_CALLS):
        dq, dk, dv, weights, column_sums = attend_back(
            queries, keys, values, logs, con_grad, normed_t, call * span, span
        )
        grads.append((dq, dk, dv))
        packed.append(narrow_part(weights))
        bias_sums.append(column_sums)
    early = jnp.concatenate(packed[:-1], axis=1)
    hid_grad = after(hid_grad, early)
    grad_tokens, norm_sums = close(grads, tokens, hid_grad, row(norm1_gain), w_query, w_key, w_value)
    block_out = block_output(
        returned.reshape(experts * capacity, width), columns, ids, logits, hidden
    )
    early = wide_part(after(early, returned))
    late = wide_part(after(packed[-1], early, norm_sums))
    early = wide_whole(after(early, late, block_out))
    late = wide_whole(after(late, early, grad_w_in, grad_w_down))
    early = narrow_whole(early)
    late = narrow_whole(late)
    bias_sums = jnp.concatenate(bias_sums, axis=1)
    prob_row = jnp.pad(prob_sums.reshape(1, experts), ((0, 0), (0, width - experts)))
    small = small_sum(
        jnp.concatenate([norm_sums[:2], bias_sums[:2], sums[:3], prob_row, router_grad], axis=0)
    )
    balance_loss = experts * jnp.sum(fraction * (small[7, :experts] / total_tokens))
    grad_w_out, *weights = unpack(early, late)
    return (
        block_out,
        balance_loss,
        grad_tokens,
        small[0],
        small[1],
        weights[0],
        small[2],
        weights[1],
        weights[2],
        small[3],
        grad_w_out,
        small[6],
        small[4],
        small[5],
        jnp.transpose(small[8:]),
        grad_w_in[None],
        grad_bias_in,
        grad_w_down[None],
        grad_bias_down,
    )


def solution(mesh):
    return jax.shard_map(
        per_device,
        mesh=mesh,
        in_specs=(
            P(("wide", "narrow"), None),
            P(("wide", "narrow"), None),
            P(("wide", "narrow"), None),
            P(),
            P(),
            P(),
            P(),
            P(),
            P(),
            P(),
            P(),
            P(),
            P(),
            P(),
            P(),
            P(),
            P(),
            P("wide", None, "narrow"),
            P("wide", "narrow"),
            P("wide", "narrow", None),
            P("wide", None),
        ),
        out_specs=(
            P(("wide", "narrow"), None),
            P(),
            P(("wide", "narrow"), None),
            P(),
            P(),
            P(),
            P(),
            P(),
            P(),
            P(),
            P(),
            P(),
            P(),
            P(),
            P(),
            P("wide", None, "narrow"),
            P("wide", "narrow"),
            P("wide", "narrow", None),
            P("wide", "narrow"),
        ),
        check_vma=False,
    )
```

time: 1480 us -> 526 us (0.36)
  waiting for transfers between devices: 549 us -> 90.4 us
  matrix products: 432 us -> 0 us
  Pallas kernels: 0 us -> 245 us
  blocking collectives: 286 us -> 69.3 us
  other arithmetic: 105 us -> 18 us
  local copies, waits for them, and re-layouts: 66.9 us -> 19.6 us
  starting transfers between devices: 11.4 us -> 58.6 us
    dot_general x33 -> x0, matrix products: 432 us -> none  [the longest x1 70.5 us: per_device(): jnp.einsum('red,efd->ref', grad_gathered, w_down, preferred_element_type=...]
    reduce_scatter x2 -> x1, waiting for transfers between devices: 276 us -> 0.01 us  [per_device(): lax.psum_scatter(after(expert_grad, arrived), 'narrow', scatter_dimension=0)]
    pallas_call x0 -> x14, Pallas kernels: none -> 245 us  [the longest x2 66.1 us: expert(): pl.pallas_call(functools.partial(expert_kernel, parts, chunk), grid=(part...]
    all_gather x2, waiting for transfers between devices: 162 us -> 0.01 us  [the longest x1 0.01 us: per_device(): gathered_in = lax.all_gather(w_in[0], 'narrow', axis=0)]
    psum x2 -> x0, blocking collectives: 133 us -> none  [per_device(): lax.psum((jnp.sum(chosen, axis=0), jnp.sum(router_probs, axis=0)), ('wide...]
    psum x1 -> x0, waiting for transfers between devices: 111 us -> none  [per_device(): lax.psum((grad_norm1_gain, grad_norm1_bias, grad_w_query, grad_bias_query...]
    all_to_all x2, blocking collectives: 153 us -> 63.7 us  [swap(): return lax.all_to_all(blocks, axis, split_axis=0, concat_axis=0, tiled=True)]
    convert_element_type x7, other arithmetic: 59.7 us -> 3.89 us  [the longest x1 2.18 us: per_device(): lax.psum_scatter(after(expert_grad, arrived), 'narrow', scatter_dimension=0)]
  transfers between devices with their start and end apart: 7 -> 28, of which waited for: 5 -> 17; matrix products, arithmetic and copies ran while one was open for 8% -> 6% of each run, Pallas kernels for 0% -> 47%
where the time goes in v1:
time: 526 us; the launch traced here: 517 us
  Pallas kernels  245 us (47%)
  waiting for transfers between devices  90.4 us (17%)
  blocking collectives  69.3 us (13%)
  starting transfers between devices  58.6 us (11%)
  local copies, waits for them, and re-layouts  19.6 us (4%)
  other arithmetic  18 us (3%)
  between operations  16.2 us (3%)
    pallas_call x2, Pallas kernels, expert(): pl.pallas_call(functools.partial(expert_kernel, parts, chunk), grid=(part...  66.1 us
    all_to_all x2, blocking collectives, swap(): return lax.all_to_all(blocks, axis, split_axis=0, concat_axis=0, tiled=True)  63.7 us
    all_to_all x8, waiting for transfers between devices, swap(): return lax.all_to_all(blocks, axis, split_axis=0, concat_axis=0, tiled=True)  48.6 us
    pallas_call x2, Pallas kernels, attend_back(): pl.pallas_call(functools.partial(attend_back_kernel, block), grid=(pairs,...  43.9 us
    ppermute x17, waiting for transfers between devices, trade(): lax.ppermute(value, axis, [(place, place ^ bit) for place in range(count)])  40.4 us
    all_to_all x8, starting transfers between devices, swap(): return lax.all_to_all(blocks, axis, split_axis=0, concat_axis=0, tiled=True)  39.9 us
    pallas_call x1, Pallas kernels, weight_grads(): pl.pallas_call(functools.partial(weight_kernel, parts), grid=(parts, 2),...  33.5 us
    pallas_call x1, Pallas kernels, attend(): pl.pallas_call(functools.partial(attend_kernel, block), grid=(pairs,), in...  25.5 us
  transfers between devices with their start and end apart: 28, of which 17 were waited for; matrix products, arithmetic and copies ran while one was open for 6% of the time, Pallas kernels for 47%

profile of v1, /device:TPU:0, one launch (start us, length us, event | category | flops | bytes accessed | tf_op | source)
XLA Modules:
  0.0 516.9 jit_solution(11784003578390348077)
XLA Ops:
  7.9 1.7 copy.49.col_ref
  9.6 9.6 %route.1 = (s32[1,1024]{1,0:T(1,128)}, s32[1024,2]{1,0:T(8,128)}, bf16[8,264,768]{2,1,0:T(8,128)(2,1)}) custom-call(s32[1,1024]{1,0:T(1,128)} %bitcast.97, s32[1024,1]{1,0:T(8,128)} %copy.49.col_ref, bf16[1024,768]{1,0:T(8,128)(2,1)} %grad_ref.3), custom_call_target="tpu_custom_call" | custom-call | flops 3221225472 | bytes 4718592 | tf_op jit(solution)/shard_map/route/pallas_call | solution.py:271
  19.3 7.4 %all-to-all-start = ((bf16[8,264,768]{2,1,0:T(8,128)(2,1)}), bf16[8,264,768]{2,1,0:T(8,128)(2,1)S(1)}, u32[]{:S(2)}, u32[]{:S(2)}) async-start(bf16[8,264,768]{2,1,0:T(8,128)(2,1)} %get-tuple-element.86), calls=%async_computation | async-start | bytes 6488064 | tf_op jit(solution)/shard_map/all_to_all | solution.py:852
  32.3 8.3 %project.1 = (bf16[768,1024]{1,0:T(8,128)(2,1)}, bf16[1024,768]{1,0:T(8,128)(2,1)}, bf16[1024,768]{1,0:T(8,128)(2,1)}, bf16[1024,768]{1,0:T(8,128)(2,1)}) custom-call(bf16[1024,768]{1,0:T(8,128)(2,1)} %refs_6_.1, f32[1,768]{1,0:T(1,128)} %reshape.180.gain_ref.refs_8_, f32[1,768]{1,0:T(1,128)} %reshape.181.shift_ref, bf16[768,768]{1,0:T(8,128)(2,1)} %refs_9_.1, ...), custom_call_target="tpu_custom_call" | custom-call | flops 3623878656 | bytes 11403264 | tf_op jit(solution)/shard_map/project/pallas_call | solution.py:311
  40.6 25.5 %attend.1 = (bf16[1024,768]{1,0:T(8,128)(2,1)}, f32[6,2,1024]{2,1,0:T(2,128)}) custom-call(bf16[1024,768]{1,0:T(8,128)(2,1)} %get-tuple-element.78.q_ref, bf16[1024,768]{1,0:T(8,128)(2,1)} %get-tuple-element.79.k_ref, bf16[1024,768]{1,0:T(8,128)(2,1)} %get-tuple-element.80.v_ref), custom_call_target="tpu_custom_call" | custom-call | flops 6442450944 | bytes 6291456 | tf_op jit(solution)/shard_map/attend/pallas_call | solution.py:81
  66.1 6.8 %settle.1 = (f32[1024,768]{1,0:T(8,128)}, bf16[1024,768]{1,0:T(8,128)(2,1)}, f32[8,1024]{1,0:T(8,128)}) custom-call(bf16[1024,768]{1,0:T(8,128)(2,1)} %get-tuple-element.81.context_ref, bf16[1024,768]{1,0:T(8,128)(2,1)} %refs_6_.1, bf16[768,768]{1,0:T(8,128)(2,1)} %w_out_ref.3, f32[1,768]{1,0:T(1,128)} %reshape.184.bias_ref, f32[1,768]{1,0:T(1,128)} %reshape.185.gain_ref, ...), custom_call_target="tpu_custom_call" | custom-call | flops 1207959552 | bytes 9043968 | tf_op jit(solution)/shard_map/settle/pallas_call | solution.py:339
  72.9 8.5 %dispatch.1 = (bf16[8,128,768]{2,1,0:T(8,128)(2,1)}, bf16[8,136,768]{2,1,0:T(8,128)(2,1)}) custom-call(f32[1,1]{1,0:T(1,128)} %bitcast.2.weight_ref, s32[1,1024]{1,0:T(1,128)} %get-tuple-element.77.slots_ref, s32[1,1024]{1,0:T(1,128)} %bitcast.98, f32[8,1024]{1,0:T(8,128)} %get-tuple-element.82.logits_ref, bf16[1024,768]{1,0:T(8,128)(2,1)} %get-tuple-element.83.moe_ref), custom_call_target="tpu_custom_call" | custom-call | flops 3221225472 | bytes 4718592 | tf_op jit(solution)/shard_map/dispatch/pallas_call | solution.py:386
  81.5 18.0 %all-to-all-done.refs_1_.g_ref = bf16[8,264,768]{2,1,0:T(8,128)(2,1)S(1)} async-done(((bf16[8,264,768]{2,1,0:T(8,128)(2,1)}), bf16[8,264,768]{2,1,0:T(8,128)(2,1)S(1)}, u32[]{:S(2)}, u32[]{:S(2)}) %all-to-all-start) | async-done | bytes 3244064 | tf_op jit(solution)/shard_map/all_to_all | solution.py:852
  99.5 41.0 %all_to_all.50.refs_0_.x0_ref = bf16[8,128,768]{2,1,0:T(8,128)(2,1)} all-to-all(bf16[8,128,768]{2,1,0:T(8,128)(2,1)} %get-tuple-element.87), channel_id=1, replica_groups=mesh['wide'=8,'narrow'=4] {'wide'}, dimensions={0} | all-to-all | bytes 3145728 | tf_op jit(solution)/shard_map/all_to_all | solution.py:852
  140.5 4.4 all-to-all-start.2
  144.9 5.6 %all-gather.1.refs_3_ = bf16[4,1,768]{2,1,0:T(2,128)(2,1)} all-gather(bf16[1,1,768]{2,1,0:T(2,128)(2,1)S(1)} %bitcast.104), channel_id=2, replica_groups=mesh['wide'=8,'narrow'=4] {'narrow'}, dimensions={0}, use_global_device_ids=true | all-gather | bytes 7680 | tf_op jit(solution)/shard_map/all_gather | solution.py:988
  150.6 33.0 %expert.2 = (bf16[4,2,1024,768]{3,2,1,0:T(8,128)(2,1)}, bf16[4,2,1024,768]{3,2,1,0:T(8,128)(2,1)}, bf16[8,256,768]{2,1,0:T(8,128)(2,1)}, bf16[8,128,768]{2,1,0:T(8,128)(2,1)}, bf16[8,8,128]{2,1,0:T(8,128)(2,1)}) custom-call(bf16[8,128,768]{2,1,0:T(8,128)(2,1)} %all_to_all.50.refs_0_.x0_ref, bf16[8,264,768]{2,1,0:T(8,128)(2,1)} %copy-done.3, ...), custom_call_target="tpu_custom_call" | custom-call | flops 14495514624 | bytes 12582912 | tf_op jit(solution)/shard_map/expert/pallas_call | solution.py:499
  183.5 6.5 %all-to-all-start.3 = ((bf16[8,128,768]{2,1,0:T(8,128)(2,1)}), bf16[8,128,768]{2,1,0:T(8,128)(2,1)S(1)}, u32[]{:S(2)}, u32[]{:S(2)}) async-start(bf16[8,128,768]{2,1,0:T(8,128)(2,1)} %get-tuple-element.97), calls=%async_computation.3 | async-start | bytes 3145728 | tf_op jit(solution)/shard_map/all_to_all | solution.py:852
  190.0 33.2 %expert.3 = (bf16[4,2,1024,768]{3,2,1,0:T(8,128)(2,1)}, bf16[4,2,1024,768]{3,2,1,0:T(8,128)(2,1)}, bf16[8,256,768]{2,1,0:T(8,128)(2,1)}, bf16[8,136,768]{2,1,0:T(8,128)(2,1)}) custom-call(bf16[8,136,768]{2,1,0:T(8,128)(2,1)} %all-to-all-done.2.refs_0_.x1_ref, ...), custom_call_target="tpu_custom_call", output_to_operand_aliasing={{0}: (6, {}), {1}: (7, {}), {2}: (8, {})} | custom-call | flops 14495514624 | bytes 12582912 | tf_op jit(solution)/shard_map/expert/pallas_call | solution.py:499
  223.2 4.3 all-to-all-done.3
  227.5 3.6 all-to-all-start.4
  231.2 1.4 convert_reduce_fusion
  232.5 33.5 %weight_grads.1 = bf16[4,1544,768]{2,1,0:T(8,128)(2,1)} custom-call(bf16[8,128,768]{2,1,0:T(8,128)(2,1)} %all_to_all.50.refs_0_.x0_ref, bf16[8,136,768]{2,1,0:T(8,128)(2,1)} %all-to-all-done.2.refs_0_.x1_ref, bf16[8,264,768]{2,1,0:T(8,128)(2,1)} %copy-done.3, bf16[4,2,1024,768]{3,2,1,0:T(8,128)(2,1)} %get-tuple-element.132.act_ref, ...), custom_call_target="tpu_custom_call" | custom-call | flops 28991029248 | bytes 25165824 | tf_op jit(solution)/shard_map/weight_grads/pallas_call | solution.py:595
  266.0 4.4 all-to-all-done.4
  270.4 4.6 all-to-all-start.5
  275.9 1.1 collective-permute-done
  277.0 1.5 collective-permute-start.1
  278.5 2.1 collective-permute-done.1
  283.2 19.0 %combine.1 = (f32[1024,768]{1,0:T(8,128)}, bf16[1024,768]{1,0:T(8,128)(2,1)}, bf16[768,768]{1,0:T(8,128)(2,1)}, f32[8,768]{1,0:T(8,128)}, f32[8,768]{1,0:T(8,128)}, /*index=5*/f32[8,1]{1,0:T(8,128)}) custom-call(f32[1,1]{1,0:T(1,128)} %bitcast.2.weight_ref, bf16[1024,768]{1,0:T(8,128)(2,1)} %bitcast.80, bf16[1088,768]{1,0:T(8,128)(2,1)} %bitcast.79, ...), custom_call_target="tpu_custom_call" | custom-call | flops 786432 | bytes 786432 | tf_op jit(solution)/shard_map/combine/pallas_call | solution.py:692
  302.2 1.1 dynamic-slice_bitcast_fusion.2
  303.4 21.8 %attend_back.2 = (bf16[1024,384]{1,0:T(8,128)(2,1)}, bf16[1024,384]{1,0:T(8,128)(2,1)}, bf16[1024,384]{1,0:T(8,128)(2,1)}, bf16[768,1152]{1,0:T(8,128)(2,1)}, f32[8,384]{1,0:T(8,128)}) custom-call(bf16[1024,768]{1,0:T(8,128)(2,1)} %get-tuple-element.78.q_ref, bf16[1024,768]{1,0:T(8,128)(2,1)} %get-tuple-element.79.k_ref, ...), custom_call_target="tpu_custom_call" | custom-call | flops 131072 | bytes 131072 | tf_op jit(solution)/shard_map/attend_back/pallas_call | solution.py:153
  325.2 2.2 dynamic-slice_bitcast_fusion.1
  327.8 22.1 %attend_back.3 = (bf16[1024,384]{1,0:T(8,128)(2,1)}, bf16[1024,384]{1,0:T(8,128)(2,1)}, bf16[1024,384]{1,0:T(8,128)(2,1)}, bf16[768,1152]{1,0:T(8,128)(2,1)}, f32[8,384]{1,0:T(8,128)}) custom-call(bf16[1024,768]{1,0:T(8,128)(2,1)} %get-tuple-element.78.q_ref, bf16[1024,768]{1,0:T(8,128)(2,1)} %get-tuple-element.79.k_ref, ...), custom_call_target="tpu_custom_call" | custom-call | flops 131072 | bytes 131072 | tf_op jit(solution)/shard_map/attend_back/pallas_call | solution.py:153
  350.1 1.7 collective-permute-start.3
  352.2 1.2 collective-permute-start.5
  353.4 1.0 dynamic-slice_bitcast_fusion
  354.4 5.7 %collective-permute-done.3 = bf16[192,768]{1,0:T(8,128)(2,1)S(1)} collective-permute-done((bf16[192,768]{1,0:T(8,128)(2,1)S(1)}, bf16[192,768]{1,0:T(8,128)(2,1)S(1)}, u32[]{:S(2)}, u32[]{:S(2)}) %collective-permute-start.3) | collective-permute-done | bytes 294944 | tf_op jit(solution)/shard_map/ppermute | solution.py:861
  360.2 8.5 %collective-permute-done.5 = bf16[192,1152]{1,0:T(8,128)(2,1)S(1)} collective-permute-done((bf16[192,1152]{1,0:T(8,128)(2,1)S(1)}, bf16[192,1152]{1,0:T(8,128)(2,1)S(1)}, u32[]{:S(2)}, u32[]{:S(2)}) %collective-permute-start.5) | collective-permute-done | bytes 442400 | tf_op jit(solution)/shard_map/ppermute | solution.py:861
  368.8 0.9 pad_maximum_fusion
  369.7 5.8 %all-to-all-start.6 = ((bf16[8,24,1920]{2,1,0:T(8,128)(2,1)}), bf16[8,24,1920]{2,1,0:T(8,128)(2,1)S(1)}, u32[]{:S(2)}, u32[]{:S(2)}) async-start(bf16[8,24,1920]{2,1,0:T(8,128)(2,1)} %bitcast.25), calls=%async_computation.6 | async-start | bytes 1474560 | tf_op jit(solution)/shard_map/all_to_all | solution.py:852
  375.8 1.6 collective-permute-start.12
  377.5 9.8 %close.1 = (bf16[1024,768]{1,0:T(8,128)(2,1)}, f32[8,768]{1,0:T(8,128)}) custom-call(bf16[1024,384]{1,0:T(8,128)(2,1)} %get-tuple-element.105.refs_0_, bf16[1024,384]{1,0:T(8,128)(2,1)} %get-tuple-element.106.refs_1_, bf16[1024,384]{1,0:T(8,128)(2,1)} %get-tuple-element.107.refs_2_, bf16[1024,384]{1,0:T(8,128)(2,1)} %get-tuple-element.108.refs_3_, ...), custom_call_target="tpu_custom_call" | custom-call | flops 3623878656 | bytes 16121856 | tf_op jit(solution)/shard_map/close/pallas_call | solution.py:774
  387.3 0.9 fusion.3
  388.2 5.8 %all-to-all-done.6 = bf16[8,24,1920]{2,1,0:T(8,128)(2,1)S(1)} async-done(((bf16[8,24,1920]{2,1,0:T(8,128)(2,1)}), bf16[8,24,1920]{2,1,0:T(8,128)(2,1)S(1)}, u32[]{:S(2)}, u32[]{:S(2)}) %all-to-all-start.6) | async-done | bytes 737312 | tf_op jit(solution)/shard_map/all_to_all | solution.py:852
  394.1 3.6 all-to-all-start.7
  397.8 7.7 %block_output.1 = bf16[1024,768]{1,0:T(8,128)(2,1)} custom-call(bf16[2048,768]{1,0:T(8,128)(2,1)} %bitcast.6.back_ref, s32[1024,2]{1,0:T(8,128)} %get-tuple-element.100.columns_ref, s32[1,1024]{1,0:T(1,128)} %bitcast.100, f32[8,1024]{1,0:T(8,128)} %get-tuple-element.82.logits_ref, f32[1024,768]{1,0:T(8,128)} %get-tuple-element.101.hidden_ref), custom_call_target="tpu_custom_call" | custom-call | flops 3221225472 | bytes 7864320 | tf_op jit(solution)/shard_map/block_output/pallas_call | solution.py:802
  405.4 5.2 %all-to-all-done.7 = bf16[8,24,1152]{2,1,0:T(8,128)(2,1)S(1)} async-done(((bf16[8,24,1152]{2,1,0:T(8,128)(2,1)}), bf16[8,24,1152]{2,1,0:T(8,128)(2,1)S(1)}, u32[]{:S(2)}, u32[]{:S(2)}) %all-to-all-start.7) | async-done | bytes 442400 | tf_op jit(solution)/shard_map/all_to_all | solution.py:852
  410.8 22.7 %all_to_all.51 = bf16[8,24,1920]{2,1,0:T(8,128)(2,1)S(1)} all-to-all(bf16[8,24,1920]{2,1,0:T(8,128)(2,1)S(1)} %broadcast_in_dim.4), channel_id=1, replica_groups=mesh['wide'=8,'narrow'=4] {'wide'}, dimensions={0} | all-to-all | bytes 1474560 | tf_op jit(solution)/shard_map/all_to_all | solution.py:852
  434.3 3.9 all-to-all-start.9
  438.2 1.6 collective-permute-start.13
  439.8 10.8 %all-to-all-done.9 = bf16[8,24,1152]{2,1,0:T(8,128)(2,1)S(1)} async-done(((bf16[8,24,1152]{2,1,0:T(8,128)(2,1)}), bf16[8,24,1152]{2,1,0:T(8,128)(2,1)S(1)}, u32[]{:S(2)}, u32[]{:S(2)}) %all-to-all-start.9) | async-done | bytes 442400 | tf_op jit(solution)/shard_map/all_to_all | solution.py:852
  450.6 1.5 collective-permute-start.15
  452.2 5.5 %collective-permute-done.13 = bf16[192,1920]{1,0:T(8,128)(2,1)S(1)} collective-permute-done((bf16[192,1920]{1,0:T(8,128)(2,1)S(1)}, bf16[192,1920]{1,0:T(8,128)(2,1)S(1)}, u32[]{:S(2)}, u32[]{:S(2)}) %collective-permute-start.13) | collective-permute-done | bytes 737312 | tf_op jit(solution)/shard_map/ppermute | solution.py:861
  458.2 7.3 %collective-permute-done.15 = bf16[192,1152]{1,0:T(8,128)(2,1)} collective-permute-done((bf16[192,1152]{1,0:T(8,128)(2,1)S(1)}, bf16[192,1152]{1,0:T(8,128)(2,1)}, u32[]{:S(2)}, u32[]{:S(2)}) %collective-permute-start.15) | collective-permute-done | bytes 442400 | tf_op jit(solution)/shard_map/ppermute | solution.py:861
  465.5 1.4 maximum_select_fusion.3
  469.9 0.9 collective-permute-done.6
  470.8 1.5 collective-permute-start.7
  472.3 2.6 collective-permute-done.7
  474.8 1.8 collective-permute-start.8
  476.6 2.3 collective-permute-done.8
  479.0 1.8 collective-permute-start.9
  480.8 2.3 collective-permute-done.9
  483.2 3.1 collective-permute-start.10
  486.2 2.1 collective-permute-done.10
  490.8 1.8 maximum_select_fusion.1.late_ref
  492.7 4.3 maximum_select_fusion.early_ref
  497.0 6.0 %unpack.1 = (f32[768,768]{1,0:T(8,128)}, f32[768,768]{1,0:T(8,128)}, f32[768,768]{1,0:T(8,128)}, f32[768,768]{1,0:T(8,128)}) custom-call(bf16[768,1920]{1,0:T(8,128)(2,1)} %maximum_select_fusion.early_ref, bf16[768,1152]{1,0:T(8,128)(2,1)} %maximum_select_fusion.1.late_ref), custom_call_target="tpu_custom_call" | custom-call | flops 589824 | bytes 14155776 | tf_op jit(solution)/shard_map/unpack/pallas_call | solution.py:836
  503.0 2.2 convert_element_type.126
  506.4 2.5 fusion.12
  (122 shorter events, 18.9 us)
Async XLA Ops:
  7.2 143.4 %all-gather.5.cloned.1.call-start = ((), (), s32[]{:S(2)}) async-start(), calls=%async_computation.11 | async-start | bytes 5898240 | tf_op jit(solution)/shard_map/all_gather | solution.py:977
  19.2 8.3 %copy-start.9 = (f32[768]{0:T(1024)S(1)}, f32[768]{0:T(1024)}, u32[]{:S(2)}) copy-start(f32[768]{0:T(1024)} %param.26) | copy-start | bytes 9220
  19.2 8.8 %copy-start.10 = (f32[768]{0:T(1024)S(1)}, f32[768]{0:T(1024)}, u32[]{:S(2)}) copy-start(f32[768]{0:T(1024)} %param.27) | copy-start | bytes 9220
  19.2 9.4 %copy-start.11 = (f32[768]{0:T(1024)S(1)}, f32[768]{0:T(1024)}, u32[]{:S(2)}) copy-start(f32[768]{0:T(1024)} %param.29) | copy-start | bytes 9220
  19.2 10.0 %copy-start.12 = (f32[768]{0:T(1024)S(1)}, f32[768]{0:T(1024)}, u32[]{:S(2)}) copy-start(f32[768]{0:T(1024)} %param.32) | copy-start | bytes 9220
  19.2 10.6 %copy-start.13 = (f32[768]{0:T(1024)S(1)}, f32[768]{0:T(1024)}, u32[]{:S(2)}) copy-start(f32[768]{0:T(1024)} %param.35) | copy-start | bytes 9220
  19.2 11.2 %copy-start.14 = (f32[768]{0:T(1024)S(1)}, f32[768]{0:T(1024)}, u32[]{:S(2)}) copy-start(f32[768]{0:T(1024)} %param.34) | copy-start | bytes 9220
  19.2 11.7 %copy-start.15 = (f32[768]{0:T(1024)S(1)}, f32[768]{0:T(1024)}, u32[]{:S(2)}) copy-start(f32[768]{0:T(1024)} %param.36) | copy-start | bytes 9220
  19.2 12.3 %copy-start.18 = (s32[8]{0:T(128)S(1)}, s32[8]{0:T(128)}, u32[]{:S(2)}) copy-start(s32[8]{0:T(128)} %param.24) | copy-start | bytes 100
  19.3 12.5 %copy-start.19 = (s32[8]{0:T(128)S(1)}, s32[8]{0:T(128)}, u32[]{:S(2)}) copy-start(s32[8]{0:T(128)} %param.25) | copy-start | bytes 100
  19.3 80.2 %all-to-all-start = ((bf16[8,264,768]{2,1,0:T(8,128)(2,1)}), bf16[8,264,768]{2,1,0:T(8,128)(2,1)S(1)}, u32[]{:S(2)}, u32[]{:S(2)}) async-start(bf16[8,264,768]{2,1,0:T(8,128)(2,1)} %get-tuple-element.86), calls=%async_computation | async-start | bytes 6488064 | tf_op jit(solution)/shard_map/all_to_all | solution.py:852
  26.7 123.9 %all-gather.7.cloned.1.call-start = ((), (), s32[]{:S(2)}) async-start(), calls=%async_computation.12 | async-start | bytes 5898240 | tf_op jit(solution)/shard_map/all_gather | solution.py:978
  99.5 41.0 %copy-start.3 = (bf16[8,264,768]{2,1,0:T(8,128)(2,1)}, bf16[8,264,768]{2,1,0:T(8,128)(2,1)S(1)}, u32[]{:S(2)}) copy-start(bf16[8,264,768]{2,1,0:T(8,128)(2,1)S(1)} %all-to-all-done.refs_1_.g_ref) | copy-start | bytes 9732100
  140.5 4.5 copy-start.17
  140.5 43.0 %all-to-all-start.2 = ((bf16[8,136,768]{2,1,0:T(8,128)(2,1)}), bf16[8,136,768]{2,1,0:T(8,128)(2,1)}, u32[]{:S(2)}, u32[]{:S(2)}) async-start(bf16[8,136,768]{2,1,0:T(8,128)(2,1)} %get-tuple-element.88), calls=%async_computation.2 | async-start | bytes 3342336 | tf_op jit(solution)/shard_map/all_to_all | solution.py:852
  183.5 43.9 %all-to-all-start.3 = ((bf16[8,128,768]{2,1,0:T(8,128)(2,1)}), bf16[8,128,768]{2,1,0:T(8,128)(2,1)S(1)}, u32[]{:S(2)}, u32[]{:S(2)}) async-start(bf16[8,128,768]{2,1,0:T(8,128)(2,1)} %get-tuple-element.97), calls=%async_computation.3 | async-start | bytes 3145728 | tf_op jit(solution)/shard_map/all_to_all | solution.py:852
  227.5 38.5 %copy-start.2 = (bf16[8,128,768]{2,1,0:T(8,128)(2,1)}, bf16[8,128,768]{2,1,0:T(8,128)(2,1)S(1)}, u32[]{:S(2)}) copy-start(bf16[8,128,768]{2,1,0:T(8,128)(2,1)S(1)} %all-to-all-done.3) | copy-start | bytes 4718596
  227.5 42.9 %all-to-all-start.4 = ((bf16[8,136,768]{2,1,0:T(8,128)(2,1)}), bf16[8,136,768]{2,1,0:T(8,128)(2,1)S(1)}, u32[]{:S(2)}, u32[]{:S(2)}) async-start(bf16[8,136,768]{2,1,0:T(8,128)(2,1)} %get-tuple-element.98), calls=%async_computation.4 | async-start | bytes 3342336 | tf_op jit(solution)/shard_map/all_to_all | solution.py:852
  231.1 271.9 %reduce-scatter.2.cloned.1.call-start = ((), (), s32[]{:S(2)}) async-start(), calls=%async_computation.13 | async-start | bytes 11857920 | tf_op jit(solution)/shard_map/reduce_scatter | solution.py:1004
  270.4 11.4 %copy-start.1 = (bf16[8,136,768]{2,1,0:T(8,128)(2,1)}, bf16[8,136,768]{2,1,0:T(8,128)(2,1)S(1)}, u32[]{:S(2)}) copy-start(bf16[8,136,768]{2,1,0:T(8,128)(2,1)S(1)} %all-to-all-done.4) | copy-start | bytes 5013508
  270.4 99.3 %all-to-all-start.5 = ((bf16[8,256,768]{2,1,0:T(8,128)(2,1)}), bf16[8,256,768]{2,1,0:T(8,128)(2,1)}, u32[]{:S(2)}, u32[]{:S(2)}) async-start(bf16[8,256,768]{2,1,0:T(8,128)(2,1)} %get-tuple-element.99), calls=%async_computation.5 | async-start | bytes 6291456 | tf_op jit(solution)/shard_map/all_to_all | solution.py:852
  275.8 1.2 collective-permute-start
  277.0 3.5 copy-start.20
  277.0 3.5 collective-permute-start.1
  280.6 0.5 copy-start.22
  303.3 46.6 %collective-permute-start.2 = (bf16[384,768]{1,0:T(8,128)(2,1)S(1)}, bf16[384,768]{1,0:T(8,128)(2,1)S(1)}, u32[]{:S(2)}, u32[]{:S(2)}) collective-permute-start(bf16[384,768]{1,0:T(8,128)(2,1)S(1)} %dynamic-slice_bitcast_fusion.2), channel_id=1, source_target_pairs={{0,1},{1,0},{2,3},{3,2},{4,5},{5,4},{6,7},{7,6},{8,9},{9,8},{10,11... | collective-permute-start | bytes 1769480 | tf_op jit(solution)/shard_map/ppermute | solution.py:861
  327.4 24.5 %collective-permute-start.4 = (bf16[384,1152]{1,0:T(8,128)(2,1)}, bf16[384,1152]{1,0:T(8,128)(2,1)S(1)}, u32[]{:S(2)}, u32[]{:S(2)}) collective-permute-start(bf16[384,1152]{1,0:T(8,128)(2,1)} %dynamic-slice_bitcast_fusion.1), channel_id=1, source_target_pairs={{0,1},{1,0},{2,3},{3,2},{4,5},{5,4},{6,7},{7,6},{8,9},{9,8},{10,11... | collective-permute-start | bytes 2654216 | tf_op jit(solution)/shard_map/ppermute | solution.py:861
  327.8 22.1 %copy-start.6 = (bf16[768,768]{1,0:T(8,128)(2,1)S(1)}, bf16[768,768]{1,0:T(8,128)(2,1)}, u32[]{:S(2)}) copy-start(bf16[768,768]{1,0:T(8,128)(2,1)} %get-tuple-element.112) | copy-start | bytes 3538948
  349.9 1.9 copy-start.4
  350.1 3.3 copy-start.5
  350.1 9.9 %collective-permute-start.3 = (bf16[192,768]{1,0:T(8,128)(2,1)S(1)}, bf16[192,768]{1,0:T(8,128)(2,1)S(1)}, u32[]{:S(2)}, u32[]{:S(2)}) collective-permute-start(bf16[192,768]{1,0:T(8,128)(2,1)S(1)} %dynamic-slice_bitcast_fusion.5), channel_id=1, source_target_pairs={{0,2},{1,3},{2,0},{3,1},{4,6},{5,7},{6,4},{7,5},{8,10},{9,11},{10,... | collective-permute-start | bytes 884744 | tf_op jit(solution)/shard_map/ppermute | solution.py:861
  352.2 16.5 %collective-permute-start.5 = (bf16[192,1152]{1,0:T(8,128)(2,1)S(1)}, bf16[192,1152]{1,0:T(8,128)(2,1)S(1)}, u32[]{:S(2)}, u32[]{:S(2)}) collective-permute-start(bf16[192,1152]{1,0:T(8,128)(2,1)S(1)} %dynamic-slice_bitcast_fusion.4), channel_id=1, source_target_pairs={{0,2},{1,3},{2,0},{3,1},{4,6},{5,7},{6,4},{7,5},{8,10},{9,11},{10,... | collective-permute-start | bytes 1327112 | tf_op jit(solution)/shard_map/ppermute | solution.py:861
  354.4 21.2 %collective-permute-start.11 = (bf16[384,1152]{1,0:T(8,128)(2,1)}, bf16[384,1152]{1,0:T(8,128)(2,1)S(1)}, u32[]{:S(2)}, u32[]{:S(2)}) collective-permute-start(bf16[384,1152]{1,0:T(8,128)(2,1)} %dynamic-slice_bitcast_fusion), channel_id=1, source_target_pairs={{0,1},{1,0},{2,3},{3,2},{4,5},{5,4},{6,7},{7,6},{8,9},{9,8},{10,11... | collective-permute-start | bytes 2654216 | tf_op jit(solution)/shard_map/ppermute | solution.py:861
  369.7 24.3 %all-to-all-start.6 = ((bf16[8,24,1920]{2,1,0:T(8,128)(2,1)}), bf16[8,24,1920]{2,1,0:T(8,128)(2,1)S(1)}, u32[]{:S(2)}, u32[]{:S(2)}) async-start(bf16[8,24,1920]{2,1,0:T(8,128)(2,1)} %bitcast.25), calls=%async_computation.6 | async-start | bytes 1474560 | tf_op jit(solution)/shard_map/all_to_all | solution.py:852
  375.8 11.5 %collective-permute-start.12 = (bf16[192,1152]{1,0:T(8,128)(2,1)S(1)}, bf16[192,1152]{1,0:T(8,128)(2,1)S(1)}, u32[]{:S(2)}, u32[]{:S(2)}) collective-permute-start(bf16[192,1152]{1,0:T(8,128)(2,1)S(1)} %dynamic-slice_bitcast_fusion.3), channel_id=1, source_target_pairs={{0,2},{1,3},{2,0},{3,1},{4,6},{5,7},{6,4},{7,5},{8,10},{9,11},{10,... | collective-permute-start | bytes 1327112 | tf_op jit(solution)/shard_map/ppermute | solution.py:861
  394.1 16.5 %all-to-all-start.7 = ((bf16[8,24,1152]{2,1,0:T(8,128)(2,1)}), bf16[8,24,1152]{2,1,0:T(8,128)(2,1)S(1)}, u32[]{:S(2)}, u32[]{:S(2)}) async-start(bf16[8,24,1152]{2,1,0:T(8,128)(2,1)} %bitcast.32), calls=%async_computation.7 | async-start | bytes 884736 | tf_op jit(solution)/shard_map/all_to_all | solution.py:852
  434.3 16.3 %all-to-all-start.9 = ((bf16[8,24,1152]{2,1,0:T(8,128)(2,1)}), bf16[8,24,1152]{2,1,0:T(8,128)(2,1)S(1)}, u32[]{:S(2)}, u32[]{:S(2)}) async-start(bf16[8,24,1152]{2,1,0:T(8,128)(2,1)} %broadcast_in_dim.5), calls=%async_computation.9 | async-start | bytes 884736 | tf_op jit(solution)/shard_map/all_to_all | solution.py:852
  438.2 19.5 %collective-permute-start.13 = (bf16[192,1920]{1,0:T(8,128)(2,1)S(1)}, bf16[192,1920]{1,0:T(8,128)(2,1)S(1)}, u32[]{:S(2)}, u32[]{:S(2)}) collective-permute-start(bf16[192,1920]{1,0:T(8,128)(2,1)S(1)} %bitcast.85), channel_id=1, source_target_pairs={{0,2},{1,3},{2,0},{3,1},{4,6},{5,7},{6,4},{7,5},{8,10},{9,11},{10,... | collective-permute-start | bytes 2211848 | tf_op jit(solution)/shard_map/ppermute | solution.py:861
  450.6 14.9 %collective-permute-start.15 = (bf16[192,1152]{1,0:T(8,128)(2,1)S(1)}, bf16[192,1152]{1,0:T(8,128)(2,1)}, u32[]{:S(2)}, u32[]{:S(2)}) collective-permute-start(bf16[192,1152]{1,0:T(8,128)(2,1)S(1)} %bitcast.93), channel_id=1, source_target_pairs={{0,2},{1,3},{2,0},{3,1},{4,6},{5,7},{6,4},{7,5},{8,10},{9,11},{10,... | collective-permute-start | bytes 1327112 | tf_op jit(solution)/shard_map/ppermute | solution.py:861
  452.2 14.8 %copy-start.8 = (f32[8,768]{1,0:T(8,128)S(1)}, f32[8,768]{1,0:T(8,128)}, u32[]{:S(2)}) copy-start(f32[8,768]{1,0:T(8,128)} %get-tuple-element.118) | copy-start | bytes 73732
  452.2 14.9 %copy-start.16 = (f32[8,1]{1,0:T(8,128)S(1)}, f32[8,1]{1,0:T(8,128)}, u32[]{:S(2)}) copy-start(f32[8,1]{1,0:T(8,128)} %get-tuple-element.119) | copy-start | bytes 100
  452.2 15.0 %copy-start.7 = (f32[8,384]{1,0:T(8,128)S(1)}, f32[8,384]{1,0:T(8,128)}, u32[]{:S(2)}) copy-start(f32[8,384]{1,0:T(8,128)} %get-tuple-element.116) | copy-start | bytes 36868
  458.1 30.2 %copy-start.21 = (f32[8]{0:T(128)S(1)}, f32[8]{0:T(128)}, u32[]{:S(2)}) copy-start(f32[8]{0:T(128)} %copy-done.20) | copy-start | bytes 100
  458.1 30.2 %copy-start.23 = (f32[8]{0:T(128)S(1)}, f32[8]{0:T(128)}, u32[]{:S(2)}) copy-start(f32[8]{0:T(128)} %copy-done.22) | copy-start | bytes 100
  458.1 34.6 %collective-permute-start.14 = (bf16[384,1920]{1,0:T(8,128)(2,1)S(1)}, bf16[384,1920]{1,0:T(8,128)(2,1)}, u32[]{:S(2)}, u32[]{:S(2)}) collective-permute-start(bf16[384,1920]{1,0:T(8,128)(2,1)S(1)} %maximum_select_fusion.2), channel_id=1, source_target_pairs={{0,1},{1,0},{2,3},{3,2},{4,5},{5,4},{6,7},{7,6},{8,9},{9,8},{10,11... | collective-permute-start | bytes 4423688 | tf_op jit(solution)/shard_map/ppermute | solution.py:861
  466.9 23.9 %collective-permute-start.16 = (bf16[384,1152]{1,0:T(8,128)(2,1)S(1)}, bf16[384,1152]{1,0:T(8,128)(2,1)S(1)}, u32[]{:S(2)}, u32[]{:S(2)}) collective-permute-start(bf16[384,1152]{1,0:T(8,128)(2,1)S(1)} %maximum_select_fusion.3), channel_id=1, source_target_pairs={{0,1},{1,0},{2,3},{3,2},{4,5},{5,4},{6,7},{7,6},{8,9},{9,8},{10,11... | collective-permute-start | bytes 2654216 | tf_op jit(solution)/shard_map/ppermute | solution.py:861
  469.4 1.4 collective-permute-start.6
  470.8 4.1 collective-permute-start.7
  474.8 4.2 collective-permute-start.8
  479.0 4.2 collective-permute-start.9
  483.2 5.1 collective-permute-start.10
  503.0 2.8 copy-start
Sparse Core Ops, SparseCore 0:
  9.6 40.2 all-gather.4
  51.4 37.3 all-gather.6
  270.6 78.8 reduce-scatter.1

commit v2 on v1

--- a/solution.py
+++ b/solution.py
@@ -17,6 +17,7 @@
 BF16 = jnp.bfloat16
 VMEM_LIMIT = 56 * 1024 * 1024
 EXTRA = 8
+COVER = 4e10
 ATTEND_CALLS = 2
 
 
@@ -55,10 +56,11 @@
     return jnp.concatenate([scores[: keys - block], last], axis=0)
 
 
-def attend_kernel(block, q_ref, k_ref, v_ref, context_ref, log_ref):
+def attend_kernel(block, q_ref, k_ref, v_ref, context_ref, weights_ref):
     rows = q_ref.shape[0]
     keys = k_ref[...]
     values_t = jnp.transpose(v_ref[...])
+    place = 0
     for first in range(0, rows, block):
         span = first + block
         query = q_ref[first:span, :]
@@ -68,24 +70,26 @@
             peak = jnp.max(scores, axis=0, keepdims=True)
             powers = jnp.exp(scores - peak)
             total = jnp.sum(powers, axis=0, keepdims=True)
-            out = mm(values_t[head * HEAD_DIM : (head + 1) * HEAD_DIM, :span], powers.astype(BF16))
-            parts.append(out / total)
-            log_ref[0, head : head + 1, first:span] = peak + jnp.log(total)
+            weights = (powers * (1.0 / total)).astype(BF16)
+            weights_ref[0, head, place : place + span, :] = weights
+            parts.append(mm(values_t[head * HEAD_DIM : (head + 1) * HEAD_DIM, :span], weights))
         context_ref[first:span, :] = jnp.transpose(jnp.concatenate(parts, axis=0)).astype(BF16)
+        place += span
 
 
 def attend(queries, keys, values, block=256):
     rows, width = queries.shape
     pairs = width // PAIR
+    kept = sum(range(block, rows + 1, block))
     spec = pl.BlockSpec((rows, PAIR), lambda p: (0, p))
     return pl.pallas_call(
         functools.partial(attend_kernel, block),
         grid=(pairs,),
         in_specs=[spec, spec, spec],
-        out_specs=[spec, pl.BlockSpec((1, 2, rows), lambda p: (p, 0, 0))],
+        out_specs=[spec, pl.BlockSpec((1, 2, kept, block), lambda p: (p, 0, 0, 0))],
         out_shape=[
             jax.ShapeDtypeStruct((rows, width), BF16),
-            jax.ShapeDtypeStruct((pairs, 2, rows), F32),
+            jax.ShapeDtypeStruct((pairs, 2, kept, block), BF16),
         ],
         compiler_params=params("arbitrary"),
         cost_estimate=cost(4 * rows * rows * width * 2, rows * width * 8, pairs * 2 * rows * rows),
@@ -93,27 +97,29 @@
     )(queries, keys, values)
 
 
-def attend_back_kernel(block, q_ref, k_ref, v_ref, log_ref, g_ref, normed_ref,
+def attend_back_kernel(block, q_ref, k_ref, v_ref, weights_ref, g_ref, normed_ref,
                        dq_ref, dk_ref, dv_ref, packed_ref, sums_ref, dq_acc, dk_acc, dv_acc):
     rows = q_ref.shape[0]
     keys = k_ref[...]
     values = v_ref[...]
     keys_t = jnp.transpose(keys)
+    place = weights_ref.shape[2]
     for first in reversed(range(0, rows, block)):
         span = first + block
+        place -= span
         query = q_ref[first:span, :]
         grad = g_ref[first:span, :]
         grad_query, probs_both, scores_both, query_both, grad_both = [], [], [], [], []
         for head in range(2):
             query_h = head_mask(query, head)
             grad_h = head_mask(grad, head)
-            scores = causal(mm_nt(keys[:span], query_h), block)
-            probs = jnp.exp(scores - log_ref[0, head : head + 1, first:span])
+            weights = weights_ref[0, head, place : place + span, :]
+            probs = weights.astype(F32)
             grad_probs = mm_nt(values[:span], grad_h)
             inner = jnp.sum(probs * grad_probs, axis=0, keepdims=True)
             grad_scores = (probs * (grad_probs - inner)).astype(BF16)
             grad_query.append(mm(keys_t[head * HEAD_DIM : (head + 1) * HEAD_DIM, :span], grad_scores))
-            probs_both.append(probs.astype(BF16))
+            probs_both.append(weights)
             scores_both.append(grad_scores)
             query_both.append(query_h)
             grad_both.append(grad_h)
@@ -146,7 +152,7 @@
     )
 
 
-def attend_back(queries, keys, values, logs, grad_context, normed_t, start, pairs, block=256):
+def attend_back(queries, keys, values, weights, grad_context, normed_t, start, pairs, block=256):
     rows, width = queries.shape
     spec = pl.BlockSpec((rows, PAIR), lambda p: (0, p + start))
     out_spec = pl.BlockSpec((rows, PAIR), lambda p: (0, p))
@@ -157,7 +163,7 @@
             spec,
             spec,
             spec,
-            pl.BlockSpec((1, 2, rows), lambda p: (p + start, 0, 0)),
+            pl.BlockSpec((1, 2) + weights.shape[2:], lambda p: (p + start, 0, 0, 0)),
             spec,
             pl.BlockSpec((width, rows), lambda p: (0, 0)),
         ],
@@ -179,9 +185,9 @@
             pltpu.VMEM((rows, PAIR), F32),
         ],
         compiler_params=params("arbitrary"),
-        cost_estimate=cost(rows * PAIR, rows * PAIR),
+        cost_estimate=cost(rows, rows),
         name="attend_back",
-    )(queries, keys, values, logs, grad_context, normed_t)
+    )(queries, keys, values, weights, grad_context, normed_t)
 
 
 def normalise(values):
@@ -235,7 +241,7 @@
     return (places == slots).astype(F32).astype(BF16)
 
 
-def route_kernel(experts, capacity, row_ref, col_ref, grad_ref, slots_ref, columns_ref, out_ref, count_row):
+def route_kernel(experts, capacity, row_ref, grad_ref, slots_ref, columns_ref, out_ref, count_row):
     step = pl.program_id(0)
     rows = row_ref.shape[1]
     width = grad_ref.shape[1]
@@ -243,22 +249,30 @@
 
     @pl.when(step == 0)
     def _():
-        first = lax.broadcasted_iota(jnp.int32, (rows, rows), 0)
-        second = lax.broadcasted_iota(jnp.int32, (rows, rows), 1)
+        block = 256
         ids = row_ref[...]
         picked = picked_rows(ids, experts).astype(F32)
-        before = mm(picked.astype(BF16), (first < second).astype(F32).astype(BF16))
-        place = jnp.sum(before * picked, axis=0, keepdims=True).astype(jnp.int32)
-        slots_ref[...] = ids * capacity + place
-        ids = col_ref[...]
-        picked = (lax.broadcasted_iota(jnp.int32, (rows, 128), 1) == ids).astype(F32)
-        before = mm((second < first).astype(F32).astype(BF16), picked.astype(BF16))
-        place = jnp.sum(before * picked, axis=1, keepdims=True).astype(jnp.int32)
+        first = lax.broadcasted_iota(jnp.int32, (block, block), 0)
+        second = lax.broadcasted_iota(jnp.int32, (block, block), 1)
+        earlier = (first < second).astype(F32).astype(BF16)
+        passed = jnp.zeros((experts, 1), F32)
+        places = []
+        for start in range(0, rows, block):
+            own = picked[:, start : start + block]
+            before = mm(own.astype(BF16), earlier) + passed
+            places.append(jnp.sum(before * own, axis=0, keepdims=True))
+            passed = passed + jnp.sum(own, axis=1, keepdims=True)
+        place = jnp.concatenate(places, axis=1).astype(jnp.int32)
+        slots = ids * capacity + place
         late = experts * half + ids * (half + EXTRA) + place - half
-        columns_ref[:, 0:1] = jnp.where(place < half, ids * half + place, late)
-        columns_ref[:, 1:2] = ids * capacity + place
+        mixed = jnp.where(place < half, ids * half + place, late)
+        slots_ref[...] = slots
+        both = jnp.concatenate([mixed, slots, jnp.zeros((6, rows), jnp.int32)], axis=0)
+        columns_ref[...] = jnp.transpose(both.astype(F32))[:, 0:2].astype(jnp.int32)
         count_row[...] = jnp.zeros_like(count_row)
-        count_row[0:1, 0:128] = jnp.sum(picked, axis=0, keepdims=True)
+        lanes = lax.broadcasted_iota(jnp.int32, (experts, 128), 1)
+        spread = jnp.where(lanes == lax.broadcasted_iota(jnp.int32, (experts, 128), 0), passed, 0.0)
+        count_row[0:1, 0:128] = jnp.sum(spread, axis=0, keepdims=True)
 
     chosen = one_hot_rows(slots_ref[...], step * capacity, capacity)
     out_ref[0, :capacity, :] = mm(chosen, grad_ref[...]).astype(BF16)
@@ -273,7 +287,6 @@
         grid=(experts,),
         in_specs=[
             pl.BlockSpec((1, rows), whole),
-            pl.BlockSpec((rows, 1), whole),
             pl.BlockSpec((rows, width), whole),
         ],
         out_specs=[
@@ -290,7 +303,7 @@
         compiler_params=params("arbitrary"),
         cost_estimate=cost(2 * experts * capacity * rows * width, 6 * rows * width),
         name="route",
-    )(routes.reshape(1, rows), routes, grad_out)
+    )(routes.reshape(1, rows), grad_out)
 
 
 def project_kernel(tokens_ref, gain_ref, shift_ref, wq_ref, bq_ref, wk_ref, wv_ref, bv_ref,
@@ -728,7 +741,7 @@
         ],
         scratch_shapes=[pltpu.VMEM((width, width), F32)],
         compiler_params=params("arbitrary"),
-        cost_estimate=cost(rows * width, rows * width),
+        cost_estimate=cost(rows, rows),
         name="combine",
     )(weight, back0, back1, dots0, dots1, columns, ids, logits, pull, hidden, grad_out, context, moe_in, w_out,
       router_rows, gain)
@@ -782,7 +795,7 @@
             jax.ShapeDtypeStruct((8, width), F32),
         ],
         compiler_params=params("arbitrary"),
-        cost_estimate=cost(6 * rows * width * width, 16 * rows * width + 6 * width * width),
+        cost_estimate=cost(COVER, 4096),
         name="close",
     )(*flat, tokens, hid_grad, gain, w_query, w_key, w_value)
 
@@ -812,40 +825,77 @@
         out_specs=row_spec,
         out_shape=jax.ShapeDtypeStruct((rows, width), BF16),
         compiler_params=params("arbitrary"),
-        cost_estimate=cost(2 * rows * width * count, 6 * rows * width + 2 * count * width),
+        cost_estimate=cost(COVER, 4096),
         name="block_output",
     )(back, columns, ids, logits, hidden)
 
 
-def unpack_kernel(early_ref, late_ref, out_ref, *refs):
-    width = out_ref.shape[1]
-    out_ref[...] = early_ref[:, :width].astype(F32)
-    place = 0
-    for ref, first in ((early_ref, width), (late_ref, 0)):
-        for base in range(first, ref.shape[1], 3 * PAIR):
+def unpack_expert_kernel(hidden, packed_ref, in_ref, down_ref, bias_ref):
+    width = in_ref.shape[0]
+    in_ref[...] = packed_ref[:width, :hidden].astype(F32)
+    down_ref[...] = packed_ref[width : width + hidden, :].astype(F32)
+    bias_ref[...] = packed_ref[width + hidden :, :].astype(F32)
+
+
+def unpack_expert(packed, hidden):
+    rows, width = packed.shape
+    return pl.pallas_call(
+        functools.partial(unpack_expert_kernel, hidden),
+        out_shape=[
+            jax.ShapeDtypeStruct((width, hidden), F32),
+            jax.ShapeDtypeStruct((hidden, width), F32),
+            jax.ShapeDtypeStruct((EXTRA, width), F32),
+        ],
+        compiler_params=params(),
+        cost_estimate=cost(COVER, 4096),
+        name="unpack_expert",
+    )(packed)
+
+
+def unpack_kernel(lead, upper_ref, own_ref, other_ref, *refs):
+    outs = refs[len(refs) - (3 + lead) :]
+    width = outs[-1].shape[1]
+
+    def write(ref):
+        base = 0
+        if lead:
+            base = outs[0].shape[1]
+            outs[0][...] = ref[:, :base].astype(F32)
+        for place in range(0, width, PAIR):
             for index in range(3):
-                lanes = ref[:, base + index * PAIR : base + (index + 1) * PAIR]
-                refs[index][:, place : place + PAIR] = lanes.astype(F32)
-            place += PAIR
-
-
-def unpack(early, late, tile=256):
-    rows = early.shape[0]
-    width = (early.shape[1] + late.shape[1]) // 4
-    spec = pl.BlockSpec((tile, width), lambda t: (t, 0))
-    return pl.pallas_call(
-        unpack_kernel,
-        grid=(rows // tile,),
-        in_specs=[
-            pl.BlockSpec((tile, early.shape[1]), lambda t: (t, 0)),
-            pl.BlockSpec((tile, late.shape[1]), lambda t: (t, 0)),
-        ],
-        out_specs=[spec] * 4,
-        out_shape=[jax.ShapeDtypeStruct((rows, width), F32)] * 4,
-        compiler_params=params("arbitrary"),
-        cost_estimate=cost(rows * width, 24 * rows * width),
+                first = base + 3 * place + index * PAIR
+                outs[lead + index][:, place : place + PAIR] = ref[:, first : first + PAIR].astype(F32)
+
+    own = pl.program_id(0) == upper_ref[0, 0]
+
+    @pl.when(own)
+    def _():
+        write(own_ref)
+
+    @pl.when(jnp.logical_not(own))
+    def _():
+        write(other_ref)
+
+
+def unpack(upper, own, other, blocks, width, lead, earlier=()):
+    total, lanes = own.shape
+    rows = total // blocks
+    span = (lanes - lead * width) // 3
+    offset = 0 if lead else width // span - 1
+    source = pl.BlockSpec((rows, lanes), lambda c, x: (x, 0))
+    return pl.pallas_call(
+        functools.partial(unpack_kernel, lead),
+        grid=(2, blocks),
+        in_specs=[pl.BlockSpec(memory_space=pltpu.SMEM), source, source]
+        + [pl.BlockSpec(memory_space=pl.ANY)] * len(earlier),
+        out_specs=[pl.BlockSpec((rows, width), lambda c, x: (c * blocks + x, 0))] * lead
+        + [pl.BlockSpec((rows, span), lambda c, x: (c * blocks + x, offset))] * 3,
+        out_shape=[jax.ShapeDtypeStruct((2 * total, width), F32)] * (3 + lead),
+        input_output_aliases={3 + index: index for index in range(len(earlier))},
+        compiler_params=params("arbitrary", "arbitrary"),
+        cost_estimate=cost(COVER, 4096),
         name="unpack",
-    )(early, late)
+    )(upper, own, other, *earlier)
 
 
 def swap(blocks, axis):
@@ -916,10 +966,10 @@
     return spread_out(value, "wide").reshape(-1, value.shape[1])
 
 
-def narrow_whole(value):
-    for bit in reversed(list(bits("narrow"))):
+def narrow_half(value):
+    for bit in reversed(list(bits("narrow"))[1:]):
         value = rejoin(value, "narrow", bit)
-    return value
+    return value, trade(value, "narrow", 1)
 
 
 def small_sum(value):
@@ -980,7 +1030,7 @@
     normed_t, queries, keys, values = project(
         tokens, row(norm1_gain), row(norm1_bias), w_query, row(bias_query), w_key, w_value, row(bias_value)
     )
-    context, logs = attend(queries, keys, values)
+    context, soft_weights = attend(queries, keys, values)
     hidden, moe_in, logits = settle(
         context, tokens, w_out, row(bias_out), row(norm2_gain), row(norm2_bias), router_rows
     )
@@ -989,7 +1039,7 @@
     x0 = swap(after(first, grad_rows), "wide")
     counted = jnp.sum(grad_rows[:, capacity, :experts].astype(F32), axis=0)
     fraction = narrow_sum(counted) / total_tokens
-    x1 = swap(after(second, x0), "wide")
+    x1 = swap(after(second, x0, fraction), "wide")
     act, up, out, back0, dots = expert(
         x0, grad_rows, gathered_in, gathered_bias, gathered_down, bias_down, 0
     )
@@ -1000,19 +1050,15 @@
     back1 = arrived = swap(after(back1, back0), "wide")
     scale = jnp.sum(x1[:, half : half + 3, :capacity].astype(F32), axis=1)
     scale = jnp.transpose(scale.reshape(wide_count, 2, half), (1, 0, 2)).reshape(2, 1, wide_count * half)
-    expert_grad = weight_grads(after(x0, back0), x1, grad_rows, act, up, scale)
-    expert_grad = lax.psum_scatter(after(expert_grad, arrived), "narrow", scatter_dimension=0).astype(F32)
+    expert_sums = weight_grads(after(x0, back0), x1, grad_rows, act, up, scale)
+    expert_grad = lax.psum_scatter(after(expert_sums, arrived), "narrow", scatter_dimension=0)
+    grad_w_in, grad_w_down, bias_rows = unpack_expert(expert_grad, hidden_cols)
     share = width // narrow_count
-    grad_w_in = expert_grad[:width, :hidden_cols]
-    grad_w_down = expert_grad[width : width + hidden_cols]
-    grad_bias_in = expert_grad[width + hidden_cols : width + hidden_cols + 1, :hidden_cols]
+    grad_bias_in = bias_rows[0:1, :hidden_cols]
     grad_bias_down = lax.dynamic_slice_in_dim(
-        expert_grad[width + hidden_cols + 1 : width + hidden_cols + 2],
-        lax.axis_index("narrow") * share,
-        share,
-        1,
-    )
-    back1 = after(back1, expert_grad)
+        bias_rows[1:2], lax.axis_index("narrow") * share, share, 1
+    )
+    back1 = after(back1, expert_sums)
     returned = swap(after(expert_out, arrived), "wide")
 
     extras = jnp.transpose(back1[:, half:, :half], (1, 0, 2))
@@ -1043,7 +1089,7 @@
     packed = [narrow_part(out_grad)]
     for call in range(ATTEND_CALLS):
         dq, dk, dv, weights, column_sums = attend_back(
-            queries, keys, values, logs, con_grad, normed_t, call * span, span
+            queries, keys, values, soft_weights, con_grad, normed_t, call * span, span
         )
         grads.append((dq, dk, dv))
         packed.append(narrow_part(weights))
@@ -1054,19 +1100,22 @@
     block_out = block_output(
         returned.reshape(experts * capacity, width), columns, ids, logits, hidden
     )
-    early = wide_part(after(early, returned))
-    late = wide_part(after(packed[-1], early, norm_sums))
-    early = wide_whole(after(early, late, block_out))
-    late = wide_whole(after(late, early, grad_w_in, grad_w_down))
-    early = narrow_whole(early)
-    late = narrow_whole(late)
     bias_sums = jnp.concatenate(bias_sums, axis=1)
     prob_row = jnp.pad(prob_sums.reshape(1, experts), ((0, 0), (0, width - experts)))
     small = small_sum(
         jnp.concatenate([norm_sums[:2], bias_sums[:2], sums[:3], prob_row, router_grad], axis=0)
     )
+    early = wide_part(after(early, returned))
+    late = wide_part(after(packed[-1], early, norm_sums))
+    early = wide_whole(after(early, late, small))
+    late = wide_whole(after(late, early, bias_rows, block_out))
+    early, early_other = narrow_half(early)
+    late, late_other = narrow_half(late)
     balance_loss = experts * jnp.sum(fraction * (small[7, :experts] / total_tokens))
-    grad_w_out, *weights = unpack(early, late)
+    upper = is_upper("narrow", 1).astype(jnp.int32).reshape(1, 1)
+    blocks = narrow_count // 2
+    grad_w_out, *weights = unpack(upper, early, early_other, blocks, width, 1)
+    weights = unpack(upper, late, late_other, blocks, width, 0, weights)
     return (
         block_out,
         balance_loss,

time: 526 us -> 491 us (0.933)
  blocking collectives: 69.3 us -> 5.49 us
  waiting for transfers between devices: 90.4 us -> 111 us
  Pallas kernels: 245 us -> 260 us
  other arithmetic: 18 us -> 7.58 us
  starting transfers between devices: 58.6 us -> 64.7 us
    all_to_all x2 -> x0, blocking collectives: 63.7 us -> none  [swap(): return lax.all_to_all(blocks, axis, split_axis=0, concat_axis=0, tiled=True)]
    all_to_all x8 -> x10, waiting for transfers between devices: 48.6 us -> 75.8 us  [swap(): return lax.all_to_all(blocks, axis, split_axis=0, concat_axis=0, tiled=True)]
    all_to_all x8 -> x10, starting transfers between devices: 39.9 us -> 49.3 us  [swap(): return lax.all_to_all(blocks, axis, split_axis=0, concat_axis=0, tiled=True)]
    pallas_call x1 -> x3, Pallas kernels: 5.99 us -> 14.2 us  [the longest x2 10.2 us: unpack(): pl.pallas_call(functools.partial(unpack_kernel, lead), grid=(2, blocks),...]
    select_n x4 -> x2, other arithmetic: 8.02 us -> 0.7 us  [rejoin(): return jnp.where(upper, jnp.concatenate([got, value], axis=0), low)]
    ppermute x17, waiting for transfers between devices: 40.4 us -> 34 us  [trade(): lax.ppermute(value, axis, [(place, place ^ bit) for place in range(count)])]
  transfers between devices with their start and end apart: 28 -> 30, of which waited for: 17 -> 19; matrix products, arithmetic and copies ran while one was open for 6% -> 5% of each run, Pallas kernels for 47% -> 53%
where the time goes in v2:
time: 491 us; the launch traced here: 482 us
  Pallas kernels  260 us (53%)
  waiting for transfers between devices  111 us (23%)
  starting transfers between devices  64.7 us (13%)
  between operations  16.5 us (3%)
  local copies, waits for them, and re-layouts  16.4 us (3%)
  other arithmetic  7.58 us (2%)
  blocking collectives  5.49 us (1%)
    all_to_all x10, waiting for transfers between devices, swap(): return lax.all_to_all(blocks, axis, split_axis=0, concat_axis=0, tiled=True)  75.8 us
    pallas_call x2, Pallas kernels, expert(): pl.pallas_call(functools.partial(expert_kernel, parts, chunk), grid=(part...  66.1 us
    all_to_all x10, starting transfers between devices, swap(): return lax.all_to_all(blocks, axis, split_axis=0, concat_axis=0, tiled=True)  49.3 us
    pallas_call x2, Pallas kernels, attend_back(): pl.pallas_call(functools.partial(attend_back_kernel, block), grid=(pairs,...  46.5 us
    ppermute x17, waiting for transfers between devices, trade(): lax.ppermute(value, axis, [(place, place ^ bit) for place in range(count)])  34 us
    pallas_call x1, Pallas kernels, weight_grads(): pl.pallas_call(functools.partial(weight_kernel, parts), grid=(parts, 2),...  33.6 us
    pallas_call x1, Pallas kernels, attend(): pl.pallas_call(functools.partial(attend_kernel, block), grid=(pairs,), in...  30.6 us
    pallas_call x1, Pallas kernels, combine(): pl.pallas_call(combine_kernel, grid=(rows // tile,), in_specs=[pl.BlockSp...  19.7 us
  transfers between devices with their start and end apart: 30, of which 19 were waited for; matrix products, arithmetic and copies ran while one was open for 5% of the time, Pallas kernels for 53%

profile of v2, /device:TPU:0, one launch (start us, length us, event | category | flops | bytes accessed | tf_op | source)
XLA Modules:
  0.0 481.6 jit_solution(13047550542953180131)
XLA Ops:
  7.9 7.8 %route.1 = (s32[1,1024]{1,0:T(1,128)}, s32[1024,2]{1,0:T(8,128)}, bf16[8,264,768]{2,1,0:T(8,128)(2,1)}) custom-call(s32[1,1024]{1,0:T(1,128)} %bitcast.100, bf16[1024,768]{1,0:T(8,128)(2,1)} %grad_ref.3), custom_call_target="tpu_custom_call" | custom-call | flops 3221225472 | bytes 4718592 | tf_op jit(solution)/shard_map/route/pallas_call | solution.py:285
  15.8 7.4 %all-to-all-start = ((bf16[8,264,768]{2,1,0:T(8,128)(2,1)}), bf16[8,264,768]{2,1,0:T(8,128)(2,1)S(1)}, u32[]{:S(2)}, u32[]{:S(2)}) async-start(bf16[8,264,768]{2,1,0:T(8,128)(2,1)} %get-tuple-element.93), calls=%async_computation | async-start | bytes 6488064 | tf_op jit(solution)/shard_map/all_to_all | solution.py:902
  23.3 0.7 all-gather.7.cloned.1.call-update
  28.9 8.3 %project.1 = (bf16[768,1024]{1,0:T(8,128)(2,1)}, bf16[1024,768]{1,0:T(8,128)(2,1)}, bf16[1024,768]{1,0:T(8,128)(2,1)}, bf16[1024,768]{1,0:T(8,128)(2,1)}) custom-call(bf16[1024,768]{1,0:T(8,128)(2,1)} %refs_6_.1, f32[1,768]{1,0:T(1,128)} %reshape.175.gain_ref.refs_8_, f32[1,768]{1,0:T(1,128)} %reshape.176.shift_ref, bf16[768,768]{1,0:T(8,128)(2,1)} %refs_9_.1, ...), custom_call_target="tpu_custom_call" | custom-call | flops 3623878656 | bytes 11403264 | tf_op jit(solution)/shard_map/project/pallas_call | solution.py:324
  37.2 30.6 %attend.1 = (bf16[1024,768]{1,0:T(8,128)(2,1)}, bf16[6,2,2560,256]{3,2,1,0:T(8,128)(2,1)}) custom-call(bf16[1024,768]{1,0:T(8,128)(2,1)} %get-tuple-element.85.q_ref, bf16[1024,768]{1,0:T(8,128)(2,1)} %get-tuple-element.86.k_ref, bf16[1024,768]{1,0:T(8,128)(2,1)} %get-tuple-element.87.v_ref), custom_call_target="tpu_custom_call" | custom-call | flops 6442450944 | bytes 6291456 | tf_op jit(solution)/shard_map/attend/pallas_call | solution.py:85
  67.8 6.9 %settle.1 = (f32[1024,768]{1,0:T(8,128)}, bf16[1024,768]{1,0:T(8,128)(2,1)}, f32[8,1024]{1,0:T(8,128)}) custom-call(bf16[1024,768]{1,0:T(8,128)(2,1)} %get-tuple-element.88.context_ref, bf16[1024,768]{1,0:T(8,128)(2,1)} %refs_6_.1, bf16[768,768]{1,0:T(8,128)(2,1)} %w_out_ref.3, f32[1,768]{1,0:T(1,128)} %reshape.179.bias_ref, f32[1,768]{1,0:T(1,128)} %reshape.180.gain_ref, ...), custom_call_target="tpu_custom_call" | custom-call | flops 1207959552 | bytes 9043968 | tf_op jit(solution)/shard_map/settle/pallas_call | solution.py:352
  74.6 8.5 %dispatch.1 = (bf16[8,128,768]{2,1,0:T(8,128)(2,1)}, bf16[8,136,768]{2,1,0:T(8,128)(2,1)}) custom-call(f32[1,1]{1,0:T(1,128)} %bitcast.2.weight_ref, s32[1,1024]{1,0:T(1,128)} %get-tuple-element.84.slots_ref, s32[1,1024]{1,0:T(1,128)} %bitcast.101, f32[8,1024]{1,0:T(8,128)} %get-tuple-element.89.logits_ref, bf16[1024,768]{1,0:T(8,128)(2,1)} %get-tuple-element.90.moe_ref), custom_call_target="tpu_custom_call" | custom-call | flops 3221225472 | bytes 4718592 | tf_op jit(solution)/shard_map/dispatch/pallas_call | solution.py:399
  83.2 12.9 %all-to-all-done.refs_1_.g_ref = bf16[8,264,768]{2,1,0:T(8,128)(2,1)S(1)} async-done(((bf16[8,264,768]{2,1,0:T(8,128)(2,1)}), bf16[8,264,768]{2,1,0:T(8,128)(2,1)S(1)}, u32[]{:S(2)}, u32[]{:S(2)}) %all-to-all-start) | async-done | bytes 3244064 | tf_op jit(solution)/shard_map/all_to_all | solution.py:902
  96.1 4.3 all-to-all-start.1
  100.5 1.1 collective-permute-done
  101.6 1.5 collective-permute-start.1
  103.1 2.0 collective-permute-done.1
  105.7 31.3 %all-to-all-done.1.refs_0_.x0_ref = bf16[8,128,768]{2,1,0:T(8,128)(2,1)} async-done(((bf16[8,128,768]{2,1,0:T(8,128)(2,1)}), bf16[8,128,768]{2,1,0:T(8,128)(2,1)}, u32[]{:S(2)}, u32[]{:S(2)}) %all-to-all-start.1) | async-done | bytes 1572896 | tf_op jit(solution)/shard_map/all_to_all | solution.py:902
  137.0 4.3 all-to-all-start.2
  141.4 5.5 %all-gather.1.refs_3_ = bf16[4,1,768]{2,1,0:T(2,128)(2,1)} all-gather(bf16[1,1,768]{2,1,0:T(2,128)(2,1)S(1)} %bitcast.104), channel_id=2, replica_groups=mesh['wide'=8,'narrow'=4] {'narrow'}, dimensions={0}, use_global_device_ids=true | all-gather | bytes 7680 | tf_op jit(solution)/shard_map/all_gather | solution.py:1038
  146.9 33.0 %expert.2 = (bf16[4,2,1024,768]{3,2,1,0:T(8,128)(2,1)}, bf16[4,2,1024,768]{3,2,1,0:T(8,128)(2,1)}, bf16[8,256,768]{2,1,0:T(8,128)(2,1)}, bf16[8,128,768]{2,1,0:T(8,128)(2,1)}, bf16[8,8,128]{2,1,0:T(8,128)(2,1)}) custom-call(bf16[8,128,768]{2,1,0:T(8,128)(2,1)} %all-to-all-done.1.refs_0_.x0_ref, bf16[8,264,768]{2,1,0:T(8,128)(2,1)} %copy-done.2, ...), custom_call_target="tpu_custom_call" | custom-call | flops 14495514624 | bytes 12582912 | tf_op jit(solution)/shard_map/expert/pallas_call | solution.py:512
  180.1 5.9 %all-to-all-start.3 = ((bf16[8,128,768]{2,1,0:T(8,128)(2,1)}), bf16[8,128,768]{2,1,0:T(8,128)(2,1)S(1)}, u32[]{:S(2)}, u32[]{:S(2)}) async-start(bf16[8,128,768]{2,1,0:T(8,128)(2,1)} %get-tuple-element.104), calls=%async_computation.3 | async-start | bytes 3145728 | tf_op jit(solution)/shard_map/all_to_all | solution.py:902
  186.0 33.2 %expert.3 = (bf16[4,2,1024,768]{3,2,1,0:T(8,128)(2,1)}, bf16[4,2,1024,768]{3,2,1,0:T(8,128)(2,1)}, bf16[8,256,768]{2,1,0:T(8,128)(2,1)}, bf16[8,136,768]{2,1,0:T(8,128)(2,1)}) custom-call(bf16[8,136,768]{2,1,0:T(8,128)(2,1)} %all-to-all-done.2.refs_0_.x1_ref, ...), custom_call_target="tpu_custom_call", output_to_operand_aliasing={{0}: (6, {}), {1}: (7, {}), {2}: (8, {})} | custom-call | flops 14495514624 | bytes 12582912 | tf_op jit(solution)/shard_map/expert/pallas_call | solution.py:512
  219.2 4.3 all-to-all-done.3
  223.5 3.6 all-to-all-start.4
  227.2 1.4 convert_reduce_fusion
  228.5 33.6 %weight_grads.1 = bf16[4,1544,768]{2,1,0:T(8,128)(2,1)} custom-call(bf16[8,128,768]{2,1,0:T(8,128)(2,1)} %all-to-all-done.1.refs_0_.x0_ref, bf16[8,136,768]{2,1,0:T(8,128)(2,1)} %all-to-all-done.2.refs_0_.x1_ref, bf16[8,264,768]{2,1,0:T(8,128)(2,1)} %copy-done.2, bf16[4,2,1024,768]{3,2,1,0:T(8,128)(2,1)} %get-tuple-element.111.act_ref, ...), custom_call_target="tpu_custom_call" | custom-call | flops 28991029248 | bytes 25165824 | tf_op jit(solution)/shard_map/weight_grads/pallas_call | solution.py:608
  262.1 4.3 all-to-all-done.4
  266.4 4.7 all-to-all-start.5
  271.9 0.7 reshape.188.dots1_ref
  273.2 19.7 %combine.1 = (f32[1024,768]{1,0:T(8,128)}, bf16[1024,768]{1,0:T(8,128)(2,1)}, bf16[768,768]{1,0:T(8,128)(2,1)}, f32[8,768]{1,0:T(8,128)}, f32[8,768]{1,0:T(8,128)}, /*index=5*/f32[8,1]{1,0:T(8,128)}) custom-call(f32[1,1]{1,0:T(1,128)} %bitcast.2.weight_ref, bf16[1024,768]{1,0:T(8,128)(2,1)} %bitcast.80, bf16[1088,768]{1,0:T(8,128)(2,1)} %bitcast.79, ...), custom_call_target="tpu_custom_call" | custom-call | flops 1024 | bytes 1024 | tf_op jit(solution)/shard_map/combine/pallas_call | solution.py:705
  292.9 1.1 dynamic-slice_bitcast_fusion.2
  294.1 23.2 %attend_back.2 = (bf16[1024,384]{1,0:T(8,128)(2,1)}, bf16[1024,384]{1,0:T(8,128)(2,1)}, bf16[1024,384]{1,0:T(8,128)(2,1)}, bf16[768,1152]{1,0:T(8,128)(2,1)}, f32[8,384]{1,0:T(8,128)}) custom-call(bf16[1024,768]{1,0:T(8,128)(2,1)} %get-tuple-element.85.q_ref, bf16[1024,768]{1,0:T(8,128)(2,1)} %get-tuple-element.86.k_ref, ...), custom_call_target="tpu_custom_call" | custom-call | flops 1024 | bytes 1024 | tf_op jit(solution)/shard_map/attend_back/pallas_call | solution.py:159
  317.3 1.3 dynamic-slice_bitcast_fusion.1
  319.3 1.7 collective-permute-start.3
  321.1 23.4 %attend_back.3 = (bf16[1024,384]{1,0:T(8,128)(2,1)}, bf16[1024,384]{1,0:T(8,128)(2,1)}, bf16[1024,384]{1,0:T(8,128)(2,1)}, bf16[768,1152]{1,0:T(8,128)(2,1)}, f32[8,384]{1,0:T(8,128)}) custom-call(bf16[1024,768]{1,0:T(8,128)(2,1)} %get-tuple-element.85.q_ref, bf16[1024,768]{1,0:T(8,128)(2,1)} %get-tuple-element.86.k_ref, ...), custom_call_target="tpu_custom_call" | custom-call | flops 1024 | bytes 1024 | tf_op jit(solution)/shard_map/attend_back/pallas_call | solution.py:159
  344.4 1.4 dynamic-slice_bitcast_fusion
  346.9 1.4 collective-permute-done.11
  349.0 10.9 %collective-permute-done.5 = bf16[192,1152]{1,0:T(8,128)(2,1)S(1)} collective-permute-done((bf16[192,1152]{1,0:T(8,128)(2,1)S(1)}, bf16[192,1152]{1,0:T(8,128)(2,1)S(1)}, u32[]{:S(2)}, u32[]{:S(2)}) %collective-permute-start.5) | collective-permute-done | bytes 442400 | tf_op jit(solution)/shard_map/ppermute | solution.py:911
  360.0 0.9 pad_maximum_fusion
  360.9 5.6 %all-to-all-start.6 = ((bf16[8,24,1920]{2,1,0:T(8,128)(2,1)}), bf16[8,24,1920]{2,1,0:T(8,128)(2,1)S(1)}, u32[]{:S(2)}, u32[]{:S(2)}) async-start(bf16[8,24,1920]{2,1,0:T(8,128)(2,1)} %bitcast.35), calls=%async_computation.6 | async-start | bytes 1474560 | tf_op jit(solution)/shard_map/all_to_all | solution.py:902
  366.6 9.8 %close.1 = (bf16[1024,768]{1,0:T(8,128)(2,1)}, f32[8,768]{1,0:T(8,128)}) custom-call(bf16[1024,384]{1,0:T(8,128)(2,1)} %get-tuple-element.116.refs_0_, bf16[1024,384]{1,0:T(8,128)(2,1)} %get-tuple-element.117.refs_1_, bf16[1024,384]{1,0:T(8,128)(2,1)} %get-tuple-element.118.refs_2_, bf16[1024,384]{1,0:T(8,128)(2,1)} %get-tuple-element.119.refs_3_, ...), custom_call_target="tpu_custom_call" | custom-call | flops 40000000000 | bytes 4096 | tf_op jit(solution)/shard_map/close/pallas_call | solution.py:787
  376.5 0.9 fusion.3
  377.3 8.0 %all-to-all-done.6 = bf16[8,24,1920]{2,1,0:T(8,128)(2,1)S(1)} async-done(((bf16[8,24,1920]{2,1,0:T(8,128)(2,1)}), bf16[8,24,1920]{2,1,0:T(8,128)(2,1)S(1)}, u32[]{:S(2)}, u32[]{:S(2)}) %all-to-all-start.6) | async-done | bytes 737312 | tf_op jit(solution)/shard_map/all_to_all | solution.py:902
  385.4 3.6 all-to-all-start.7
  389.2 0.7 slice.62
  390.0 1.2 collective-permute-done.6
  392.0 3.5 collective-permute-done.7
  395.4 2.1 collective-permute-start.8
  397.5 2.1 collective-permute-done.8
  399.6 2.1 collective-permute-start.9
  401.7 2.1 collective-permute-done.9
  403.7 3.5 collective-permute-start.10
  407.2 2.1 collective-permute-done.10
  409.4 0.9 broadcast_in_dim.8
  410.3 6.0 %all-to-all-start.8 = ((bf16[8,24,1920]{2,1,0:T(8,128)(2,1)}), bf16[8,24,1920]{2,1,0:T(8,128)(2,1)S(1)}, u32[]{:S(2)}, u32[]{:S(2)}) async-start(bf16[8,24,1920]{2,1,0:T(8,128)(2,1)} %broadcast_in_dim.8), calls=%async_computation.8 | async-start | bytes 1474560 | tf_op jit(solution)/shard_map/all_to_all | solution.py:902
  416.3 7.7 %block_output.1 = bf16[1024,768]{1,0:T(8,128)(2,1)} custom-call(bf16[2048,768]{1,0:T(8,128)(2,1)} %bitcast.6.back_ref, s32[1024,2]{1,0:T(8,128)} %get-tuple-element.107.columns_ref, s32[1,1024]{1,0:T(1,128)} %bitcast.103, f32[8,1024]{1,0:T(8,128)} %get-tuple-element.89.logits_ref, f32[1024,768]{1,0:T(8,128)} %get-tuple-element.108.hidden_ref), custom_call_target="tpu_custom_call" | custom-call | flops 40000000000 | bytes 4096 | tf_op jit(solution)/shard_map/block_output/pallas_call | solution.py:815
  424.0 7.9 %all-to-all-done.8 = bf16[8,24,1920]{2,1,0:T(8,128)(2,1)S(1)} async-done(((bf16[8,24,1920]{2,1,0:T(8,128)(2,1)}), bf16[8,24,1920]{2,1,0:T(8,128)(2,1)S(1)}, u32[]{:S(2)}, u32[]{:S(2)}) %all-to-all-start.8) | async-done | bytes 737312 | tf_op jit(solution)/shard_map/all_to_all | solution.py:902
  432.5 4.0 unpack_expert.1
  436.5 0.8 broadcast_in_dim.9
  437.3 3.7 all-to-all-start.9
  441.0 3.3 collective-permute-done.15
  444.8 6.9 %all-to-all-done.9 = bf16[8,24,1152]{2,1,0:T(8,128)(2,1)S(1)} async-done(((bf16[8,24,1152]{2,1,0:T(8,128)(2,1)}), bf16[8,24,1152]{2,1,0:T(8,128)(2,1)S(1)}, u32[]{:S(2)}, u32[]{:S(2)}) %all-to-all-start.9) | async-done | bytes 442400 | tf_op jit(solution)/shard_map/all_to_all | solution.py:902
  451.7 1.4 collective-permute-start.13
  455.6 4.4 collective-permute-done.13
  460.4 5.8 %unpack.2 = (f32[768,768]{1,0:T(8,128)}, f32[768,768]{1,0:T(8,128)}, f32[768,768]{1,0:T(8,128)}, f32[768,768]{1,0:T(8,128)}) custom-call(s32[1,1]{1,0:T(1,128)} %bitcast.28.upper_ref, bf16[384,1920]{1,0:T(8,128)(2,1)} %copy-done.5, bf16[384,1920]{1,0:T(8,128)(2,1)} %collective-permute-done.16.other_ref), custom_call_target="tpu_custom_call" | custom-call | flops 40000000000 | bytes 4096 | tf_op jit(solution)/shard_map/unpack/pallas_call | solution.py:886
  466.2 1.4 fusion.11
  468.3 0.9 copy-done.24
  469.2 4.3 unpack.3
  (122 shorter events, 15.6 us)
Async XLA Ops:
  7.2 139.7 %all-gather.5.cloned.1.call-start = ((), (), s32[]{:S(2)}) async-start(), calls=%async_computation.11 | async-start | bytes 5898240 | tf_op jit(solution)/shard_map/all_gather | solution.py:1027
  15.8 8.3 %copy-start.12 = (f32[768]{0:T(1024)S(1)}, f32[768]{0:T(1024)}, u32[]{:S(2)}) copy-start(f32[768]{0:T(1024)} %param.26) | copy-start | bytes 9220
  15.8 8.8 %copy-start.13 = (f32[768]{0:T(1024)S(1)}, f32[768]{0:T(1024)}, u32[]{:S(2)}) copy-start(f32[768]{0:T(1024)} %param.27) | copy-start | bytes 9220
  15.8 9.4 %copy-start.14 = (f32[768]{0:T(1024)S(1)}, f32[768]{0:T(1024)}, u32[]{:S(2)}) copy-start(f32[768]{0:T(1024)} %param.29) | copy-start | bytes 9220
  15.8 10.0 %copy-start.15 = (f32[768]{0:T(1024)S(1)}, f32[768]{0:T(1024)}, u32[]{:S(2)}) copy-start(f32[768]{0:T(1024)} %param.32) | copy-start | bytes 9220
  15.8 10.6 %copy-start.16 = (f32[768]{0:T(1024)S(1)}, f32[768]{0:T(1024)}, u32[]{:S(2)}) copy-start(f32[768]{0:T(1024)} %param.35) | copy-start | bytes 9220
  15.8 11.2 %copy-start.17 = (f32[768]{0:T(1024)S(1)}, f32[768]{0:T(1024)}, u32[]{:S(2)}) copy-start(f32[768]{0:T(1024)} %param.34) | copy-start | bytes 9220
  15.8 11.7 %copy-start.18 = (f32[768]{0:T(1024)S(1)}, f32[768]{0:T(1024)}, u32[]{:S(2)}) copy-start(f32[768]{0:T(1024)} %param.36) | copy-start | bytes 9220
  15.8 12.3 %copy-start.21 = (s32[8]{0:T(128)S(1)}, s32[8]{0:T(128)}, u32[]{:S(2)}) copy-start(s32[8]{0:T(128)} %param.24) | copy-start | bytes 100
  15.8 12.5 %copy-start.22 = (s32[8]{0:T(128)S(1)}, s32[8]{0:T(128)}, u32[]{:S(2)}) copy-start(s32[8]{0:T(128)} %param.25) | copy-start | bytes 100
  15.8 80.2 %all-to-all-start = ((bf16[8,264,768]{2,1,0:T(8,128)(2,1)}), bf16[8,264,768]{2,1,0:T(8,128)(2,1)S(1)}, u32[]{:S(2)}, u32[]{:S(2)}) async-start(bf16[8,264,768]{2,1,0:T(8,128)(2,1)} %get-tuple-element.93), calls=%async_computation | async-start | bytes 6488064 | tf_op jit(solution)/shard_map/all_to_all | solution.py:902
  23.3 123.6 %all-gather.7.cloned.1.call-start = ((), (), s32[]{:S(2)}) async-start(), calls=%async_computation.12 | async-start | bytes 5898240 | tf_op jit(solution)/shard_map/all_gather | solution.py:1028
  96.1 40.9 %copy-start.2 = (bf16[8,264,768]{2,1,0:T(8,128)(2,1)}, bf16[8,264,768]{2,1,0:T(8,128)(2,1)S(1)}, u32[]{:S(2)}) copy-start(bf16[8,264,768]{2,1,0:T(8,128)(2,1)S(1)} %all-to-all-done.refs_1_.g_ref) | copy-start | bytes 9732100
  96.1 40.9 %all-to-all-start.1 = ((bf16[8,128,768]{2,1,0:T(8,128)(2,1)}), bf16[8,128,768]{2,1,0:T(8,128)(2,1)}, u32[]{:S(2)}, u32[]{:S(2)}) async-start(bf16[8,128,768]{2,1,0:T(8,128)(2,1)} %get-tuple-element.94), calls=%async_computation.1 | async-start | bytes 3145728 | tf_op jit(solution)/shard_map/all_to_all | solution.py:902
  100.4 41.0 %copy-start.20 = (bf16[1,768]{1,0:T(2,128)(2,1)S(1)}, bf16[1,768]{1,0:T(2,128)(2,1)}, u32[]{:S(2)}) copy-start(bf16[1,768]{1,0:T(2,128)(2,1)} %param.39) | copy-start | bytes 4612
  100.4 1.2 collective-permute-start
  101.6 3.5 collective-permute-start.1
  137.0 43.0 %all-to-all-start.2 = ((bf16[8,136,768]{2,1,0:T(8,128)(2,1)}), bf16[8,136,768]{2,1,0:T(8,128)(2,1)}, u32[]{:S(2)}, u32[]{:S(2)}) async-start(bf16[8,136,768]{2,1,0:T(8,128)(2,1)} %get-tuple-element.95), calls=%async_computation.2 | async-start | bytes 3342336 | tf_op jit(solution)/shard_map/all_to_all | solution.py:902
  180.1 43.4 %all-to-all-start.3 = ((bf16[8,128,768]{2,1,0:T(8,128)(2,1)}), bf16[8,128,768]{2,1,0:T(8,128)(2,1)S(1)}, u32[]{:S(2)}, u32[]{:S(2)}) async-start(bf16[8,128,768]{2,1,0:T(8,128)(2,1)} %get-tuple-element.104), calls=%async_computation.3 | async-start | bytes 3145728 | tf_op jit(solution)/shard_map/all_to_all | solution.py:902
  223.5 38.6 %copy-start.1 = (bf16[8,128,768]{2,1,0:T(8,128)(2,1)}, bf16[8,128,768]{2,1,0:T(8,128)(2,1)S(1)}, u32[]{:S(2)}) copy-start(bf16[8,128,768]{2,1,0:T(8,128)(2,1)S(1)} %all-to-all-done.3) | copy-start | bytes 4718596
  223.5 42.9 %all-to-all-start.4 = ((bf16[8,136,768]{2,1,0:T(8,128)(2,1)}), bf16[8,136,768]{2,1,0:T(8,128)(2,1)S(1)}, u32[]{:S(2)}, u32[]{:S(2)}) async-start(bf16[8,136,768]{2,1,0:T(8,128)(2,1)} %get-tuple-element.105), calls=%async_computation.4 | async-start | bytes 3342336 | tf_op jit(solution)/shard_map/all_to_all | solution.py:902
  227.1 205.4 %reduce-scatter.2.cloned.1.call-start = ((), (), s32[]{:S(2)}) async-start(), calls=%async_computation.13 | async-start | bytes 11857920 | tf_op jit(solution)/shard_map/reduce_scatter | solution.py:1054
  266.4 5.4 %copy-start = (bf16[8,136,768]{2,1,0:T(8,128)(2,1)}, bf16[8,136,768]{2,1,0:T(8,128)(2,1)S(1)}, u32[]{:S(2)}) copy-start(bf16[8,136,768]{2,1,0:T(8,128)(2,1)S(1)} %all-to-all-done.4) | copy-start | bytes 5013508
  266.4 94.5 %all-to-all-start.5 = ((bf16[8,256,768]{2,1,0:T(8,128)(2,1)}), bf16[8,256,768]{2,1,0:T(8,128)(2,1)}, u32[]{:S(2)}, u32[]{:S(2)}) async-start(bf16[8,256,768]{2,1,0:T(8,128)(2,1)} %get-tuple-element.106), calls=%async_computation.5 | async-start | bytes 6291456 | tf_op jit(solution)/shard_map/all_to_all | solution.py:902
  294.0 25.2 %collective-permute-start.2 = (bf16[384,768]{1,0:T(8,128)(2,1)S(1)}, bf16[384,768]{1,0:T(8,128)(2,1)S(1)}, u32[]{:S(2)}, u32[]{:S(2)}) collective-permute-start(bf16[384,768]{1,0:T(8,128)(2,1)S(1)} %dynamic-slice_bitcast_fusion.2), channel_id=1, source_target_pairs={{0,1},{1,0},{2,3},{3,2},{4,5},{5,4},{6,7},{7,6},{8,9},{9,8},{10,11... | collective-permute-start | bytes 1769480 | tf_op jit(solution)/shard_map/ppermute | solution.py:911
  317.3 1.9 copy-start.6
  318.6 27.4 %collective-permute-start.4 = (bf16[384,1152]{1,0:T(8,128)(2,1)S(1)}, bf16[384,1152]{1,0:T(8,128)(2,1)S(1)}, u32[]{:S(2)}, u32[]{:S(2)}) collective-permute-start(bf16[384,1152]{1,0:T(8,128)(2,1)S(1)} %dynamic-slice_bitcast_fusion.1), channel_id=1, source_target_pairs={{0,1},{1,0},{2,3},{3,2},{4,5},{5,4},{6,7},{7,6},{8,9},{9,8},{10,11... | collective-permute-start | bytes 2654216 | tf_op jit(solution)/shard_map/ppermute | solution.py:911
  319.3 26.6 %collective-permute-start.3 = (bf16[192,768]{1,0:T(8,128)(2,1)S(1)}, bf16[192,768]{1,0:T(8,128)(2,1)S(1)}, u32[]{:S(2)}, u32[]{:S(2)}) collective-permute-start(bf16[192,768]{1,0:T(8,128)(2,1)S(1)} %dynamic-slice_bitcast_fusion.5), channel_id=1, source_target_pairs={{0,2},{1,3},{2,0},{3,1},{4,6},{5,7},{6,4},{7,5},{8,10},{9,11},{10,... | collective-permute-start | bytes 884744 | tf_op jit(solution)/shard_map/ppermute | solution.py:911
  344.4 1.7 copy-start.3
  345.8 2.5 collective-permute-start.11
  346.0 2.3 copy-start.4
  346.5 13.4 %collective-permute-start.5 = (bf16[192,1152]{1,0:T(8,128)(2,1)S(1)}, bf16[192,1152]{1,0:T(8,128)(2,1)S(1)}, u32[]{:S(2)}, u32[]{:S(2)}) collective-permute-start(bf16[192,1152]{1,0:T(8,128)(2,1)S(1)} %dynamic-slice_bitcast_fusion.4), channel_id=1, source_target_pairs={{0,2},{1,3},{2,0},{3,1},{4,6},{5,7},{6,4},{7,5},{8,10},{9,11},{10,... | collective-permute-start | bytes 1327112 | tf_op jit(solution)/shard_map/ppermute | solution.py:911
  348.6 27.9 %collective-permute-start.12 = (bf16[192,1152]{1,0:T(8,128)(2,1)S(1)}, bf16[192,1152]{1,0:T(8,128)(2,1)S(1)}, u32[]{:S(2)}, u32[]{:S(2)}) collective-permute-start(bf16[192,1152]{1,0:T(8,128)(2,1)S(1)} %dynamic-slice_bitcast_fusion.3), channel_id=1, source_target_pairs={{0,2},{1,3},{2,0},{3,1},{4,6},{5,7},{6,4},{7,5},{8,10},{9,11},{10,... | collective-permute-start | bytes 1327112 | tf_op jit(solution)/shard_map/ppermute | solution.py:911
  360.9 24.4 %all-to-all-start.6 = ((bf16[8,24,1920]{2,1,0:T(8,128)(2,1)}), bf16[8,24,1920]{2,1,0:T(8,128)(2,1)S(1)}, u32[]{:S(2)}, u32[]{:S(2)}) async-start(bf16[8,24,1920]{2,1,0:T(8,128)(2,1)} %bitcast.35), calls=%async_computation.6 | async-start | bytes 1474560 | tf_op jit(solution)/shard_map/all_to_all | solution.py:902
  376.4 12.6 %copy-start.11 = (f32[8,768]{1,0:T(8,128)S(1)}, f32[8,768]{1,0:T(8,128)}, u32[]{:S(2)}) copy-start(f32[8,768]{1,0:T(8,128)} %get-tuple-element.129) | copy-start | bytes 73732
  376.4 12.6 %copy-start.19 = (f32[8,1]{1,0:T(8,128)S(1)}, f32[8,1]{1,0:T(8,128)}, u32[]{:S(2)}) copy-start(f32[8,1]{1,0:T(8,128)} %get-tuple-element.130) | copy-start | bytes 100
  376.4 12.7 %copy-start.9 = (f32[8,384]{1,0:T(8,128)S(1)}, f32[8,384]{1,0:T(8,128)}, u32[]{:S(2)}) copy-start(f32[8,384]{1,0:T(8,128)} %get-tuple-element.127) | copy-start | bytes 36868
  376.4 12.7 %copy-start.10 = (f32[8,384]{1,0:T(8,128)S(1)}, f32[8,384]{1,0:T(8,128)}, u32[]{:S(2)}) copy-start(f32[8,384]{1,0:T(8,128)} %get-tuple-element.128) | copy-start | bytes 36868
  376.4 13.5 %copy-start.8 = (f32[8,768]{1,0:T(8,128)S(1)}, f32[8,768]{1,0:T(8,128)}, u32[]{:S(2)}) copy-start(f32[8,768]{1,0:T(8,128)} %get-tuple-element.131) | copy-start | bytes 73732
  385.4 23.9 %all-to-all-start.7 = ((bf16[8,24,1152]{2,1,0:T(8,128)(2,1)}), bf16[8,24,1152]{2,1,0:T(8,128)(2,1)S(1)}, u32[]{:S(2)}, u32[]{:S(2)}) async-start(bf16[8,24,1152]{2,1,0:T(8,128)(2,1)} %bitcast.36), calls=%async_computation.7 | async-start | bytes 884736 | tf_op jit(solution)/shard_map/all_to_all | solution.py:902
  390.0 1.3 collective-permute-start.6
  391.3 4.2 collective-permute-start.7
  395.4 4.2 collective-permute-start.8
  399.6 4.2 collective-permute-start.9
  403.7 5.6 %collective-permute-start.10 = (f32[16,768]{1,0:T(8,128)S(1)}, f32[16,768]{1,0:T(8,128)S(1)}, u32[]{:S(2)}, u32[]{:S(2)}) collective-permute-start(f32[16,768]{1,0:T(8,128)S(1)} %add.109), channel_id=1, source_target_pairs={{0,16},{4,20},{8,24},{12,28},{16,0},{20,4},{24,8},{28,12},{1,17},{... | collective-permute-start | bytes 147464 | tf_op jit(solution)/shard_map/ppermute | solution.py:911
  410.3 21.6 %all-to-all-start.8 = ((bf16[8,24,1920]{2,1,0:T(8,128)(2,1)}), bf16[8,24,1920]{2,1,0:T(8,128)(2,1)S(1)}, u32[]{:S(2)}, u32[]{:S(2)}) async-start(bf16[8,24,1920]{2,1,0:T(8,128)(2,1)} %broadcast_in_dim.8), calls=%async_computation.8 | async-start | bytes 1474560 | tf_op jit(solution)/shard_map/all_to_all | solution.py:902
  431.9 12.5 %collective-permute-start.15 = (bf16[192,1920]{1,0:T(8,128)(2,1)S(1)}, bf16[192,1920]{1,0:T(8,128)(2,1)S(1)}, u32[]{:S(2)}, u32[]{:S(2)}) collective-permute-start(bf16[192,1920]{1,0:T(8,128)(2,1)S(1)} %bitcast.85), channel_id=1, source_target_pairs={{0,2},{1,3},{2,0},{3,1},{4,6},{5,7},{6,4},{7,5},{8,10},{9,11},{10,... | collective-permute-start | bytes 2211848 | tf_op jit(solution)/shard_map/ppermute | solution.py:911
  437.3 15.8 %copy-start.23 = (f32[8]{0:T(128)S(1)}, f32[8]{0:T(128)}, u32[]{:S(2)}) copy-start(f32[8]{0:T(128)} %get-tuple-element.159) | copy-start | bytes 100
  437.3 14.4 %all-to-all-start.9 = ((bf16[8,24,1152]{2,1,0:T(8,128)(2,1)}), bf16[8,24,1152]{2,1,0:T(8,128)(2,1)S(1)}, u32[]{:S(2)}, u32[]{:S(2)}) async-start(bf16[8,24,1152]{2,1,0:T(8,128)(2,1)} %broadcast_in_dim.9), calls=%async_computation.10 | async-start | bytes 884736 | tf_op jit(solution)/shard_map/all_to_all | solution.py:902
  444.8 15.6 %copy-start.5 = (bf16[384,1920]{1,0:T(8,128)(2,1)}, bf16[384,1920]{1,0:T(8,128)(2,1)S(1)}, u32[]{:S(2)}) copy-start(bf16[384,1920]{1,0:T(8,128)(2,1)S(1)} %maximum_select_fusion.own_ref) | copy-start | bytes 4423684
  444.8 15.6 %collective-permute-start.16 = (bf16[384,1920]{1,0:T(8,128)(2,1)S(1)}, bf16[384,1920]{1,0:T(8,128)(2,1)}, u32[]{:S(2)}, u32[]{:S(2)}) collective-permute-start(bf16[384,1920]{1,0:T(8,128)(2,1)S(1)} %maximum_select_fusion.own_ref), channel_id=1, source_target_pairs={{0,1},{1,0},{2,3},{3,2},{4,5},{5,4},{6,7},{7,6},{8,9},{9,8},{10,11... | collective-permute-start | bytes 4423688 | tf_op jit(solution)/shard_map/ppermute | solution.py:911
  451.7 8.3 %collective-permute-start.13 = (bf16[192,1152]{1,0:T(8,128)(2,1)S(1)}, bf16[192,1152]{1,0:T(8,128)(2,1)S(1)}, u32[]{:S(2)}, u32[]{:S(2)}) collective-permute-start(bf16[192,1152]{1,0:T(8,128)(2,1)S(1)} %bitcast.93), channel_id=1, source_target_pairs={{0,2},{1,3},{2,0},{3,1},{4,6},{5,7},{6,4},{7,5},{8,10},{9,11},{10,... | collective-permute-start | bytes 1327112 | tf_op jit(solution)/shard_map/ppermute | solution.py:911
  460.3 6.0 %copy-start.7 = (bf16[384,1152]{1,0:T(8,128)(2,1)}, bf16[384,1152]{1,0:T(8,128)(2,1)S(1)}, u32[]{:S(2)}) copy-start(bf16[384,1152]{1,0:T(8,128)(2,1)S(1)} %maximum_select_fusion.1.own_ref) | copy-start | bytes 2654212
  460.3 8.0 %collective-permute-start.14 = (bf16[384,1152]{1,0:T(8,128)(2,1)S(1)}, bf16[384,1152]{1,0:T(8,128)(2,1)S(1)}, u32[]{:S(2)}, u32[]{:S(2)}) collective-permute-start(bf16[384,1152]{1,0:T(8,128)(2,1)S(1)} %maximum_select_fusion.1.own_ref), channel_id=1, source_target_pairs={{0,1},{1,0},{2,3},{3,2},{4,5},{5,4},{6,7},{7,6},{8,9},{9,8},{10,11... | collective-permute-start | bytes 2654216 | tf_op jit(solution)/shard_map/ppermute | solution.py:911
  468.3 0.9 copy-start.24
Sparse Core Ops, SparseCore 0:
  9.6 40.1 all-gather.4
  51.3 37.4 all-gather.6
  266.6 85.9 reduce-scatter.1

commit v3 on v2

--- a/solution.py
+++ b/solution.py
@@ -59,12 +59,12 @@
 def attend_kernel(block, q_ref, k_ref, v_ref, context_ref, weights_ref):
     rows = q_ref.shape[0]
     keys = k_ref[...]
-    values_t = jnp.transpose(v_ref[...])
+    values = v_ref[...]
     place = 0
     for first in range(0, rows, block):
         span = first + block
         query = q_ref[first:span, :]
-        parts = []
+        weights_both, values_both = [], []
         for head in range(2):
             scores = causal(mm_nt(keys[:span], head_mask(query, head)), block)
             peak = jnp.max(scores, axis=0, keepdims=True)
@@ -72,8 +72,10 @@
             total = jnp.sum(powers, axis=0, keepdims=True)
             weights = (powers * (1.0 / total)).astype(BF16)
             weights_ref[0, head, place : place + span, :] = weights
-            parts.append(mm(values_t[head * HEAD_DIM : (head + 1) * HEAD_DIM, :span], weights))
-        context_ref[first:span, :] = jnp.transpose(jnp.concatenate(parts, axis=0)).astype(BF16)
+            weights_both.append(weights)
+            values_both.append(head_mask(values[:span], head))
+        out = mm_tn(jnp.concatenate(weights_both, axis=0), jnp.concatenate(values_both, axis=0))
+        context_ref[first:span, :] = out.astype(BF16)
         place += span
 
 
@@ -102,14 +104,13 @@
     rows = q_ref.shape[0]
     keys = k_ref[...]
     values = v_ref[...]
-    keys_t = jnp.transpose(keys)
     place = weights_ref.shape[2]
     for first in reversed(range(0, rows, block)):
         span = first + block
         place -= span
         query = q_ref[first:span, :]
         grad = g_ref[first:span, :]
-        grad_query, probs_both, scores_both, query_both, grad_both = [], [], [], [], []
+        probs_both, scores_both, query_both, grad_both = [], [], [], []
         for head in range(2):
             query_h = head_mask(query, head)
             grad_h = head_mask(grad, head)
@@ -118,7 +119,6 @@
             grad_probs = mm_nt(values[:span], grad_h)
             inner = jnp.sum(probs * grad_probs, axis=0, keepdims=True)
             grad_scores = (probs * (grad_probs - inner)).astype(BF16)
-            grad_query.append(mm(keys_t[head * HEAD_DIM : (head + 1) * HEAD_DIM, :span], grad_scores))
             probs_both.append(weights)
             scores_both.append(grad_scores)
             query_both.append(query_h)
@@ -131,7 +131,8 @@
         else:
             dv_acc[:span, :] += dv
             dk_acc[:span, :] += dk
-        dq = jnp.transpose(jnp.concatenate(grad_query, axis=0)) * 0.125
+        keys_both = jnp.concatenate([head_mask(keys[:span], head) for head in range(2)], axis=0)
+        dq = mm_tn(jnp.concatenate(scores_both, axis=0), keys_both) * 0.125
         dq_acc[first:span, :] = dq.astype(BF16)
     dq = dq_acc[...]
     dk = dk_acc[...].astype(BF16)
@@ -550,7 +551,7 @@
 
 
 def weight_kernel(parts, x0_ref, x1_ref, g_ref, act_ref, up_ref, scale_ref,
-                  grad_ref, down_acc, in_acc, bias_acc, bias_down_acc, flipped):
+                  down_ref, in_ref, down_acc, in_acc, bias_acc, bias_down_acc, flipped):
     part = pl.program_id(0)
     chunk = pl.program_id(1)
     sources, half, width = x0_ref.shape
@@ -585,8 +586,8 @@
 
     @pl.when(chunk == 1)
     def _():
-        grad_ref[0, width : width + hidden, :] = (down_acc[...] + down).astype(BF16)
-        grad_ref[0, :width, 0:hidden] = (in_acc[...] + into).astype(BF16)
+        down_ref[0, :hidden, :] = (down_acc[...] + down).astype(BF16)
+        in_ref[0] = (in_acc[...] + into).astype(BF16)
 
     @pl.when(part == 0)
     def _():
@@ -595,10 +596,9 @@
 
     @pl.when(chunk == 1)
     def _():
-        first = width + hidden
-        grad_ref[0, first:, :] = jnp.zeros((EXTRA, width), BF16)
-        grad_ref[0, first : first + 1, 0:hidden] = (bias_acc[...] + bias_in).astype(BF16)
-        grad_ref[0, first + 1 : first + 2, :] = bias_down_acc[...].astype(BF16)
+        down_ref[0, hidden:, :] = jnp.zeros((EXTRA, width), BF16)
+        down_ref[0, hidden : hidden + 1, 0:hidden] = (bias_acc[...] + bias_in).astype(BF16)
+        down_ref[0, hidden + 1 : hidden + 2, :] = bias_down_acc[...].astype(BF16)
 
 
 def weight_grads(x0, x1, g, act, up, scale):
@@ -616,8 +616,14 @@
             wide_spec,
             pl.BlockSpec((1, 1, rows), lambda p, t: (t, 0, 0)),
         ],
-        out_specs=pl.BlockSpec((1, width + hidden + EXTRA, width), lambda p, t: (p, 0, 0)),
-        out_shape=jax.ShapeDtypeStruct((parts, width + hidden + EXTRA, width), BF16),
+        out_specs=[
+            pl.BlockSpec((1, hidden + EXTRA, width), lambda p, t: (p, 0, 0)),
+            pl.BlockSpec((1, width, hidden), lambda p, t: (p, 0, 0)),
+        ],
+        out_shape=[
+            jax.ShapeDtypeStruct((parts, hidden + EXTRA, width), BF16),
+            jax.ShapeDtypeStruct((parts, width, hidden), BF16),
+        ],
         scratch_shapes=[
             pltpu.VMEM((hidden, width), F32),
             pltpu.VMEM((width, hidden), F32),
@@ -633,7 +639,7 @@
 
 def combine_kernel(weight_ref, back0_ref, back1_ref, dots0_ref, dots1_ref, columns_ref, ids_ref, logits_ref, pull_ref,
                    hidden_ref, grad_ref, context_ref, moe_ref, w_out_ref, router_ref, gain_ref,
-                   hid_grad_ref, con_grad_ref, out_grad_ref, sums_ref, router_grad_ref, probs_ref, out_acc):
+                   hid_grad_ref, con_grad_ref, out_grad_ref, sums_ref, router_grad_ref, probs_ref, branches):
     step = pl.program_id(0)
     experts = logits_ref.shape[0]
     count0 = back0_ref.shape[0]
@@ -661,7 +667,7 @@
     branch = hid_grad.astype(BF16)
     hid_grad_ref[...] = hid_grad
     con_grad_ref[...] = mm_nt(branch, w_out_ref[...]).astype(BF16)
-    out_grad = mm_tn(context_ref[...], branch)
+    branches[pl.ds(pl.multiple_of(step * branch.shape[0], branch.shape[0]), branch.shape[0]), :] = branch
     router_grad = mm(logit_grad, moe_ref[...])
     prob_sum = jnp.sum(probs, axis=1, keepdims=True)
     sums = jnp.concatenate(
@@ -676,21 +682,19 @@
 
     @pl.when(step == 0)
     def _():
-        out_acc[...] = out_grad
         router_grad_ref[...] = router_grad
         probs_ref[...] = prob_sum
         sums_ref[...] = sums
 
     @pl.when(step > 0)
     def _():
-        out_acc[...] += out_grad
         router_grad_ref[...] += router_grad
         probs_ref[...] += prob_sum
         sums_ref[...] += sums
 
     @pl.when(step == pl.num_programs(0) - 1)
     def _():
-        out_grad_ref[...] = out_acc[...].astype(BF16)
+        out_grad_ref[...] = mm_tn(context_ref[...], branches[...]).astype(BF16)
 
 
 def combine(weight, back0, back1, dots0, dots1, columns, ids, logits, pull, hidden, grad_out, context, moe_in,
@@ -717,7 +721,7 @@
             pl.BlockSpec((experts, 1), whole),
             row_spec,
             row_spec,
-            row_spec,
+            pl.BlockSpec((rows, width), whole),
             row_spec,
             square,
             pl.BlockSpec((experts, width), whole),
@@ -739,7 +743,7 @@
             jax.ShapeDtypeStruct((experts, width), F32),
             jax.ShapeDtypeStruct((experts, 1), F32),
         ],
-        scratch_shapes=[pltpu.VMEM((width, width), F32)],
+        scratch_shapes=[pltpu.VMEM((rows, width), BF16)],
         compiler_params=params("arbitrary"),
         cost_estimate=cost(rows, rows),
         name="combine",
@@ -830,26 +834,37 @@
     )(back, columns, ids, logits, hidden)
 
 
-def unpack_expert_kernel(hidden, packed_ref, in_ref, down_ref, bias_ref):
-    width = in_ref.shape[0]
-    in_ref[...] = packed_ref[:width, :hidden].astype(F32)
-    down_ref[...] = packed_ref[width : width + hidden, :].astype(F32)
-    bias_ref[...] = packed_ref[width + hidden :, :].astype(F32)
-
-
-def unpack_expert(packed, hidden):
-    rows, width = packed.shape
+def unpack_expert_kernel(place_ref, down_rows, in_rows, in_ref, down_ref, bias_in_ref, bias_down_ref):
+    width, hidden = in_ref.shape
+    share = bias_down_ref.shape[1]
+    in_ref[...] = in_rows[...].astype(F32)
+    down_ref[...] = down_rows[:hidden, :].astype(F32)
+    extra = down_rows[hidden:, :].astype(F32)
+    bias_in_ref[...] = extra[0:1, :hidden]
+    for place in range(width // share):
+
+        @pl.when(place_ref[0, 0] == place)
+        def _():
+            bias_down_ref[...] = extra[1:2, place * share : (place + 1) * share]
+
+
+def unpack_expert(place, down_rows, in_rows, share):
+    width, hidden = in_rows.shape
+    memory = pl.BlockSpec(memory_space=pltpu.VMEM)
     return pl.pallas_call(
-        functools.partial(unpack_expert_kernel, hidden),
+        unpack_expert_kernel,
+        in_specs=[pl.BlockSpec(memory_space=pltpu.SMEM), memory, memory],
+        out_specs=[memory] * 4,
         out_shape=[
             jax.ShapeDtypeStruct((width, hidden), F32),
             jax.ShapeDtypeStruct((hidden, width), F32),
-            jax.ShapeDtypeStruct((EXTRA, width), F32),
+            jax.ShapeDtypeStruct((1, hidden), F32),
+            jax.ShapeDtypeStruct((1, share), F32),
         ],
         compiler_params=params(),
-        cost_estimate=cost(COVER, 4096),
+        cost_estimate=cost(COVER, width * hidden),
         name="unpack_expert",
-    )(packed)
+    )(place, down_rows, in_rows)
 
 
 def unpack_kernel(lead, upper_ref, own_ref, other_ref, *refs):
@@ -918,12 +933,6 @@
         bit *= 2
 
 
-def narrow_sum(value):
-    for bit in bits("narrow"):
-        value = value + trade(value, "narrow", bit)
-    return value
-
-
 def is_upper(axis, bit):
     return (lax.axis_index(axis) // bit) % 2
 
@@ -949,10 +958,18 @@
     return swap(copies, axis)
 
 
-def narrow_part(value):
-    for bit in bits("narrow"):
+def core_part(value):
+    return halve(value, "narrow", 1)
+
+
+def outer_part(value):
+    for bit in list(bits("narrow"))[1:]:
         value = halve(value, "narrow", bit)
     return value
+
+
+def narrow_part(value):
+    return outer_part(core_part(value))
 
 
 def wide_part(value):
@@ -966,16 +983,15 @@
     return spread_out(value, "wide").reshape(-1, value.shape[1])
 
 
-def narrow_half(value):
-    for bit in reversed(list(bits("narrow"))[1:]):
+def outer_whole(value):
+    for bit in list(bits("narrow"))[1:]:
         value = rejoin(value, "narrow", bit)
-    return value, trade(value, "narrow", 1)
-
-
-def small_sum(value):
-    for axis in ("narrow", "wide"):
-        for bit in bits(axis):
-            value = value + trade(value, axis, bit)
+    return value
+
+
+def axis_sum(value, axis):
+    for bit in bits(axis):
+        value = value + trade(value, axis, bit)
     return value
 
 
@@ -1038,7 +1054,7 @@
     gathered_bias = lax.all_gather(after(bias_in, first), "narrow", axis=0)
     x0 = swap(after(first, grad_rows), "wide")
     counted = jnp.sum(grad_rows[:, capacity, :experts].astype(F32), axis=0)
-    fraction = narrow_sum(counted) / total_tokens
+    fraction = axis_sum(counted, "narrow") / total_tokens
     x1 = swap(after(second, x0, fraction), "wide")
     act, up, out, back0, dots = expert(
         x0, grad_rows, gathered_in, gathered_bias, gathered_down, bias_down, 0
@@ -1050,15 +1066,9 @@
     back1 = arrived = swap(after(back1, back0), "wide")
     scale = jnp.sum(x1[:, half : half + 3, :capacity].astype(F32), axis=1)
     scale = jnp.transpose(scale.reshape(wide_count, 2, half), (1, 0, 2)).reshape(2, 1, wide_count * half)
-    expert_sums = weight_grads(after(x0, back0), x1, grad_rows, act, up, scale)
-    expert_grad = lax.psum_scatter(after(expert_sums, arrived), "narrow", scatter_dimension=0)
-    grad_w_in, grad_w_down, bias_rows = unpack_expert(expert_grad, hidden_cols)
-    share = width // narrow_count
-    grad_bias_in = bias_rows[0:1, :hidden_cols]
-    grad_bias_down = lax.dynamic_slice_in_dim(
-        bias_rows[1:2], lax.axis_index("narrow") * share, share, 1
-    )
-    back1 = after(back1, expert_sums)
+    down_sums, in_sums = weight_grads(after(x0, back0), x1, grad_rows, act, up, scale)
+    in_grad = lax.psum_scatter(after(in_sums, arrived), "narrow", scatter_dimension=0)
+    back1 = after(back1, in_sums)
     returned = swap(after(expert_out, arrived), "wide")
 
     extras = jnp.transpose(back1[:, half:, :half], (1, 0, 2))
@@ -1086,36 +1096,49 @@
     pairs = width // PAIR
     span = pairs // ATTEND_CALLS
     grads, bias_sums = [], []
-    packed = [narrow_part(out_grad)]
+    out_core = core_part(out_grad)
+    packed = [outer_part(out_core)]
     for call in range(ATTEND_CALLS):
         dq, dk, dv, weights, column_sums = attend_back(
-            queries, keys, values, soft_weights, con_grad, normed_t, call * span, span
+            queries,
+            keys,
+            values,
+            soft_weights,
+            after(con_grad, out_core) if call else con_grad,
+            normed_t,
+            call * span,
+            span,
         )
         grads.append((dq, dk, dv))
         packed.append(narrow_part(weights))
         bias_sums.append(column_sums)
     early = jnp.concatenate(packed[:-1], axis=1)
     hid_grad = after(hid_grad, early)
+    down_grad = lax.psum_scatter(after(down_sums, early, in_grad), "narrow", scatter_dimension=0)
+    place = lax.axis_index("narrow").reshape(1, 1)
+    grad_w_in, grad_w_down, grad_bias_in, grad_bias_down = unpack_expert(
+        place, down_grad, in_grad, width // narrow_count
+    )
     grad_tokens, norm_sums = close(grads, tokens, hid_grad, row(norm1_gain), w_query, w_key, w_value)
     block_out = block_output(
         returned.reshape(experts * capacity, width), columns, ids, logits, hidden
     )
     bias_sums = jnp.concatenate(bias_sums, axis=1)
     prob_row = jnp.pad(prob_sums.reshape(1, experts), ((0, 0), (0, width - experts)))
-    small = small_sum(
-        jnp.concatenate([norm_sums[:2], bias_sums[:2], sums[:3], prob_row, router_grad], axis=0)
-    )
+    small = jnp.concatenate([norm_sums[:2], bias_sums[:2], sums[:3], prob_row, router_grad], axis=0)
+    small = axis_sum(small, "narrow")
     early = wide_part(after(early, returned))
-    late = wide_part(after(packed[-1], early, norm_sums))
+    late = wide_part(after(packed[-1], early, small))
+    small = axis_sum(small, "wide")
     early = wide_whole(after(early, late, small))
-    late = wide_whole(after(late, early, bias_rows, block_out))
-    early, early_other = narrow_half(early)
-    late, late_other = narrow_half(late)
-    balance_loss = experts * jnp.sum(fraction * (small[7, :experts] / total_tokens))
+    late = wide_whole(after(late, early, grad_w_in, block_out))
     upper = is_upper("narrow", 1).astype(jnp.int32).reshape(1, 1)
     blocks = narrow_count // 2
-    grad_w_out, *weights = unpack(upper, early, early_other, blocks, width, 1)
-    weights = unpack(upper, late, late_other, blocks, width, 0, weights)
+    early = outer_whole(early)
+    grad_w_out, *weights = unpack(upper, early, trade(early, "narrow", 1), blocks, width, 1)
+    late = outer_whole(late)
+    weights = unpack(upper, late, trade(late, "narrow", 1), blocks, width, 0, weights)
+    balance_loss = experts * jnp.sum(fraction * (small[7, :experts] / total_tokens))
     return (
         block_out,
         balance_loss,

time: 491 us -> 470 us (0.957); the launches traced: 482 us -> 469 us
  Pallas kernels: 260 us -> 240 us
  waiting for transfers between devices: 111 us -> 116 us
    pallas_call x2, Pallas kernels: 46.5 us -> 35.7 us  [attend_back(): pl.pallas_call(functools.partial(attend_back_kernel, block), grid=(pairs,...]
    pallas_call x1, Pallas kernels: 30.6 us -> 20.5 us  [attend(): pl.pallas_call(functools.partial(attend_kernel, block), grid=(pairs,), in...]
  transfers between devices with their start and end apart: 30 -> 31, of which waited for: 19 -> 17; matrix products, arithmetic and copies ran while one was open for 5% -> 5% of each run, Pallas kernels for 53% -> 50%
where the time goes in v3:
time: 470 us; the launch traced here: 469 us
  Pallas kernels  240 us (51%)
  waiting for transfers between devices  116 us (25%)
  starting transfers between devices  66.3 us (14%)
  between operations  16.1 us (3%)
  local copies, waits for them, and re-layouts  14.9 us (3%)
  other arithmetic  9.68 us (2%)
  blocking collectives  5.49 us (1%)
    all_to_all x10, waiting for transfers between devices, swap(): return lax.all_to_all(blocks, axis, split_axis=0, concat_axis=0, tiled=True)  79.9 us
    pallas_call x2, Pallas kernels, expert(): pl.pallas_call(functools.partial(expert_kernel, parts, chunk), grid=(part...  66.1 us
    all_to_all x10, starting transfers between devices, swap(): return lax.all_to_all(blocks, axis, split_axis=0, concat_axis=0, tiled=True)  50.4 us
    pallas_call x2, Pallas kernels, attend_back(): pl.pallas_call(functools.partial(attend_back_kernel, block), grid=(pairs,...  35.7 us
    ppermute x17, waiting for transfers between devices, trade(): lax.ppermute(value, axis, [(place, place ^ bit) for place in range(count)])  34.9 us
    pallas_call x1, Pallas kernels, weight_grads(): pl.pallas_call(functools.partial(weight_kernel, parts), grid=(parts, 2),...  33.5 us
    pallas_call x1, Pallas kernels, attend(): pl.pallas_call(functools.partial(attend_kernel, block), grid=(pairs,), in...  20.5 us
    pallas_call x1, Pallas kernels, combine(): pl.pallas_call(combine_kernel, grid=(rows // tile,), in_specs=[pl.BlockSp...  19.1 us
  transfers between devices with their start and end apart: 31, of which 17 were waited for; matrix products, arithmetic and copies ran while one was open for 5% of the time, Pallas kernels for 50%

profile of v3, /device:TPU:0, one launch (start us, length us, event | category | flops | bytes accessed | tf_op | source)
XLA Modules:
  0.0 468.5 jit_solution(8069582337238861403)
XLA Ops:
  7.9 7.8 %route.1 = (s32[1,1024]{1,0:T(1,128)}, s32[1024,2]{1,0:T(8,128)}, bf16[8,264,768]{2,1,0:T(8,128)(2,1)}) custom-call(s32[1,1024]{1,0:T(1,128)} %bitcast.102, bf16[1024,768]{1,0:T(8,128)(2,1)} %grad_ref.3), custom_call_target="tpu_custom_call" | custom-call | flops 3221225472 | bytes 4718592 | tf_op jit(solution)/shard_map/route/pallas_call | solution.py:286
  15.8 7.4 %all-to-all-start = ((bf16[8,264,768]{2,1,0:T(8,128)(2,1)}), bf16[8,264,768]{2,1,0:T(8,128)(2,1)S(1)}, u32[]{:S(2)}, u32[]{:S(2)}) async-start(bf16[8,264,768]{2,1,0:T(8,128)(2,1)} %get-tuple-element.98), calls=%async_computation | async-start | bytes 6488064 | tf_op jit(solution)/shard_map/all_to_all | solution.py:917
  23.3 0.7 all-gather.7.cloned.1.call-update
  28.9 8.3 %project.1 = (bf16[768,1024]{1,0:T(8,128)(2,1)}, bf16[1024,768]{1,0:T(8,128)(2,1)}, bf16[1024,768]{1,0:T(8,128)(2,1)}, bf16[1024,768]{1,0:T(8,128)(2,1)}) custom-call(bf16[1024,768]{1,0:T(8,128)(2,1)} %refs_6_.1, f32[1,768]{1,0:T(1,128)} %reshape.178.gain_ref.refs_8_, f32[1,768]{1,0:T(1,128)} %reshape.179.shift_ref, bf16[768,768]{1,0:T(8,128)(2,1)} %refs_9_.1, ...), custom_call_target="tpu_custom_call" | custom-call | flops 3623878656 | bytes 11403264 | tf_op jit(solution)/shard_map/project/pallas_call | solution.py:325
  37.2 20.5 %attend.1 = (bf16[1024,768]{1,0:T(8,128)(2,1)}, bf16[6,2,2560,256]{3,2,1,0:T(8,128)(2,1)}) custom-call(bf16[1024,768]{1,0:T(8,128)(2,1)} %get-tuple-element.90.q_ref, bf16[1024,768]{1,0:T(8,128)(2,1)} %get-tuple-element.91.k_ref, bf16[1024,768]{1,0:T(8,128)(2,1)} %get-tuple-element.92.v_ref), custom_call_target="tpu_custom_call" | custom-call | flops 6442450944 | bytes 6291456 | tf_op jit(solution)/shard_map/attend/pallas_call | solution.py:87
  57.7 7.2 %settle.1 = (f32[1024,768]{1,0:T(8,128)}, bf16[1024,768]{1,0:T(8,128)(2,1)}, f32[8,1024]{1,0:T(8,128)}) custom-call(bf16[1024,768]{1,0:T(8,128)(2,1)} %get-tuple-element.93.context_ref, bf16[1024,768]{1,0:T(8,128)(2,1)} %refs_6_.1, bf16[768,768]{1,0:T(8,128)(2,1)} %w_out_ref.3, f32[1,768]{1,0:T(1,128)} %reshape.182.bias_ref, f32[1,768]{1,0:T(1,128)} %reshape.183.gain_ref, ...), custom_call_target="tpu_custom_call" | custom-call | flops 1207959552 | bytes 9043968 | tf_op jit(solution)/shard_map/settle/pallas_call | solution.py:353
  64.9 8.6 %dispatch.1 = (bf16[8,128,768]{2,1,0:T(8,128)(2,1)}, bf16[8,136,768]{2,1,0:T(8,128)(2,1)}) custom-call(f32[1,1]{1,0:T(1,128)} %bitcast.2.weight_ref, s32[1,1024]{1,0:T(1,128)} %get-tuple-element.89.slots_ref, s32[1,1024]{1,0:T(1,128)} %bitcast.103, f32[8,1024]{1,0:T(8,128)} %get-tuple-element.94.logits_ref, bf16[1024,768]{1,0:T(8,128)(2,1)} %get-tuple-element.95.moe_ref), custom_call_target="tpu_custom_call" | custom-call | flops 3221225472 | bytes 4718592 | tf_op jit(solution)/shard_map/dispatch/pallas_call | solution.py:400
  73.4 22.6 %all-to-all-done.refs_1_.g_ref = bf16[8,264,768]{2,1,0:T(8,128)(2,1)S(1)} async-done(((bf16[8,264,768]{2,1,0:T(8,128)(2,1)}), bf16[8,264,768]{2,1,0:T(8,128)(2,1)S(1)}, u32[]{:S(2)}, u32[]{:S(2)}) %all-to-all-start) | async-done | bytes 3244064 | tf_op jit(solution)/shard_map/all_to_all | solution.py:917
  96.1 4.3 all-to-all-start.1
  100.5 1.1 collective-permute-done
  101.6 1.5 collective-permute-start.1
  103.1 2.0 collective-permute-done.1
  105.7 31.3 %all-to-all-done.1.refs_0_.x0_ref = bf16[8,128,768]{2,1,0:T(8,128)(2,1)} async-done(((bf16[8,128,768]{2,1,0:T(8,128)(2,1)}), bf16[8,128,768]{2,1,0:T(8,128)(2,1)}, u32[]{:S(2)}, u32[]{:S(2)}) %all-to-all-start.1) | async-done | bytes 1572896 | tf_op jit(solution)/shard_map/all_to_all | solution.py:917
  137.0 4.3 all-to-all-start.2
  141.4 5.5 %all-gather.1.refs_3_ = bf16[4,1,768]{2,1,0:T(2,128)(2,1)} all-gather(bf16[1,1,768]{2,1,0:T(2,128)(2,1)S(1)} %bitcast.106), channel_id=2, replica_groups=mesh['wide'=8,'narrow'=4] {'narrow'}, dimensions={0}, use_global_device_ids=true | all-gather | bytes 7680 | tf_op jit(solution)/shard_map/all_gather | solution.py:1054
  146.9 33.0 %expert.2 = (bf16[4,2,1024,768]{3,2,1,0:T(8,128)(2,1)}, bf16[4,2,1024,768]{3,2,1,0:T(8,128)(2,1)}, bf16[8,256,768]{2,1,0:T(8,128)(2,1)}, bf16[8,128,768]{2,1,0:T(8,128)(2,1)}, bf16[8,8,128]{2,1,0:T(8,128)(2,1)}) custom-call(bf16[8,128,768]{2,1,0:T(8,128)(2,1)} %all-to-all-done.1.refs_0_.x0_ref, bf16[8,264,768]{2,1,0:T(8,128)(2,1)} %copy-done.2, ...), custom_call_target="tpu_custom_call" | custom-call | flops 14495514624 | bytes 12582912 | tf_op jit(solution)/shard_map/expert/pallas_call | solution.py:513
  180.1 5.7 %all-to-all-start.3 = ((bf16[8,128,768]{2,1,0:T(8,128)(2,1)}), bf16[8,128,768]{2,1,0:T(8,128)(2,1)S(1)}, u32[]{:S(2)}, u32[]{:S(2)}) async-start(bf16[8,128,768]{2,1,0:T(8,128)(2,1)} %get-tuple-element.109), calls=%async_computation.3 | async-start | bytes 3145728 | tf_op jit(solution)/shard_map/all_to_all | solution.py:917
  185.8 33.2 %expert.3 = (bf16[4,2,1024,768]{3,2,1,0:T(8,128)(2,1)}, bf16[4,2,1024,768]{3,2,1,0:T(8,128)(2,1)}, bf16[8,256,768]{2,1,0:T(8,128)(2,1)}, bf16[8,136,768]{2,1,0:T(8,128)(2,1)}) custom-call(bf16[8,136,768]{2,1,0:T(8,128)(2,1)} %all-to-all-done.2.refs_0_.x1_ref, ...), custom_call_target="tpu_custom_call", output_to_operand_aliasing={{0}: (6, {}), {1}: (7, {}), {2}: (8, {})} | custom-call | flops 14495514624 | bytes 12582912 | tf_op jit(solution)/shard_map/expert/pallas_call | solution.py:513
  218.9 4.4 all-to-all-done.3
  223.3 3.6 all-to-all-start.4
  227.2 1.4 convert_reduce_fusion
  228.6 33.5 %weight_grads.1 = (bf16[4,776,768]{2,1,0:T(8,128)(2,1)}, bf16[4,768,768]{2,1,0:T(8,128)(2,1)}) custom-call(bf16[8,128,768]{2,1,0:T(8,128)(2,1)} %all-to-all-done.1.refs_0_.x0_ref, bf16[8,136,768]{2,1,0:T(8,128)(2,1)} %all-to-all-done.2.refs_0_.x1_ref, bf16[8,264,768]{2,1,0:T(8,128)(2,1)} %copy-done.2, bf16[4,2,1024,768]{3,2,1,0:T(8,128)(2,1)} %get-tuple-element.116.act_ref, ...), custom_call_target="tpu_custom_call" | custom-call | flops 28991029248 | bytes 25165824 | tf_op jit(solution)/shard_map/weight_grads/pallas_call | solution.py:608
  262.1 4.2 all-to-all-done.4
  266.3 4.5 all-to-all-start.5
  271.6 0.7 reshape.191.dots1_ref
  272.9 19.1 %combine.1 = (f32[1024,768]{1,0:T(8,128)}, bf16[1024,768]{1,0:T(8,128)(2,1)}, bf16[768,768]{1,0:T(8,128)(2,1)}, f32[8,768]{1,0:T(8,128)}, f32[8,768]{1,0:T(8,128)}, /*index=5*/f32[8,1]{1,0:T(8,128)}) custom-call(f32[1,1]{1,0:T(1,128)} %bitcast.2.weight_ref, bf16[1024,768]{1,0:T(8,128)(2,1)} %bitcast.82, bf16[1088,768]{1,0:T(8,128)(2,1)} %bitcast.81, ...), custom_call_target="tpu_custom_call" | custom-call | flops 1024 | bytes 1024 | tf_op jit(solution)/shard_map/combine/pallas_call | solution.py:709
  292.0 1.1 dynamic-slice_bitcast_fusion.2
  293.2 17.9 %attend_back.2 = (bf16[1024,384]{1,0:T(8,128)(2,1)}, bf16[1024,384]{1,0:T(8,128)(2,1)}, bf16[1024,384]{1,0:T(8,128)(2,1)}, bf16[768,1152]{1,0:T(8,128)(2,1)}, f32[8,384]{1,0:T(8,128)}) custom-call(bf16[1024,768]{1,0:T(8,128)(2,1)} %get-tuple-element.90.q_ref, bf16[1024,768]{1,0:T(8,128)(2,1)} %get-tuple-element.91.k_ref, ...), custom_call_target="tpu_custom_call" | custom-call | flops 1024 | bytes 1024 | tf_op jit(solution)/shard_map/attend_back/pallas_call | solution.py:160
  311.1 1.3 dynamic-slice_bitcast_fusion.1
  313.0 0.7 slice.58
  315.0 1.2 fusion.2
  316.3 1.7 collective-permute-start.3
  318.0 17.7 %attend_back.3 = (bf16[1024,384]{1,0:T(8,128)(2,1)}, bf16[1024,384]{1,0:T(8,128)(2,1)}, bf16[1024,384]{1,0:T(8,128)(2,1)}, bf16[768,1152]{1,0:T(8,128)(2,1)}, f32[8,384]{1,0:T(8,128)}) custom-call(bf16[1024,768]{1,0:T(8,128)(2,1)} %get-tuple-element.90.q_ref, bf16[1024,768]{1,0:T(8,128)(2,1)} %get-tuple-element.91.k_ref, ...), custom_call_target="tpu_custom_call" | custom-call | flops 1024 | bytes 1024 | tf_op jit(solution)/shard_map/attend_back/pallas_call | solution.py:160
  338.1 9.9 %collective-permute-done.5 = bf16[192,1152]{1,0:T(8,128)(2,1)S(1)} collective-permute-done((bf16[192,1152]{1,0:T(8,128)(2,1)S(1)}, bf16[192,1152]{1,0:T(8,128)(2,1)S(1)}, u32[]{:S(2)}, u32[]{:S(2)}) %collective-permute-start.5) | collective-permute-done | bytes 442400 | tf_op jit(solution)/shard_map/ppermute | solution.py:926
  348.1 0.9 pad_maximum_fusion
  349.3 0.8 collective-permute-start.12
  350.1 5.7 %all-to-all-start.6 = ((bf16[8,24,1920]{2,1,0:T(8,128)(2,1)}), bf16[8,24,1920]{2,1,0:T(8,128)(2,1)S(1)}, u32[]{:S(2)}, u32[]{:S(2)}) async-start(bf16[8,24,1920]{2,1,0:T(8,128)(2,1)} %bitcast.35), calls=%async_computation.6 | async-start | bytes 1474560 | tf_op jit(solution)/shard_map/all_to_all | solution.py:917
  355.8 11.1 %close.1 = (bf16[1024,768]{1,0:T(8,128)(2,1)}, f32[8,768]{1,0:T(8,128)}) custom-call(bf16[1024,384]{1,0:T(8,128)(2,1)} %get-tuple-element.122.refs_0_, bf16[1024,384]{1,0:T(8,128)(2,1)} %get-tuple-element.123.refs_1_, bf16[1024,384]{1,0:T(8,128)(2,1)} %get-tuple-element.124.refs_2_, bf16[1024,384]{1,0:T(8,128)(2,1)} %get-tuple-element.127.refs_3_, ...), custom_call_target="tpu_custom_call" | custom-call | flops 40000000000 | bytes 4096 | tf_op jit(solution)/shard_map/close/pallas_call | solution.py:791
  366.9 0.7 slice.56
  367.8 1.2 collective-permute-done.6
  369.0 1.2 collective-permute-start.7
  370.2 4.1 collective-permute-done.7
  374.3 0.9 fusion.3
  375.3 6.1 %all-to-all-start.7 = ((bf16[8,24,1152]{2,1,0:T(8,128)(2,1)}), bf16[8,24,1152]{2,1,0:T(8,128)(2,1)S(1)}, u32[]{:S(2)}, u32[]{:S(2)}) async-start(bf16[8,24,1152]{2,1,0:T(8,128)(2,1)} %bitcast.36), calls=%async_computation.7 | async-start | bytes 884736 | tf_op jit(solution)/shard_map/all_to_all | solution.py:917
  381.4 2.0 collective-permute-start.8
  383.4 4.1 collective-permute-done.8
  387.5 2.6 collective-permute-start.9
  390.1 2.1 collective-permute-done.9
  392.1 2.3 collective-permute-start.10
  394.4 2.8 collective-permute-done.10
  397.3 0.9 broadcast_in_dim.8
  398.2 5.1 %all-to-all-start.8 = ((bf16[8,24,1920]{2,1,0:T(8,128)(2,1)}), bf16[8,24,1920]{2,1,0:T(8,128)(2,1)S(1)}, u32[]{:S(2)}, u32[]{:S(2)}) async-start(bf16[8,24,1920]{2,1,0:T(8,128)(2,1)} %broadcast_in_dim.8), calls=%async_computation.8 | async-start | bytes 1474560 | tf_op jit(solution)/shard_map/all_to_all | solution.py:917
  403.3 7.7 %block_output.1 = bf16[1024,768]{1,0:T(8,128)(2,1)} custom-call(bf16[2048,768]{1,0:T(8,128)(2,1)} %bitcast.6.back_ref, s32[1024,2]{1,0:T(8,128)} %get-tuple-element.112.columns_ref, s32[1,1024]{1,0:T(1,128)} %bitcast.105, f32[8,1024]{1,0:T(8,128)} %get-tuple-element.94.logits_ref, f32[1024,768]{1,0:T(8,128)} %get-tuple-element.113.hidden_ref), custom_call_target="tpu_custom_call" | custom-call | flops 40000000000 | bytes 4096 | tf_op jit(solution)/shard_map/block_output/pallas_call | solution.py:819
  410.9 8.6 %all-to-all-done.8 = bf16[8,24,1920]{2,1,0:T(8,128)(2,1)S(1)} async-done(((bf16[8,24,1920]{2,1,0:T(8,128)(2,1)}), bf16[8,24,1920]{2,1,0:T(8,128)(2,1)S(1)}, u32[]{:S(2)}, u32[]{:S(2)}) %all-to-all-start.8) | async-done | bytes 737312 | tf_op jit(solution)/shard_map/all_to_all | solution.py:917
  419.5 1.5 collective-permute-start.15
  421.0 4.1 unpack_expert.1
  425.1 0.8 broadcast_in_dim.9
  425.9 3.7 all-to-all-start.9
  429.6 2.3 collective-permute-done.15
  432.5 8.6 %all-to-all-done.9 = bf16[8,24,1152]{2,1,0:T(8,128)(2,1)S(1)} async-done(((bf16[8,24,1152]{2,1,0:T(8,128)(2,1)}), bf16[8,24,1152]{2,1,0:T(8,128)(2,1)S(1)}, u32[]{:S(2)}, u32[]{:S(2)}) %all-to-all-start.9) | async-done | bytes 442400 | tf_op jit(solution)/shard_map/all_to_all | solution.py:917
  444.2 5.2 %collective-permute-done.13 = bf16[192,1152]{1,0:T(8,128)(2,1)S(1)} collective-permute-done((bf16[192,1152]{1,0:T(8,128)(2,1)S(1)}, bf16[192,1152]{1,0:T(8,128)(2,1)S(1)}, u32[]{:S(2)}, u32[]{:S(2)}) %collective-permute-start.13) | collective-permute-done | bytes 442400 | tf_op jit(solution)/shard_map/ppermute | solution.py:926
  449.8 5.8 %unpack.2 = (f32[768,768]{1,0:T(8,128)}, f32[768,768]{1,0:T(8,128)}, f32[768,768]{1,0:T(8,128)}, f32[768,768]{1,0:T(8,128)}) custom-call(s32[1,1]{1,0:T(1,128)} %bitcast.28.upper_ref, bf16[384,1920]{1,0:T(8,128)(2,1)} %copy-done.5, bf16[384,1920]{1,0:T(8,128)(2,1)} %collective-permute-done.16.other_ref), custom_call_target="tpu_custom_call" | custom-call | flops 40000000000 | bytes 4096 | tf_op jit(solution)/shard_map/unpack/pallas_call | solution.py:901
  455.6 0.9 copy-done.24
  456.6 4.3 unpack.3
  (123 shorter events, 16.2 us)
Async XLA Ops:
  7.2 139.7 %all-gather.5.cloned.1.call-start = ((), (), s32[]{:S(2)}) async-start(), calls=%async_computation.12 | async-start | bytes 5898240 | tf_op jit(solution)/shard_map/all_gather | solution.py:1043
  15.8 8.3 %copy-start.12 = (f32[768]{0:T(1024)S(1)}, f32[768]{0:T(1024)}, u32[]{:S(2)}) copy-start(f32[768]{0:T(1024)} %param.26) | copy-start | bytes 9220
  15.8 8.9 %copy-start.13 = (f32[768]{0:T(1024)S(1)}, f32[768]{0:T(1024)}, u32[]{:S(2)}) copy-start(f32[768]{0:T(1024)} %param.27) | copy-start | bytes 9220
  15.8 9.4 %copy-start.14 = (f32[768]{0:T(1024)S(1)}, f32[768]{0:T(1024)}, u32[]{:S(2)}) copy-start(f32[768]{0:T(1024)} %param.29) | copy-start | bytes 9220
  15.8 10.0 %copy-start.15 = (f32[768]{0:T(1024)S(1)}, f32[768]{0:T(1024)}, u32[]{:S(2)}) copy-start(f32[768]{0:T(1024)} %param.32) | copy-start | bytes 9220
  15.8 10.6 %copy-start.16 = (f32[768]{0:T(1024)S(1)}, f32[768]{0:T(1024)}, u32[]{:S(2)}) copy-start(f32[768]{0:T(1024)} %param.35) | copy-start | bytes 9220
  15.8 11.2 %copy-start.17 = (f32[768]{0:T(1024)S(1)}, f32[768]{0:T(1024)}, u32[]{:S(2)}) copy-start(f32[768]{0:T(1024)} %param.34) | copy-start | bytes 9220
  15.8 11.7 %copy-start.18 = (f32[768]{0:T(1024)S(1)}, f32[768]{0:T(1024)}, u32[]{:S(2)}) copy-start(f32[768]{0:T(1024)} %param.36) | copy-start | bytes 9220
  15.8 12.3 %copy-start.21 = (s32[8]{0:T(128)S(1)}, s32[8]{0:T(128)}, u32[]{:S(2)}) copy-start(s32[8]{0:T(128)} %param.24) | copy-start | bytes 100
  15.8 12.5 %copy-start.22 = (s32[8]{0:T(128)S(1)}, s32[8]{0:T(128)}, u32[]{:S(2)}) copy-start(s32[8]{0:T(128)} %param.25) | copy-start | bytes 100
  15.8 80.2 %all-to-all-start = ((bf16[8,264,768]{2,1,0:T(8,128)(2,1)}), bf16[8,264,768]{2,1,0:T(8,128)(2,1)S(1)}, u32[]{:S(2)}, u32[]{:S(2)}) async-start(bf16[8,264,768]{2,1,0:T(8,128)(2,1)} %get-tuple-element.98), calls=%async_computation | async-start | bytes 6488064 | tf_op jit(solution)/shard_map/all_to_all | solution.py:917
  23.3 123.6 %all-gather.7.cloned.1.call-start = ((), (), s32[]{:S(2)}) async-start(), calls=%async_computation.13 | async-start | bytes 5898240 | tf_op jit(solution)/shard_map/all_gather | solution.py:1044
  96.1 40.9 %copy-start.2 = (bf16[8,264,768]{2,1,0:T(8,128)(2,1)}, bf16[8,264,768]{2,1,0:T(8,128)(2,1)S(1)}, u32[]{:S(2)}) copy-start(bf16[8,264,768]{2,1,0:T(8,128)(2,1)S(1)} %all-to-all-done.refs_1_.g_ref) | copy-start | bytes 9732100
  96.1 40.9 %all-to-all-start.1 = ((bf16[8,128,768]{2,1,0:T(8,128)(2,1)}), bf16[8,128,768]{2,1,0:T(8,128)(2,1)}, u32[]{:S(2)}, u32[]{:S(2)}) async-start(bf16[8,128,768]{2,1,0:T(8,128)(2,1)} %get-tuple-element.99), calls=%async_computation.1 | async-start | bytes 3145728 | tf_op jit(solution)/shard_map/all_to_all | solution.py:917
  100.4 41.0 %copy-start.20 = (bf16[1,768]{1,0:T(2,128)(2,1)S(1)}, bf16[1,768]{1,0:T(2,128)(2,1)}, u32[]{:S(2)}) copy-start(bf16[1,768]{1,0:T(2,128)(2,1)} %param.39) | copy-start | bytes 4612
  100.4 1.2 collective-permute-start
  101.6 3.5 collective-permute-start.1
  137.0 43.0 %all-to-all-start.2 = ((bf16[8,136,768]{2,1,0:T(8,128)(2,1)}), bf16[8,136,768]{2,1,0:T(8,128)(2,1)}, u32[]{:S(2)}, u32[]{:S(2)}) async-start(bf16[8,136,768]{2,1,0:T(8,128)(2,1)} %get-tuple-element.100), calls=%async_computation.2 | async-start | bytes 3342336 | tf_op jit(solution)/shard_map/all_to_all | solution.py:917
  180.1 43.2 %all-to-all-start.3 = ((bf16[8,128,768]{2,1,0:T(8,128)(2,1)}), bf16[8,128,768]{2,1,0:T(8,128)(2,1)S(1)}, u32[]{:S(2)}, u32[]{:S(2)}) async-start(bf16[8,128,768]{2,1,0:T(8,128)(2,1)} %get-tuple-element.109), calls=%async_computation.3 | async-start | bytes 3145728 | tf_op jit(solution)/shard_map/all_to_all | solution.py:917
  223.3 38.8 %copy-start.1 = (bf16[8,128,768]{2,1,0:T(8,128)(2,1)}, bf16[8,128,768]{2,1,0:T(8,128)(2,1)S(1)}, u32[]{:S(2)}) copy-start(bf16[8,128,768]{2,1,0:T(8,128)(2,1)S(1)} %all-to-all-done.3) | copy-start | bytes 4718596
  223.3 42.9 %all-to-all-start.4 = ((bf16[8,136,768]{2,1,0:T(8,128)(2,1)}), bf16[8,136,768]{2,1,0:T(8,128)(2,1)S(1)}, u32[]{:S(2)}, u32[]{:S(2)}) async-start(bf16[8,136,768]{2,1,0:T(8,128)(2,1)} %get-tuple-element.110), calls=%async_computation.4 | async-start | bytes 3342336 | tf_op jit(solution)/shard_map/all_to_all | solution.py:917
  227.0 122.1 %reduce-scatter.3.cloned.1.call-start = ((), (), s32[]{:S(2)}) async-start(), calls=%async_computation.14 | async-start | bytes 5898240 | tf_op jit(solution)/shard_map/reduce_scatter | solution.py:1070
  266.3 5.2 %copy-start = (bf16[8,136,768]{2,1,0:T(8,128)(2,1)}, bf16[8,136,768]{2,1,0:T(8,128)(2,1)S(1)}, u32[]{:S(2)}) copy-start(bf16[8,136,768]{2,1,0:T(8,128)(2,1)S(1)} %all-to-all-done.4) | copy-start | bytes 5013508
  266.3 83.8 %all-to-all-start.5 = ((bf16[8,256,768]{2,1,0:T(8,128)(2,1)}), bf16[8,256,768]{2,1,0:T(8,128)(2,1)}, u32[]{:S(2)}, u32[]{:S(2)}) async-start(bf16[8,256,768]{2,1,0:T(8,128)(2,1)} %get-tuple-element.111), calls=%async_computation.5 | async-start | bytes 6291456 | tf_op jit(solution)/shard_map/all_to_all | solution.py:917
  270.8 150.2 %reduce-scatter.5.cloned.1.call-start = ((), (), s32[]{:S(2)}) async-start(), calls=%async_computation.15 | async-start | bytes 5959680 | tf_op jit(solution)/shard_map/reduce_scatter | solution.py:1117
  293.1 21.9 %collective-permute-start.2 = (bf16[384,768]{1,0:T(8,128)(2,1)S(1)}, bf16[384,768]{1,0:T(8,128)(2,1)}, u32[]{:S(2)}, u32[]{:S(2)}) collective-permute-start(bf16[384,768]{1,0:T(8,128)(2,1)S(1)} %dynamic-slice_bitcast_fusion.2), channel_id=1, source_target_pairs={{0,1},{1,0},{2,3},{3,2},{4,5},{5,4},{6,7},{7,6},{8,9},{9,8},{10,11... | collective-permute-start | bytes 1769480 | tf_op jit(solution)/shard_map/ppermute | solution.py:926
  311.1 2.6 copy-start.19
  311.1 3.9 copy-start.6
  312.4 23.3 %collective-permute-start.4 = (bf16[384,1152]{1,0:T(8,128)(2,1)S(1)}, bf16[384,1152]{1,0:T(8,128)(2,1)S(1)}, u32[]{:S(2)}, u32[]{:S(2)}) collective-permute-start(bf16[384,1152]{1,0:T(8,128)(2,1)S(1)} %dynamic-slice_bitcast_fusion.1), channel_id=1, source_target_pairs={{0,1},{1,0},{2,3},{3,2},{4,5},{5,4},{6,7},{7,6},{8,9},{9,8},{10,11... | collective-permute-start | bytes 2654216 | tf_op jit(solution)/shard_map/ppermute | solution.py:926
  316.2 19.5 %copy-start.3 = (bf16[768,1152]{1,0:T(8,128)(2,1)S(1)}, bf16[768,1152]{1,0:T(8,128)(2,1)}, u32[]{:S(2)}) copy-start(bf16[768,1152]{1,0:T(8,128)(2,1)} %get-tuple-element.131) | copy-start | bytes 5308420
  316.3 21.7 %collective-permute-start.3 = (bf16[192,768]{1,0:T(8,128)(2,1)S(1)}, bf16[192,768]{1,0:T(8,128)(2,1)S(1)}, u32[]{:S(2)}, u32[]{:S(2)}) collective-permute-start(bf16[192,768]{1,0:T(8,128)(2,1)S(1)} %dynamic-slice_bitcast_fusion.5), channel_id=1, source_target_pairs={{0,2},{1,3},{2,0},{3,1},{4,6},{5,7},{6,4},{7,5},{8,10},{9,11},{10,... | collective-permute-start | bytes 884744 | tf_op jit(solution)/shard_map/ppermute | solution.py:926
  335.7 1.5 copy-start.4
  336.0 1.4 copy-start.10
  336.0 1.4 copy-start.11
  336.1 11.9 %collective-permute-start.5 = (bf16[192,1152]{1,0:T(8,128)(2,1)S(1)}, bf16[192,1152]{1,0:T(8,128)(2,1)S(1)}, u32[]{:S(2)}, u32[]{:S(2)}) collective-permute-start(bf16[192,1152]{1,0:T(8,128)(2,1)S(1)} %dynamic-slice_bitcast_fusion.4), channel_id=1, source_target_pairs={{0,2},{1,3},{2,0},{3,1},{4,6},{5,7},{6,4},{7,5},{8,10},{9,11},{10,... | collective-permute-start | bytes 1327112 | tf_op jit(solution)/shard_map/ppermute | solution.py:926
  337.3 11.8 %collective-permute-start.11 = (bf16[384,1152]{1,0:T(8,128)(2,1)S(1)}, bf16[384,1152]{1,0:T(8,128)(2,1)S(1)}, u32[]{:S(2)}, u32[]{:S(2)}) collective-permute-start(bf16[384,1152]{1,0:T(8,128)(2,1)S(1)} %dynamic-slice_bitcast_fusion), channel_id=1, source_target_pairs={{0,1},{1,0},{2,3},{3,2},{4,5},{5,4},{6,7},{7,6},{8,9},{9,8},{10,11... | collective-permute-start | bytes 2654216 | tf_op jit(solution)/shard_map/ppermute | solution.py:926
  349.3 25.0 %collective-permute-start.12 = (bf16[192,1152]{1,0:T(8,128)(2,1)S(1)}, bf16[192,1152]{1,0:T(8,128)(2,1)S(1)}, u32[]{:S(2)}, u32[]{:S(2)}) collective-permute-start(bf16[192,1152]{1,0:T(8,128)(2,1)S(1)} %dynamic-slice_bitcast_fusion.3), channel_id=1, source_target_pairs={{0,2},{1,3},{2,0},{3,1},{4,6},{5,7},{6,4},{7,5},{8,10},{9,11},{10,... | collective-permute-start | bytes 1327112 | tf_op jit(solution)/shard_map/ppermute | solution.py:926
  350.1 25.1 %all-to-all-start.6 = ((bf16[8,24,1920]{2,1,0:T(8,128)(2,1)}), bf16[8,24,1920]{2,1,0:T(8,128)(2,1)S(1)}, u32[]{:S(2)}, u32[]{:S(2)}) async-start(bf16[8,24,1920]{2,1,0:T(8,128)(2,1)} %bitcast.35), calls=%async_computation.6 | async-start | bytes 1474560 | tf_op jit(solution)/shard_map/all_to_all | solution.py:917
  355.8 11.9 %copy-start.8 = (f32[8,768]{1,0:T(8,128)S(1)}, f32[8,768]{1,0:T(8,128)}, u32[]{:S(2)}) copy-start(f32[8,768]{1,0:T(8,128)} %get-tuple-element.138) | copy-start | bytes 73732
  355.8 11.9 %copy-start.9 = (f32[2,768]{1,0:T(2,128)S(1)}, f32[2,768]{1,0:T(2,128)}, u32[]{:S(2)}) copy-start(f32[2,768]{1,0:T(2,128)} %pad_maximum_fusion.1) | copy-start | bytes 18436
  367.7 1.3 collective-permute-start.6
  369.0 5.3 %collective-permute-start.7 = (f32[16,768]{1,0:T(8,128)S(1)}, f32[16,768]{1,0:T(8,128)S(1)}, u32[]{:S(2)}, u32[]{:S(2)}) collective-permute-start(f32[16,768]{1,0:T(8,128)S(1)} %add.105), channel_id=1, source_target_pairs={{0,2},{1,3},{2,0},{3,1},{4,6},{5,7},{6,4},{7,5},{8,10},{9,11},{10,... | collective-permute-start | bytes 147464 | tf_op jit(solution)/shard_map/ppermute | solution.py:926
  375.3 21.9 %all-to-all-start.7 = ((bf16[8,24,1152]{2,1,0:T(8,128)(2,1)}), bf16[8,24,1152]{2,1,0:T(8,128)(2,1)S(1)}, u32[]{:S(2)}, u32[]{:S(2)}) async-start(bf16[8,24,1152]{2,1,0:T(8,128)(2,1)} %bitcast.36), calls=%async_computation.7 | async-start | bytes 884736 | tf_op jit(solution)/shard_map/all_to_all | solution.py:917
  381.4 6.1 %collective-permute-start.8 = (f32[16,768]{1,0:T(8,128)S(1)}, f32[16,768]{1,0:T(8,128)S(1)}, u32[]{:S(2)}, u32[]{:S(2)}) collective-permute-start(f32[16,768]{1,0:T(8,128)S(1)} %add.106), channel_id=1, source_target_pairs={{0,4},{4,0},{8,12},{12,8},{16,20},{20,16},{24,28},{28,24},{1,5},{5... | collective-permute-start | bytes 147464 | tf_op jit(solution)/shard_map/ppermute | solution.py:926
  387.5 4.6 collective-permute-start.9
  392.1 5.0 %collective-permute-start.10 = (f32[16,768]{1,0:T(8,128)S(1)}, f32[16,768]{1,0:T(8,128)S(1)}, u32[]{:S(2)}, u32[]{:S(2)}) collective-permute-start(f32[16,768]{1,0:T(8,128)S(1)} %add.108), channel_id=1, source_target_pairs={{0,16},{4,20},{8,24},{12,28},{16,0},{20,4},{24,8},{28,12},{1,17},{... | collective-permute-start | bytes 147464 | tf_op jit(solution)/shard_map/ppermute | solution.py:926
  398.2 21.3 %all-to-all-start.8 = ((bf16[8,24,1920]{2,1,0:T(8,128)(2,1)}), bf16[8,24,1920]{2,1,0:T(8,128)(2,1)S(1)}, u32[]{:S(2)}, u32[]{:S(2)}) async-start(bf16[8,24,1920]{2,1,0:T(8,128)(2,1)} %broadcast_in_dim.8), calls=%async_computation.8 | async-start | bytes 1474560 | tf_op jit(solution)/shard_map/all_to_all | solution.py:917
  419.5 12.5 %collective-permute-start.15 = (bf16[192,1920]{1,0:T(8,128)(2,1)S(1)}, bf16[192,1920]{1,0:T(8,128)(2,1)S(1)}, u32[]{:S(2)}, u32[]{:S(2)}) collective-permute-start(bf16[192,1920]{1,0:T(8,128)(2,1)S(1)} %bitcast.87), channel_id=1, source_target_pairs={{0,2},{1,3},{2,0},{3,1},{4,6},{5,7},{6,4},{7,5},{8,10},{9,11},{10,... | collective-permute-start | bytes 2211848 | tf_op jit(solution)/shard_map/ppermute | solution.py:926
  425.9 15.7 %copy-start.23 = (f32[8]{0:T(128)S(1)}, f32[8]{0:T(128)}, u32[]{:S(2)}) copy-start(f32[8]{0:T(128)} %get-tuple-element.167) | copy-start | bytes 100
  425.9 15.2 %all-to-all-start.9 = ((bf16[8,24,1152]{2,1,0:T(8,128)(2,1)}), bf16[8,24,1152]{2,1,0:T(8,128)(2,1)S(1)}, u32[]{:S(2)}, u32[]{:S(2)}) async-start(bf16[8,24,1152]{2,1,0:T(8,128)(2,1)} %broadcast_in_dim.9), calls=%async_computation.11 | async-start | bytes 884736 | tf_op jit(solution)/shard_map/all_to_all | solution.py:917
  432.4 17.4 %copy-start.5 = (bf16[384,1920]{1,0:T(8,128)(2,1)}, bf16[384,1920]{1,0:T(8,128)(2,1)S(1)}, u32[]{:S(2)}) copy-start(bf16[384,1920]{1,0:T(8,128)(2,1)S(1)} %maximum_select_fusion.own_ref) | copy-start | bytes 4423684
  432.4 17.3 %collective-permute-start.16 = (bf16[384,1920]{1,0:T(8,128)(2,1)S(1)}, bf16[384,1920]{1,0:T(8,128)(2,1)}, u32[]{:S(2)}, u32[]{:S(2)}) collective-permute-start(bf16[384,1920]{1,0:T(8,128)(2,1)S(1)} %maximum_select_fusion.own_ref), channel_id=1, source_target_pairs={{0,1},{1,0},{2,3},{3,2},{4,5},{5,4},{6,7},{7,6},{8,9},{9,8},{10,11... | collective-permute-start | bytes 4423688 | tf_op jit(solution)/shard_map/ppermute | solution.py:926
  441.1 8.3 %collective-permute-start.13 = (bf16[192,1152]{1,0:T(8,128)(2,1)S(1)}, bf16[192,1152]{1,0:T(8,128)(2,1)S(1)}, u32[]{:S(2)}, u32[]{:S(2)}) collective-permute-start(bf16[192,1152]{1,0:T(8,128)(2,1)S(1)} %bitcast.95), channel_id=1, source_target_pairs={{0,2},{1,3},{2,0},{3,1},{4,6},{5,7},{6,4},{7,5},{8,10},{9,11},{10,... | collective-permute-start | bytes 1327112 | tf_op jit(solution)/shard_map/ppermute | solution.py:926
  449.7 6.0 %copy-start.7 = (bf16[384,1152]{1,0:T(8,128)(2,1)}, bf16[384,1152]{1,0:T(8,128)(2,1)S(1)}, u32[]{:S(2)}) copy-start(bf16[384,1152]{1,0:T(8,128)(2,1)S(1)} %maximum_select_fusion.1.own_ref) | copy-start | bytes 2654212
  449.7 5.9 %collective-permute-start.14 = (bf16[384,1152]{1,0:T(8,128)(2,1)S(1)}, bf16[384,1152]{1,0:T(8,128)(2,1)S(1)}, u32[]{:S(2)}, u32[]{:S(2)}) collective-permute-start(bf16[384,1152]{1,0:T(8,128)(2,1)S(1)} %maximum_select_fusion.1.own_ref), channel_id=1, source_target_pairs={{0,1},{1,0},{2,3},{3,2},{4,5},{5,4},{6,7},{7,6},{8,9},{9,8},{10,11... | collective-permute-start | bytes 2654216 | tf_op jit(solution)/shard_map/ppermute | solution.py:926
  455.6 0.9 copy-start.24
Sparse Core Ops, SparseCore 0:
  9.6 40.1 all-gather.4
  51.3 37.4 all-gather.6
  266.4 46.9 reduce-scatter.2
  349.2 49.5 reduce-scatter.4

commit v4 on v3

--- a/solution.py
+++ b/solution.py
@@ -99,8 +99,9 @@
     )(queries, keys, values)
 
 
-def attend_back_kernel(block, q_ref, k_ref, v_ref, weights_ref, g_ref, normed_ref,
-                       dq_ref, dk_ref, dv_ref, packed_ref, sums_ref, dq_acc, dk_acc, dv_acc):
+def attend_back_kernel(block, shares, place_ref, q_ref, k_ref, v_ref, weights_ref, g_ref, normed_ref,
+                       dq_ref, dk_ref, dv_ref, sums_ref, *refs):
+    share_refs, (packed_ref, dq_acc, dk_acc, dv_acc) = refs[:shares], refs[shares:]
     rows = q_ref.shape[0]
     keys = k_ref[...]
     values = v_ref[...]
@@ -143,6 +144,7 @@
     normed = normed_ref[...]
     packed_ref[:, : 2 * PAIR] = mm(normed, jnp.concatenate([dq, dk], axis=1)).astype(BF16)
     packed_ref[:, 2 * PAIR :] = mm(normed, dv).astype(BF16)
+    deal(packed_ref, share_refs, place_ref[0, 0])
     sums_ref[...] = jnp.concatenate(
         [
             jnp.sum(dq.astype(F32), axis=0, keepdims=True),
@@ -153,14 +155,15 @@
     )
 
 
-def attend_back(queries, keys, values, weights, grad_context, normed_t, start, pairs, block=256):
+def attend_back(queries, keys, values, weights, grad_context, normed_t, place, shares, start, pairs, block=256):
     rows, width = queries.shape
     spec = pl.BlockSpec((rows, PAIR), lambda p: (0, p + start))
     out_spec = pl.BlockSpec((rows, PAIR), lambda p: (0, p))
     return pl.pallas_call(
-        functools.partial(attend_back_kernel, block),
+        functools.partial(attend_back_kernel, block, shares),
         grid=(pairs,),
         in_specs=[
+            pl.BlockSpec(memory_space=pltpu.SMEM),
             spec,
             spec,
             spec,
@@ -172,15 +175,14 @@
             out_spec,
             out_spec,
             out_spec,
-            pl.BlockSpec((width, 3 * PAIR), lambda p: (0, p)),
             pl.BlockSpec((8, PAIR), lambda p: (0, p)),
-        ],
+        ]
+        + [pl.BlockSpec((width // shares, 3 * PAIR), lambda p: (0, p))] * shares,
         out_shape=[jax.ShapeDtypeStruct((rows, pairs * PAIR), BF16)] * 3
-        + [
-            jax.ShapeDtypeStruct((width, 3 * pairs * PAIR), BF16),
-            jax.ShapeDtypeStruct((8, pairs * PAIR), F32),
-        ],
+        + [jax.ShapeDtypeStruct((8, pairs * PAIR), F32)]
+        + [jax.ShapeDtypeStruct((width // shares, 3 * pairs * PAIR), BF16)] * shares,
         scratch_shapes=[
+            pltpu.VMEM((width, 3 * PAIR), BF16),
             pltpu.VMEM((rows, PAIR), BF16),
             pltpu.VMEM((rows, PAIR), F32),
             pltpu.VMEM((rows, PAIR), F32),
@@ -188,7 +190,7 @@
         compiler_params=params("arbitrary"),
         cost_estimate=cost(rows, rows),
         name="attend_back",
-    )(queries, keys, values, weights, grad_context, normed_t)
+    )(place, queries, keys, values, weights, grad_context, normed_t)
 
 
 def normalise(values):
@@ -637,9 +639,17 @@
     )(x0, x1, g, act, up, scale)
 
 
-def combine_kernel(weight_ref, back0_ref, back1_ref, dots0_ref, dots1_ref, columns_ref, ids_ref, logits_ref, pull_ref,
+def deal(rows_ref, share_refs, place):
+    count = share_refs[0].shape[0]
+    for index, share_ref in enumerate(share_refs):
+        first = jnp.bitwise_xor(place, index) * count
+        share_ref[...] = rows_ref[pl.ds(pl.multiple_of(first, count), count), :]
+
+
+def combine_kernel(shares, weight_ref, place_ref, back0_ref, back1_ref, dots0_ref, dots1_ref, columns_ref, ids_ref, logits_ref, pull_ref,
                    hidden_ref, grad_ref, context_ref, moe_ref, w_out_ref, router_ref, gain_ref,
-                   hid_grad_ref, con_grad_ref, out_grad_ref, sums_ref, router_grad_ref, probs_ref, branches):
+                   hid_grad_ref, con_grad_ref, sums_ref, router_grad_ref, probs_ref, *refs):
+    out_refs, (branches, out_rows) = refs[:shares], refs[shares:]
     step = pl.program_id(0)
     experts = logits_ref.shape[0]
     count0 = back0_ref.shape[0]
@@ -694,10 +704,11 @@
 
     @pl.when(step == pl.num_programs(0) - 1)
     def _():
-        out_grad_ref[...] = mm_tn(context_ref[...], branches[...]).astype(BF16)
-
-
-def combine(weight, back0, back1, dots0, dots1, columns, ids, logits, pull, hidden, grad_out, context, moe_in,
+        out_rows[...] = mm_tn(context_ref[...], branches[...]).astype(BF16)
+        deal(out_rows, out_refs, place_ref[0, 0])
+
+
+def combine(weight, place, shares, back0, back1, dots0, dots1, columns, ids, logits, pull, hidden, grad_out, context, moe_in,
             w_out, router_rows, gain, tile=256):
     rows, width = hidden.shape
     experts = logits.shape[0]
@@ -707,9 +718,10 @@
     row_spec = pl.BlockSpec((tile, width), lambda t: (t, 0))
     square = pl.BlockSpec((width, width), whole)
     return pl.pallas_call(
-        combine_kernel,
+        functools.partial(combine_kernel, shares),
         grid=(rows // tile,),
         in_specs=[
+            pl.BlockSpec(memory_space=pltpu.SMEM),
             pl.BlockSpec(memory_space=pltpu.SMEM),
             pl.BlockSpec((count, width), whole),
             pl.BlockSpec((count1, width), whole),
@@ -730,24 +742,24 @@
         out_specs=[
             row_spec,
             row_spec,
-            square,
             pl.BlockSpec((8, width), whole),
             pl.BlockSpec((experts, width), whole),
             pl.BlockSpec((experts, 1), whole),
-        ],
+        ]
+        + [pl.BlockSpec((width // shares, width), whole)] * shares,
         out_shape=[
             jax.ShapeDtypeStruct((rows, width), F32),
             jax.ShapeDtypeStruct((rows, width), BF16),
-            jax.ShapeDtypeStruct((width, width), BF16),
             jax.ShapeDtypeStruct((8, width), F32),
             jax.ShapeDtypeStruct((experts, width), F32),
             jax.ShapeDtypeStruct((experts, 1), F32),
-        ],
-        scratch_shapes=[pltpu.VMEM((rows, width), BF16)],
+        ]
+        + [jax.ShapeDtypeStruct((width // shares, width), BF16)] * shares,
+        scratch_shapes=[pltpu.VMEM((rows, width), BF16), pltpu.VMEM((width, width), BF16)],
         compiler_params=params("arbitrary"),
         cost_estimate=cost(rows, rows),
         name="combine",
-    )(weight, back0, back1, dots0, dots1, columns, ids, logits, pull, hidden, grad_out, context, moe_in, w_out,
+    )(weight, place, back0, back1, dots0, dots1, columns, ids, logits, pull, hidden, grad_out, context, moe_in, w_out,
       router_rows, gain)
 
 
@@ -903,8 +915,8 @@
         grid=(2, blocks),
         in_specs=[pl.BlockSpec(memory_space=pltpu.SMEM), source, source]
         + [pl.BlockSpec(memory_space=pl.ANY)] * len(earlier),
-        out_specs=[pl.BlockSpec((rows, width), lambda c, x: (c * blocks + x, 0))] * lead
-        + [pl.BlockSpec((rows, span), lambda c, x: (c * blocks + x, offset))] * 3,
+        out_specs=[pl.BlockSpec((rows, width), lambda c, x: (2 * x + c, 0))] * lead
+        + [pl.BlockSpec((rows, span), lambda c, x: (2 * x + c, offset))] * 3,
         out_shape=[jax.ShapeDtypeStruct((2 * total, width), F32)] * (3 + lead),
         input_output_aliases={3 + index: index for index in range(len(earlier))},
         compiler_params=params("arbitrary", "arbitrary"),
@@ -937,14 +949,6 @@
     return (lax.axis_index(axis) // bit) % 2
 
 
-def halve(value, axis, bit):
-    upper = is_upper(axis, bit)
-    halves = value.reshape((2, value.shape[0] // 2) + value.shape[1:])
-    mine = lax.dynamic_index_in_dim(halves, upper, 0, keepdims=False)
-    other = lax.dynamic_index_in_dim(halves, 1 - upper, 0, keepdims=False)
-    return (mine.astype(F32) + trade(other, axis, bit).astype(F32)).astype(value.dtype)
-
-
 def rejoin(value, axis, bit):
     got = trade(value, axis, bit)
     upper = is_upper(axis, bit) == 1
@@ -958,18 +962,11 @@
     return swap(copies, axis)
 
 
-def core_part(value):
-    return halve(value, "narrow", 1)
-
-
-def outer_part(value):
-    for bit in list(bits("narrow"))[1:]:
-        value = halve(value, "narrow", bit)
-    return value
-
-
-def narrow_part(value):
-    return outer_part(core_part(value))
+def narrow_part(shares):
+    total = shares[0].astype(F32)
+    for index, share in enumerate(shares[1:], 1):
+        total = total + trade(share, "narrow", index).astype(F32)
+    return total.astype(BF16)
 
 
 def wide_part(value):
@@ -1037,6 +1034,7 @@
     weight = jnp.sum(member * factor).reshape(1, 1)
     ids = routes.reshape(1, rows)
     router_rows = jnp.transpose(router)
+    place = lax.axis_index("narrow").reshape(1, 1)
 
     slots, columns, grad_outgoing = route(routes, grad_out, experts, capacity)
     grad_rows = swap(grad_outgoing, "wide")
@@ -1075,8 +1073,10 @@
     dots1 = jnp.pad(extras, ((0, 0), (0, 0), (0, EXTRA))).reshape(EXTRA, experts * (half + EXTRA))
     dots0 = jnp.concatenate([extras[3:], extras[:3]], axis=0).reshape(EXTRA, experts * half)
     pull = (BALANCE * experts * fraction).reshape(experts, 1)
-    hid_grad, con_grad, out_grad, sums, router_grad, prob_sums = combine(
+    hid_grad, con_grad, sums, router_grad, prob_sums, *out_grad = combine(
         weight,
+        place,
+        narrow_count,
         back0.reshape(experts * half, width),
         back1.reshape(experts * (half + EXTRA), width),
         dots0,
@@ -1096,16 +1096,17 @@
     pairs = width // PAIR
     span = pairs // ATTEND_CALLS
     grads, bias_sums = [], []
-    out_core = core_part(out_grad)
-    packed = [outer_part(out_core)]
+    packed = [narrow_part(out_grad)]
     for call in range(ATTEND_CALLS):
-        dq, dk, dv, weights, column_sums = attend_back(
+        dq, dk, dv, column_sums, *weights = attend_back(
             queries,
             keys,
             values,
             soft_weights,
-            after(con_grad, out_core) if call else con_grad,
+            con_grad,
             normed_t,
+            place,
+            narrow_count,
             call * span,
             span,
         )
@@ -1114,8 +1115,7 @@
         bias_sums.append(column_sums)
     early = jnp.concatenate(packed[:-1], axis=1)
     hid_grad = after(hid_grad, early)
-    down_grad = lax.psum_scatter(after(down_sums, early, in_grad), "narrow", scatter_dimension=0)
-    place = lax.axis_index("narrow").reshape(1, 1)
+    down_grad = lax.psum_scatter(after(down_sums, early, in_grad, column_sums), "narrow", scatter_dimension=0)
     grad_w_in, grad_w_down, grad_bias_in, grad_bias_down = unpack_expert(
         place, down_grad, in_grad, width // narrow_count
     )

time: 470 us -> 467 us (level)
    ppermute x17 -> x20, waiting for transfers between devices: 34.9 us -> 36.5 us  [trade(): lax.ppermute(value, axis, [(place, place ^ bit) for place in range(count)])]
    ppermute x17 -> x20, starting transfers between devices: 15.6 us -> 16.5 us  [trade(): lax.ppermute(value, axis, [(place, place ^ bit) for place in range(count)])]
  transfers between devices with their start and end apart: 31 -> 34, of which waited for: 17 -> 20; matrix products, arithmetic and copies ran while one was open for 5% -> 4% of each run, Pallas kernels for 50% -> 51%
where the time goes in v4:
time: 467 us; the launch traced here: 465 us
  Pallas kernels  240 us (51%)
  waiting for transfers between devices  118 us (25%)
  starting transfers between devices  65.9 us (14%)
  between operations  16 us (3%)
  local copies, waits for them, and re-layouts  12.2 us (3%)
  other arithmetic  7.22 us (2%)
  blocking collectives  5.61 us (1%)
    all_to_all x10, waiting for transfers between devices, swap(): return lax.all_to_all(blocks, axis, split_axis=0, concat_axis=0, tiled=True)  80.1 us
    pallas_call x2, Pallas kernels, expert(): pl.pallas_call(functools.partial(expert_kernel, parts, chunk), grid=(part...  66.1 us
    all_to_all x10, starting transfers between devices, swap(): return lax.all_to_all(blocks, axis, split_axis=0, concat_axis=0, tiled=True)  49.1 us
    ppermute x20, waiting for transfers between devices, trade(): lax.ppermute(value, axis, [(place, place ^ bit) for place in range(count)])  36.5 us
    pallas_call x2, Pallas kernels, attend_back(): pl.pallas_call(functools.partial(attend_back_kernel, block, shares), grid...  36.2 us
    pallas_call x1, Pallas kernels, weight_grads(): pl.pallas_call(functools.partial(weight_kernel, parts), grid=(parts, 2),...  33.5 us
    pallas_call x1, Pallas kernels, attend(): pl.pallas_call(functools.partial(attend_kernel, block), grid=(pairs,), in...  20.5 us
    pallas_call x1, Pallas kernels, combine(): pl.pallas_call(functools.partial(combine_kernel, shares), grid=(rows // t...  19.1 us
  transfers between devices with their start and end apart: 34, of which 20 were waited for; matrix products, arithmetic and copies ran while one was open for 4% of the time, Pallas kernels for 51%

profile of v4, /device:TPU:0, one launch (start us, length us, event | category | flops | bytes accessed | tf_op | source)
XLA Modules:
  0.0 465.1 jit_solution(15021585032804157554)
XLA Ops:
  7.9 7.8 %route.1 = (s32[1,1024]{1,0:T(1,128)}, s32[1024,2]{1,0:T(8,128)}, bf16[8,264,768]{2,1,0:T(8,128)(2,1)}) custom-call(s32[1,1024]{1,0:T(1,128)} %bitcast.54, bf16[1024,768]{1,0:T(8,128)(2,1)} %grad_ref.3), custom_call_target="tpu_custom_call" | custom-call | flops 3221225472 | bytes 4718592 | tf_op jit(solution)/shard_map/route/pallas_call | solution.py:288
  15.8 7.4 %all-to-all-start = ((bf16[8,264,768]{2,1,0:T(8,128)(2,1)}), bf16[8,264,768]{2,1,0:T(8,128)(2,1)S(1)}, u32[]{:S(2)}, u32[]{:S(2)}) async-start(bf16[8,264,768]{2,1,0:T(8,128)(2,1)} %get-tuple-element.106), calls=%async_computation | async-start | bytes 6488064 | tf_op jit(solution)/shard_map/all_to_all | solution.py:929
  28.9 8.3 %project.1 = (bf16[768,1024]{1,0:T(8,128)(2,1)}, bf16[1024,768]{1,0:T(8,128)(2,1)}, bf16[1024,768]{1,0:T(8,128)(2,1)}, bf16[1024,768]{1,0:T(8,128)(2,1)}) custom-call(bf16[1024,768]{1,0:T(8,128)(2,1)} %refs_6_.1, f32[1,768]{1,0:T(1,128)} %reshape.148.gain_ref.refs_8_, f32[1,768]{1,0:T(1,128)} %reshape.149.shift_ref, bf16[768,768]{1,0:T(8,128)(2,1)} %refs_9_.1, ...), custom_call_target="tpu_custom_call" | custom-call | flops 3623878656 | bytes 11403264 | tf_op jit(solution)/shard_map/project/pallas_call | solution.py:327
  37.2 20.5 %attend.1 = (bf16[1024,768]{1,0:T(8,128)(2,1)}, bf16[6,2,2560,256]{3,2,1,0:T(8,128)(2,1)}) custom-call(bf16[1024,768]{1,0:T(8,128)(2,1)} %get-tuple-element.98.q_ref, bf16[1024,768]{1,0:T(8,128)(2,1)} %get-tuple-element.99.k_ref, bf16[1024,768]{1,0:T(8,128)(2,1)} %get-tuple-element.100.v_ref), custom_call_target="tpu_custom_call" | custom-call | flops 6442450944 | bytes 6291456 | tf_op jit(solution)/shard_map/attend/pallas_call | solution.py:87
  57.7 7.2 %settle.1 = (f32[1024,768]{1,0:T(8,128)}, bf16[1024,768]{1,0:T(8,128)(2,1)}, f32[8,1024]{1,0:T(8,128)}) custom-call(bf16[1024,768]{1,0:T(8,128)(2,1)} %get-tuple-element.101.context_ref, bf16[1024,768]{1,0:T(8,128)(2,1)} %refs_6_.1, bf16[768,768]{1,0:T(8,128)(2,1)} %w_out_ref.3, f32[1,768]{1,0:T(1,128)} %reshape.152.bias_ref, f32[1,768]{1,0:T(1,128)} %reshape.153.gain_ref, ...), custom_call_target="tpu_custom_call" | custom-call | flops 1207959552 | bytes 9043968 | tf_op jit(solution)/shard_map/settle/pallas_call | solution.py:355
  64.9 8.6 %dispatch.1 = (bf16[8,128,768]{2,1,0:T(8,128)(2,1)}, bf16[8,136,768]{2,1,0:T(8,128)(2,1)}) custom-call(f32[1,1]{1,0:T(1,128)} %bitcast.2.weight_ref, s32[1,1024]{1,0:T(1,128)} %get-tuple-element.97.slots_ref, s32[1,1024]{1,0:T(1,128)} %bitcast.55, f32[8,1024]{1,0:T(8,128)} %get-tuple-element.102.logits_ref, bf16[1024,768]{1,0:T(8,128)(2,1)} %get-tuple-element.103.moe_ref), custom_call_target="tpu_custom_call" | custom-call | flops 3221225472 | bytes 4718592 | tf_op jit(solution)/shard_map/dispatch/pallas_call | solution.py:402
  73.4 22.6 %all-to-all-done.refs_1_.g_ref = bf16[8,264,768]{2,1,0:T(8,128)(2,1)S(1)} async-done(((bf16[8,264,768]{2,1,0:T(8,128)(2,1)}), bf16[8,264,768]{2,1,0:T(8,128)(2,1)S(1)}, u32[]{:S(2)}, u32[]{:S(2)}) %all-to-all-start) | async-done | bytes 3244064 | tf_op jit(solution)/shard_map/all_to_all | solution.py:929
  96.1 4.3 all-to-all-start.1
  100.5 1.1 collective-permute-done
  101.6 1.5 collective-permute-start.1
  103.1 2.0 collective-permute-done.1
  105.6 31.4 %all-to-all-done.1.refs_0_.x0_ref = bf16[8,128,768]{2,1,0:T(8,128)(2,1)} async-done(((bf16[8,128,768]{2,1,0:T(8,128)(2,1)}), bf16[8,128,768]{2,1,0:T(8,128)(2,1)}, u32[]{:S(2)}, u32[]{:S(2)}) %all-to-all-start.1) | async-done | bytes 1572896 | tf_op jit(solution)/shard_map/all_to_all | solution.py:929
  137.0 4.4 all-to-all-start.2
  141.5 5.6 %all-gather.1.refs_3_ = bf16[4,1,768]{2,1,0:T(2,128)(2,1)} all-gather(bf16[1,1,768]{2,1,0:T(2,128)(2,1)S(1)} %bitcast.58), channel_id=2, replica_groups=mesh['wide'=8,'narrow'=4] {'narrow'}, dimensions={0}, use_global_device_ids=true | all-gather | bytes 7680 | tf_op jit(solution)/shard_map/all_gather | solution.py:1052
  147.1 33.0 %expert.2 = (bf16[4,2,1024,768]{3,2,1,0:T(8,128)(2,1)}, bf16[4,2,1024,768]{3,2,1,0:T(8,128)(2,1)}, bf16[8,256,768]{2,1,0:T(8,128)(2,1)}, bf16[8,128,768]{2,1,0:T(8,128)(2,1)}, bf16[8,8,128]{2,1,0:T(8,128)(2,1)}) custom-call(bf16[8,128,768]{2,1,0:T(8,128)(2,1)} %all-to-all-done.1.refs_0_.x0_ref, bf16[8,264,768]{2,1,0:T(8,128)(2,1)} %copy-done.2, ...), custom_call_target="tpu_custom_call" | custom-call | flops 14495514624 | bytes 12582912 | tf_op jit(solution)/shard_map/expert/pallas_call | solution.py:515
  180.2 5.8 %all-to-all-start.3 = ((bf16[8,128,768]{2,1,0:T(8,128)(2,1)}), bf16[8,128,768]{2,1,0:T(8,128)(2,1)S(1)}, u32[]{:S(2)}, u32[]{:S(2)}) async-start(bf16[8,128,768]{2,1,0:T(8,128)(2,1)} %get-tuple-element.117), calls=%async_computation.3 | async-start | bytes 3145728 | tf_op jit(solution)/shard_map/all_to_all | solution.py:929
  186.0 33.2 %expert.3 = (bf16[4,2,1024,768]{3,2,1,0:T(8,128)(2,1)}, bf16[4,2,1024,768]{3,2,1,0:T(8,128)(2,1)}, bf16[8,256,768]{2,1,0:T(8,128)(2,1)}, bf16[8,136,768]{2,1,0:T(8,128)(2,1)}) custom-call(bf16[8,136,768]{2,1,0:T(8,128)(2,1)} %all-to-all-done.2.refs_0_.x1_ref, ...), custom_call_target="tpu_custom_call", output_to_operand_aliasing={{0}: (6, {}), {1}: (7, {}), {2}: (8, {})} | custom-call | flops 14495514624 | bytes 12582912 | tf_op jit(solution)/shard_map/expert/pallas_call | solution.py:515
  219.1 4.4 all-to-all-done.3
  223.5 1.1 copy-done.1
  224.6 3.6 all-to-all-start.4
  228.5 1.4 convert_reduce_fusion
  229.9 33.5 %weight_grads.1 = (bf16[4,776,768]{2,1,0:T(8,128)(2,1)}, bf16[4,768,768]{2,1,0:T(8,128)(2,1)}) custom-call(bf16[8,128,768]{2,1,0:T(8,128)(2,1)} %all-to-all-done.1.refs_0_.x0_ref, bf16[8,136,768]{2,1,0:T(8,128)(2,1)} %all-to-all-done.2.refs_0_.x1_ref, bf16[8,264,768]{2,1,0:T(8,128)(2,1)} %copy-done.2, bf16[4,2,1024,768]{3,2,1,0:T(8,128)(2,1)} %get-tuple-element.124.act_ref, ...), custom_call_target="tpu_custom_call" | custom-call | flops 28991029248 | bytes 25165824 | tf_op jit(solution)/shard_map/weight_grads/pallas_call | solution.py:610
  263.4 4.2 all-to-all-done.4
  267.6 4.5 all-to-all-start.5
  272.9 0.7 reshape.162.dots1_ref
  274.2 19.1 %combine.1 = (f32[1024,768]{1,0:T(8,128)}, bf16[1024,768]{1,0:T(8,128)(2,1)}, f32[8,768]{1,0:T(8,128)}, f32[8,768]{1,0:T(8,128)}, f32[8,1]{1,0:T(8,128)}, /*inde...) custom-call(f32[1,1]{1,0:T(1,128)} %bitcast.2.weight_ref, ...), custom_call_target="tpu_custom_call" | custom-call | flops 1024 | bytes 1024 | tf_op jit(solution)/shard_map/combine/pallas_call | solution.py:720
  293.5 1.7 collective-permute-start.3
  295.3 18.0 %attend_back.2 = (bf16[1024,384]{1,0:T(8,128)(2,1)}, bf16[1024,384]{1,0:T(8,128)(2,1)}, bf16[1024,384]{1,0:T(8,128)(2,1)}, f32[8,384]{1,0:T(8,128)}, bf16[192,11...) custom-call(s32[1,1]{1,0:T(1,128)} %bitcast.7.place_ref, ...), custom_call_target="tpu_custom_call" | custom-call | flops 1024 | bytes 1024 | tf_op jit(solution)/shard_map/attend_back/pallas_call | solution.py:162
  313.7 1.6 collective-permute-start.6
  315.3 18.2 %attend_back.3 = (bf16[1024,384]{1,0:T(8,128)(2,1)}, bf16[1024,384]{1,0:T(8,128)(2,1)}, bf16[1024,384]{1,0:T(8,128)(2,1)}, f32[8,384]{1,0:T(8,128)}, bf16[192,11...) custom-call(s32[1,1]{1,0:T(1,128)} %bitcast.7.place_ref, ...), custom_call_target="tpu_custom_call" | custom-call | flops 1024 | bytes 1024 | tf_op jit(solution)/shard_map/attend_back/pallas_call | solution.py:162
  333.8 1.7 collective-permute-done.6
  335.5 9.1 %collective-permute-done.7 = bf16[192,1152]{1,0:T(8,128)(2,1)S(1)} collective-permute-done((bf16[192,1152]{1,0:T(8,128)(2,1)}, bf16[192,1152]{1,0:T(8,128)(2,1)S(1)}, u32[]{:S(2)}, u32[]{:S(2)}) %collective-permute-start.7) | collective-permute-done | bytes 442400 | tf_op jit(solution)/shard_map/ppermute | solution.py:938
  344.8 0.9 pad_maximum_fusion
  346.0 0.8 copy-done.26
  347.1 1.1 collective-permute-start.15
  348.4 5.5 %all-to-all-start.6 = ((bf16[8,24,1920]{2,1,0:T(8,128)(2,1)}), bf16[8,24,1920]{2,1,0:T(8,128)(2,1)S(1)}, u32[]{:S(2)}, u32[]{:S(2)}) async-start(bf16[8,24,1920]{2,1,0:T(8,128)(2,1)} %bitcast.18), calls=%async_computation.6 | async-start | bytes 1474560 | tf_op jit(solution)/shard_map/all_to_all | solution.py:929
  353.9 10.8 %close.1 = (bf16[1024,768]{1,0:T(8,128)(2,1)}, f32[8,768]{1,0:T(8,128)}) custom-call(bf16[1024,384]{1,0:T(8,128)(2,1)} %get-tuple-element.130.refs_0_, bf16[1024,384]{1,0:T(8,128)(2,1)} %get-tuple-element.131.refs_1_, bf16[1024,384]{1,0:T(8,128)(2,1)} %get-tuple-element.132.refs_2_, bf16[1024,384]{1,0:T(8,128)(2,1)} %get-tuple-element.133.refs_3_, ...), custom_call_target="tpu_custom_call" | custom-call | flops 40000000000 | bytes 4096 | tf_op jit(solution)/shard_map/close/pallas_call | solution.py:803
  364.7 0.7 slice.56
  365.9 0.9 collective-permute-done.8
  366.8 1.1 collective-permute-start.9
  368.3 1.0 add_convert_fusion
  369.3 3.3 collective-permute-done.9
  372.5 1.4 all-to-all-done.6
  374.0 4.3 all-to-all-start.7
  378.3 2.0 collective-permute-start.10
  380.4 4.6 collective-permute-done.10
  385.0 2.1 collective-permute-start.11
  387.1 2.2 collective-permute-done.11
  389.2 1.8 collective-permute-start.12
  391.1 3.2 collective-permute-done.12
  394.4 0.9 broadcast_in_dim.8
  395.3 5.6 %all-to-all-start.8 = ((bf16[8,24,1920]{2,1,0:T(8,128)(2,1)}), bf16[8,24,1920]{2,1,0:T(8,128)(2,1)S(1)}, u32[]{:S(2)}, u32[]{:S(2)}) async-start(bf16[8,24,1920]{2,1,0:T(8,128)(2,1)} %broadcast_in_dim.8), calls=%async_computation.8 | async-start | bytes 1474560 | tf_op jit(solution)/shard_map/all_to_all | solution.py:929
  400.9 7.7 %block_output.1 = bf16[1024,768]{1,0:T(8,128)(2,1)} custom-call(bf16[2048,768]{1,0:T(8,128)(2,1)} %bitcast.6.back_ref, s32[1024,2]{1,0:T(8,128)} %get-tuple-element.120.columns_ref, s32[1,1024]{1,0:T(1,128)} %bitcast.57, f32[8,1024]{1,0:T(8,128)} %get-tuple-element.102.logits_ref, f32[1024,768]{1,0:T(8,128)} %get-tuple-element.121.hidden_ref), custom_call_target="tpu_custom_call" | custom-call | flops 40000000000 | bytes 4096 | tf_op jit(solution)/shard_map/block_output/pallas_call | solution.py:831
  408.6 8.5 %all-to-all-done.8 = bf16[8,24,1920]{2,1,0:T(8,128)(2,1)S(1)} async-done(((bf16[8,24,1920]{2,1,0:T(8,128)(2,1)}), bf16[8,24,1920]{2,1,0:T(8,128)(2,1)S(1)}, u32[]{:S(2)}, u32[]{:S(2)}) %all-to-all-start.8) | async-done | bytes 737312 | tf_op jit(solution)/shard_map/all_to_all | solution.py:929
  417.7 4.1 unpack_expert.1
  421.8 0.8 broadcast_in_dim.9
  422.6 3.6 all-to-all-start.9
  426.2 3.3 collective-permute-done.18
  430.1 7.6 %all-to-all-done.9 = bf16[8,24,1152]{2,1,0:T(8,128)(2,1)S(1)} async-done(((bf16[8,24,1152]{2,1,0:T(8,128)(2,1)}), bf16[8,24,1152]{2,1,0:T(8,128)(2,1)S(1)}, u32[]{:S(2)}, u32[]{:S(2)}) %all-to-all-start.9) | async-done | bytes 442400 | tf_op jit(solution)/shard_map/all_to_all | solution.py:929
  437.7 1.2 collective-permute-start.16
  441.4 4.6 collective-permute-done.16
  446.4 5.8 %unpack.2 = (f32[768,768]{1,0:T(8,128)}, f32[768,768]{1,0:T(8,128)}, f32[768,768]{1,0:T(8,128)}, f32[768,768]{1,0:T(8,128)}) custom-call(s32[1,1]{1,0:T(1,128)} %bitcast.17.upper_ref, bf16[384,1920]{1,0:T(8,128)(2,1)} %copy-done.3, bf16[384,1920]{1,0:T(8,128)(2,1)} %collective-permute-done.19.other_ref), custom_call_target="tpu_custom_call" | custom-call | flops 40000000000 | bytes 4096 | tf_op jit(solution)/shard_map/unpack/pallas_call | solution.py:913
  452.2 0.9 copy-done.24
  453.1 4.3 unpack.3
  (124 shorter events, 14.8 us)
Async XLA Ops:
  7.2 139.9 %all-gather.5.cloned.1.call-start = ((), (), s32[]{:S(2)}) async-start(), calls=%async_computation.12 | async-start | bytes 5898240 | tf_op jit(solution)/shard_map/all_gather | solution.py:1041
  15.8 8.3 %copy-start.12 = (f32[768]{0:T(1024)S(1)}, f32[768]{0:T(1024)}, u32[]{:S(2)}) copy-start(f32[768]{0:T(1024)} %param.26) | copy-start | bytes 9220
  15.8 8.9 %copy-start.13 = (f32[768]{0:T(1024)S(1)}, f32[768]{0:T(1024)}, u32[]{:S(2)}) copy-start(f32[768]{0:T(1024)} %param.27) | copy-start | bytes 9220
  15.8 9.4 %copy-start.14 = (f32[768]{0:T(1024)S(1)}, f32[768]{0:T(1024)}, u32[]{:S(2)}) copy-start(f32[768]{0:T(1024)} %param.29) | copy-start | bytes 9220
  15.8 10.0 %copy-start.15 = (f32[768]{0:T(1024)S(1)}, f32[768]{0:T(1024)}, u32[]{:S(2)}) copy-start(f32[768]{0:T(1024)} %param.32) | copy-start | bytes 9220
  15.8 10.6 %copy-start.16 = (f32[768]{0:T(1024)S(1)}, f32[768]{0:T(1024)}, u32[]{:S(2)}) copy-start(f32[768]{0:T(1024)} %param.35) | copy-start | bytes 9220
  15.8 11.2 %copy-start.17 = (f32[768]{0:T(1024)S(1)}, f32[768]{0:T(1024)}, u32[]{:S(2)}) copy-start(f32[768]{0:T(1024)} %param.34) | copy-start | bytes 9220
  15.8 11.7 %copy-start.18 = (f32[768]{0:T(1024)S(1)}, f32[768]{0:T(1024)}, u32[]{:S(2)}) copy-start(f32[768]{0:T(1024)} %param.36) | copy-start | bytes 9220
  15.8 12.3 %copy-start.21 = (s32[8]{0:T(128)S(1)}, s32[8]{0:T(128)}, u32[]{:S(2)}) copy-start(s32[8]{0:T(128)} %param.24) | copy-start | bytes 100
  15.8 12.5 %copy-start.22 = (s32[8]{0:T(128)S(1)}, s32[8]{0:T(128)}, u32[]{:S(2)}) copy-start(s32[8]{0:T(128)} %param.25) | copy-start | bytes 100
  15.8 80.2 %all-to-all-start = ((bf16[8,264,768]{2,1,0:T(8,128)(2,1)}), bf16[8,264,768]{2,1,0:T(8,128)(2,1)S(1)}, u32[]{:S(2)}, u32[]{:S(2)}) async-start(bf16[8,264,768]{2,1,0:T(8,128)(2,1)} %get-tuple-element.106), calls=%async_computation | async-start | bytes 6488064 | tf_op jit(solution)/shard_map/all_to_all | solution.py:929
  23.3 123.8 %all-gather.7.cloned.1.call-start = ((), (), s32[]{:S(2)}) async-start(), calls=%async_computation.13 | async-start | bytes 5898240 | tf_op jit(solution)/shard_map/all_gather | solution.py:1042
  96.1 41.0 %copy-start.2 = (bf16[8,264,768]{2,1,0:T(8,128)(2,1)}, bf16[8,264,768]{2,1,0:T(8,128)(2,1)S(1)}, u32[]{:S(2)}) copy-start(bf16[8,264,768]{2,1,0:T(8,128)(2,1)S(1)} %all-to-all-done.refs_1_.g_ref) | copy-start | bytes 9732100
  96.1 40.9 %all-to-all-start.1 = ((bf16[8,128,768]{2,1,0:T(8,128)(2,1)}), bf16[8,128,768]{2,1,0:T(8,128)(2,1)}, u32[]{:S(2)}, u32[]{:S(2)}) async-start(bf16[8,128,768]{2,1,0:T(8,128)(2,1)} %get-tuple-element.107), calls=%async_computation.1 | async-start | bytes 3145728 | tf_op jit(solution)/shard_map/all_to_all | solution.py:929
  100.4 1.2 collective-permute-start
  101.6 3.5 collective-permute-start.1
  137.0 4.5 copy-start.20
  137.0 43.2 %all-to-all-start.2 = ((bf16[8,136,768]{2,1,0:T(8,128)(2,1)}), bf16[8,136,768]{2,1,0:T(8,128)(2,1)}, u32[]{:S(2)}, u32[]{:S(2)}) async-start(bf16[8,136,768]{2,1,0:T(8,128)(2,1)} %get-tuple-element.108), calls=%async_computation.2 | async-start | bytes 3342336 | tf_op jit(solution)/shard_map/all_to_all | solution.py:929
  180.2 43.3 %all-to-all-start.3 = ((bf16[8,128,768]{2,1,0:T(8,128)(2,1)}), bf16[8,128,768]{2,1,0:T(8,128)(2,1)S(1)}, u32[]{:S(2)}, u32[]{:S(2)}) async-start(bf16[8,128,768]{2,1,0:T(8,128)(2,1)} %get-tuple-element.117), calls=%async_computation.3 | async-start | bytes 3145728 | tf_op jit(solution)/shard_map/all_to_all | solution.py:929
  223.5 1.1 copy-start.1
  224.6 42.9 %all-to-all-start.4 = ((bf16[8,136,768]{2,1,0:T(8,128)(2,1)}), bf16[8,136,768]{2,1,0:T(8,128)(2,1)S(1)}, u32[]{:S(2)}, u32[]{:S(2)}) async-start(bf16[8,136,768]{2,1,0:T(8,128)(2,1)} %get-tuple-element.118), calls=%async_computation.4 | async-start | bytes 3342336 | tf_op jit(solution)/shard_map/all_to_all | solution.py:929
  228.3 117.5 %reduce-scatter.3.cloned.1.call-start = ((), (), s32[]{:S(2)}) async-start(), calls=%async_computation.14 | async-start | bytes 5898240 | tf_op jit(solution)/shard_map/reduce_scatter | solution.py:1068
  267.6 5.2 %copy-start = (bf16[8,136,768]{2,1,0:T(8,128)(2,1)}, bf16[8,136,768]{2,1,0:T(8,128)(2,1)S(1)}, u32[]{:S(2)}) copy-start(bf16[8,136,768]{2,1,0:T(8,128)(2,1)S(1)} %all-to-all-done.4) | copy-start | bytes 5013508
  267.6 80.8 %all-to-all-start.5 = ((bf16[8,256,768]{2,1,0:T(8,128)(2,1)}), bf16[8,256,768]{2,1,0:T(8,128)(2,1)}, u32[]{:S(2)}, u32[]{:S(2)}) async-start(bf16[8,256,768]{2,1,0:T(8,128)(2,1)} %get-tuple-element.119), calls=%async_computation.5 | async-start | bytes 6291456 | tf_op jit(solution)/shard_map/all_to_all | solution.py:929
  272.1 145.6 %reduce-scatter.5.cloned.1.call-start = ((), (), s32[]{:S(2)}) async-start(), calls=%async_computation.15 | async-start | bytes 5959680 | tf_op jit(solution)/shard_map/reduce_scatter | solution.py:1118
  293.4 21.9 %collective-permute-start.2 = (bf16[192,768]{1,0:T(8,128)(2,1)}, bf16[192,768]{1,0:T(8,128)(2,1)S(1)}, u32[]{:S(2)}, u32[]{:S(2)}) collective-permute-start(bf16[192,768]{1,0:T(8,128)(2,1)} %get-tuple-element.138), channel_id=1, source_target_pairs={{0,1},{1,0},{2,3},{3,2},{4,5},{5,4},{6,7},{7,6},{8,9},{9,8},{10,11... | collective-permute-start | bytes 884744 | tf_op jit(solution)/shard_map/ppermute | solution.py:938
  293.5 40.1 %collective-permute-start.3 = (bf16[192,768]{1,0:T(8,128)(2,1)}, bf16[192,768]{1,0:T(8,128)(2,1)S(1)}, u32[]{:S(2)}, u32[]{:S(2)}) collective-permute-start(bf16[192,768]{1,0:T(8,128)(2,1)} %get-tuple-element.139), channel_id=1, source_target_pairs={{0,2},{1,3},{2,0},{3,1},{4,6},{5,7},{6,4},{7,5},{8,10},{9,11},{10,... | collective-permute-start | bytes 884744 | tf_op jit(solution)/shard_map/ppermute | solution.py:938
  295.2 38.4 %collective-permute-start.4 = (bf16[192,768]{1,0:T(8,128)(2,1)}, bf16[192,768]{1,0:T(8,128)(2,1)S(1)}, u32[]{:S(2)}, u32[]{:S(2)}) collective-permute-start(bf16[192,768]{1,0:T(8,128)(2,1)} %get-tuple-element.140), channel_id=1, source_target_pairs={{0,3},{1,2},{2,1},{3,0},{4,7},{5,6},{6,5},{7,4},{8,11},{9,10},{10,... | collective-permute-start | bytes 884744 | tf_op jit(solution)/shard_map/ppermute | solution.py:938
  313.3 20.4 %collective-permute-start.5 = (bf16[192,1152]{1,0:T(8,128)(2,1)}, bf16[192,1152]{1,0:T(8,128)(2,1)S(1)}, u32[]{:S(2)}, u32[]{:S(2)}) collective-permute-start(bf16[192,1152]{1,0:T(8,128)(2,1)} %get-tuple-element.142), channel_id=1, source_target_pairs={{0,1},{1,0},{2,3},{3,2},{4,5},{5,4},{6,7},{7,6},{8,9},{9,8},{10,11... | collective-permute-start | bytes 1327112 | tf_op jit(solution)/shard_map/ppermute | solution.py:938
  313.7 21.8 %collective-permute-start.6 = (bf16[192,1152]{1,0:T(8,128)(2,1)}, bf16[192,1152]{1,0:T(8,128)(2,1)S(1)}, u32[]{:S(2)}, u32[]{:S(2)}) collective-permute-start(bf16[192,1152]{1,0:T(8,128)(2,1)} %get-tuple-element.143), channel_id=1, source_target_pairs={{0,2},{1,3},{2,0},{3,1},{4,6},{5,7},{6,4},{7,5},{8,10},{9,11},{10,... | collective-permute-start | bytes 1327112 | tf_op jit(solution)/shard_map/ppermute | solution.py:938
  315.3 18.3 %copy-start.7 = (bf16[192,768]{1,0:T(8,128)(2,1)S(1)}, bf16[192,768]{1,0:T(8,128)(2,1)}, u32[]{:S(2)}) copy-start(bf16[192,768]{1,0:T(8,128)(2,1)} %get-tuple-element.137) | copy-start | bytes 884740
  315.3 29.3 %collective-permute-start.7 = (bf16[192,1152]{1,0:T(8,128)(2,1)}, bf16[192,1152]{1,0:T(8,128)(2,1)S(1)}, u32[]{:S(2)}, u32[]{:S(2)}) collective-permute-start(bf16[192,1152]{1,0:T(8,128)(2,1)} %get-tuple-element.144), channel_id=1, source_target_pairs={{0,3},{1,2},{2,1},{3,0},{4,7},{5,6},{6,5},{7,4},{8,11},{9,10},{10,... | collective-permute-start | bytes 1327112 | tf_op jit(solution)/shard_map/ppermute | solution.py:938
  333.6 11.0 %copy-start.6 = (bf16[192,1152]{1,0:T(8,128)(2,1)S(1)}, bf16[192,1152]{1,0:T(8,128)(2,1)}, u32[]{:S(2)}) copy-start(bf16[192,1152]{1,0:T(8,128)(2,1)} %get-tuple-element.141) | copy-start | bytes 1327108
  345.7 1.0 copy-start.26
  345.7 1.3 copy-start.25
  345.7 2.5 copy-start.11
  345.8 2.5 copy-start.19
  345.8 2.6 copy-start.9
  345.8 2.6 copy-start.10
  345.8 22.1 %collective-permute-start.13 = (bf16[192,1152]{1,0:T(8,128)(2,1)}, bf16[192,1152]{1,0:T(8,128)(2,1)S(1)}, u32[]{:S(2)}, u32[]{:S(2)}) collective-permute-start(bf16[192,1152]{1,0:T(8,128)(2,1)} %get-tuple-element.154), channel_id=1, source_target_pairs={{0,1},{1,0},{2,3},{3,2},{4,5},{5,4},{6,7},{7,6},{8,9},{9,8},{10,11... | collective-permute-start | bytes 1327112 | tf_op jit(solution)/shard_map/ppermute | solution.py:938
  346.8 21.1 %collective-permute-start.14 = (bf16[192,1152]{1,0:T(8,128)(2,1)S(1)}, bf16[192,1152]{1,0:T(8,128)(2,1)S(1)}, u32[]{:S(2)}, u32[]{:S(2)}) collective-permute-start(bf16[192,1152]{1,0:T(8,128)(2,1)S(1)} %copy-done.26), channel_id=1, source_target_pairs={{0,2},{1,3},{2,0},{3,1},{4,6},{5,7},{6,4},{7,5},{8,10},{9,11},{10,... | collective-permute-start | bytes 1327112 | tf_op jit(solution)/shard_map/ppermute | solution.py:938
  347.1 21.2 %collective-permute-start.15 = (bf16[192,1152]{1,0:T(8,128)(2,1)S(1)}, bf16[192,1152]{1,0:T(8,128)(2,1)S(1)}, u32[]{:S(2)}, u32[]{:S(2)}) collective-permute-start(bf16[192,1152]{1,0:T(8,128)(2,1)S(1)} %copy-done.25), channel_id=1, source_target_pairs={{0,3},{1,2},{2,1},{3,0},{4,7},{5,6},{6,5},{7,4},{8,11},{9,10},{10,... | collective-permute-start | bytes 1327112 | tf_op jit(solution)/shard_map/ppermute | solution.py:938
  348.4 25.5 %all-to-all-start.6 = ((bf16[8,24,1920]{2,1,0:T(8,128)(2,1)}), bf16[8,24,1920]{2,1,0:T(8,128)(2,1)S(1)}, u32[]{:S(2)}, u32[]{:S(2)}) async-start(bf16[8,24,1920]{2,1,0:T(8,128)(2,1)} %bitcast.18), calls=%async_computation.6 | async-start | bytes 1474560 | tf_op jit(solution)/shard_map/all_to_all | solution.py:929
  353.9 11.6 %copy-start.8 = (f32[8,768]{1,0:T(8,128)S(1)}, f32[8,768]{1,0:T(8,128)}, u32[]{:S(2)}) copy-start(f32[8,768]{1,0:T(8,128)} %get-tuple-element.151) | copy-start | bytes 73732
  353.9 14.3 %copy-start.5 = (bf16[192,1152]{1,0:T(8,128)(2,1)S(1)}, bf16[192,1152]{1,0:T(8,128)(2,1)}, u32[]{:S(2)}) copy-start(bf16[192,1152]{1,0:T(8,128)(2,1)} %get-tuple-element.153) | copy-start | bytes 1327108
  365.5 1.3 collective-permute-start.8
  366.8 5.7 %collective-permute-start.9 = (f32[16,768]{1,0:T(8,128)S(1)}, f32[16,768]{1,0:T(8,128)S(1)}, u32[]{:S(2)}, u32[]{:S(2)}) collective-permute-start(f32[16,768]{1,0:T(8,128)S(1)} %add.78), channel_id=1, source_target_pairs={{0,2},{1,3},{2,0},{3,1},{4,6},{5,7},{6,4},{7,5},{8,10},{9,11},{10,... | collective-permute-start | bytes 147464 | tf_op jit(solution)/shard_map/ppermute | solution.py:938
  374.0 20.3 %all-to-all-start.7 = ((bf16[8,24,1152]{2,1,0:T(8,128)(2,1)}), bf16[8,24,1152]{2,1,0:T(8,128)(2,1)S(1)}, u32[]{:S(2)}, u32[]{:S(2)}) async-start(bf16[8,24,1152]{2,1,0:T(8,128)(2,1)} %bitcast.19), calls=%async_computation.7 | async-start | bytes 884736 | tf_op jit(solution)/shard_map/all_to_all | solution.py:929
  378.3 6.7 %collective-permute-start.10 = (f32[16,768]{1,0:T(8,128)S(1)}, f32[16,768]{1,0:T(8,128)S(1)}, u32[]{:S(2)}, u32[]{:S(2)}) collective-permute-start(f32[16,768]{1,0:T(8,128)S(1)} %add.79), channel_id=1, source_target_pairs={{0,4},{4,0},{8,12},{12,8},{16,20},{20,16},{24,28},{28,24},{1,5},{5... | collective-permute-start | bytes 147464 | tf_op jit(solution)/shard_map/ppermute | solution.py:938
  385.0 4.3 collective-permute-start.11
  389.2 5.0 %collective-permute-start.12 = (f32[16,768]{1,0:T(8,128)S(1)}, f32[16,768]{1,0:T(8,128)S(1)}, u32[]{:S(2)}, u32[]{:S(2)}) collective-permute-start(f32[16,768]{1,0:T(8,128)S(1)} %add.81), channel_id=1, source_target_pairs={{0,16},{4,20},{8,24},{12,28},{16,0},{20,4},{24,8},{28,12},{1,17},{... | collective-permute-start | bytes 147464 | tf_op jit(solution)/shard_map/ppermute | solution.py:938
  395.3 21.8 %all-to-all-start.8 = ((bf16[8,24,1920]{2,1,0:T(8,128)(2,1)}), bf16[8,24,1920]{2,1,0:T(8,128)(2,1)S(1)}, u32[]{:S(2)}, u32[]{:S(2)}) async-start(bf16[8,24,1920]{2,1,0:T(8,128)(2,1)} %broadcast_in_dim.8), calls=%async_computation.8 | async-start | bytes 1474560 | tf_op jit(solution)/shard_map/all_to_all | solution.py:929
  417.1 12.5 %collective-permute-start.18 = (bf16[192,1920]{1,0:T(8,128)(2,1)S(1)}, bf16[192,1920]{1,0:T(8,128)(2,1)S(1)}, u32[]{:S(2)}, u32[]{:S(2)}) collective-permute-start(bf16[192,1920]{1,0:T(8,128)(2,1)S(1)} %bitcast.47), channel_id=1, source_target_pairs={{0,2},{1,3},{2,0},{3,1},{4,6},{5,7},{6,4},{7,5},{8,10},{9,11},{10,... | collective-permute-start | bytes 2211848 | tf_op jit(solution)/shard_map/ppermute | solution.py:938
  422.6 15.0 %all-to-all-start.9 = ((bf16[8,24,1152]{2,1,0:T(8,128)(2,1)}), bf16[8,24,1152]{2,1,0:T(8,128)(2,1)S(1)}, u32[]{:S(2)}, u32[]{:S(2)}) async-start(bf16[8,24,1152]{2,1,0:T(8,128)(2,1)} %broadcast_in_dim.9), calls=%async_computation.11 | async-start | bytes 884736 | tf_op jit(solution)/shard_map/all_to_all | solution.py:929
  426.2 12.7 %copy-start.23 = (f32[8]{0:T(128)S(1)}, f32[8]{0:T(128)}, u32[]{:S(2)}) copy-start(f32[8]{0:T(128)} %get-tuple-element.183) | copy-start | bytes 100
  430.0 16.4 %copy-start.3 = (bf16[384,1920]{1,0:T(8,128)(2,1)}, bf16[384,1920]{1,0:T(8,128)(2,1)S(1)}, u32[]{:S(2)}) copy-start(bf16[384,1920]{1,0:T(8,128)(2,1)S(1)} %maximum_select_fusion.own_ref) | copy-start | bytes 4423684
  430.0 16.4 %collective-permute-start.19 = (bf16[384,1920]{1,0:T(8,128)(2,1)S(1)}, bf16[384,1920]{1,0:T(8,128)(2,1)}, u32[]{:S(2)}, u32[]{:S(2)}) collective-permute-start(bf16[384,1920]{1,0:T(8,128)(2,1)S(1)} %maximum_select_fusion.own_ref), channel_id=1, source_target_pairs={{0,1},{1,0},{2,3},{3,2},{4,5},{5,4},{6,7},{7,6},{8,9},{9,8},{10,11... | collective-permute-start | bytes 4423688 | tf_op jit(solution)/shard_map/ppermute | solution.py:938
  437.7 8.3 %collective-permute-start.16 = (bf16[192,1152]{1,0:T(8,128)(2,1)S(1)}, bf16[192,1152]{1,0:T(8,128)(2,1)S(1)}, u32[]{:S(2)}, u32[]{:S(2)}) collective-permute-start(bf16[192,1152]{1,0:T(8,128)(2,1)S(1)} %bitcast.49), channel_id=1, source_target_pairs={{0,2},{1,3},{2,0},{3,1},{4,6},{5,7},{6,4},{7,5},{8,10},{9,11},{10,... | collective-permute-start | bytes 1327112 | tf_op jit(solution)/shard_map/ppermute | solution.py:938
  446.3 6.0 %copy-start.4 = (bf16[384,1152]{1,0:T(8,128)(2,1)}, bf16[384,1152]{1,0:T(8,128)(2,1)S(1)}, u32[]{:S(2)}) copy-start(bf16[384,1152]{1,0:T(8,128)(2,1)S(1)} %maximum_select_fusion.1.own_ref) | copy-start | bytes 2654212
  446.3 5.9 %collective-permute-start.17 = (bf16[384,1152]{1,0:T(8,128)(2,1)S(1)}, bf16[384,1152]{1,0:T(8,128)(2,1)S(1)}, u32[]{:S(2)}, u32[]{:S(2)}) collective-permute-start(bf16[384,1152]{1,0:T(8,128)(2,1)S(1)} %maximum_select_fusion.1.own_ref), channel_id=1, source_target_pairs={{0,1},{1,0},{2,3},{3,2},{4,5},{5,4},{6,7},{7,6},{8,9},{9,8},{10,11... | collective-permute-start | bytes 2654216 | tf_op jit(solution)/shard_map/ppermute | solution.py:938
  452.2 0.9 copy-start.24
Sparse Core Ops, SparseCore 0:
  9.6 40.1 all-gather.4
  51.3 37.4 all-gather.6
  267.7 63.3 reduce-scatter.2
  345.9 50.5 reduce-scatter.4

commit v5 on v4

--- a/solution.py
+++ b/solution.py
@@ -277,17 +277,21 @@
         spread = jnp.where(lanes == lax.broadcasted_iota(jnp.int32, (experts, 128), 0), passed, 0.0)
         count_row[0:1, 0:128] = jnp.sum(spread, axis=0, keepdims=True)
 
-    chosen = one_hot_rows(slots_ref[...], step * capacity, capacity)
-    out_ref[0, :capacity, :] = mm(chosen, grad_ref[...]).astype(BF16)
-    out_ref[0, capacity:, :] = count_row[...].astype(BF16)
+    group = out_ref.shape[0]
+    chosen = one_hot_rows(slots_ref[...], step * group * capacity, group * capacity)
+    dealt = mm(chosen, grad_ref[...]).astype(BF16)
+    for index in range(group):
+        out_ref[index, :capacity, :] = dealt[index * capacity : (index + 1) * capacity]
+        out_ref[index, capacity:, :] = count_row[...].astype(BF16)
 
 
 def route(routes, grad_out, experts, capacity):
     rows, width = grad_out.shape
     whole = lambda e: (0, 0)
+    group = 2
     return pl.pallas_call(
         functools.partial(route_kernel, experts, capacity),
-        grid=(experts,),
+        grid=(experts // group,),
         in_specs=[
             pl.BlockSpec((1, rows), whole),
             pl.BlockSpec((rows, width), whole),
@@ -295,7 +299,7 @@
         out_specs=[
             pl.BlockSpec((1, rows), whole),
             pl.BlockSpec((rows, 2), whole),
-            pl.BlockSpec((1, capacity + EXTRA, width), lambda e: (e, 0, 0)),
+            pl.BlockSpec((group, capacity + EXTRA, width), lambda e: (e, 0, 0)),
         ],
         out_shape=[
             jax.ShapeDtypeStruct((1, rows), jnp.int32),
@@ -1053,7 +1057,8 @@
     x0 = swap(after(first, grad_rows), "wide")
     counted = jnp.sum(grad_rows[:, capacity, :experts].astype(F32), axis=0)
     fraction = axis_sum(counted, "narrow") / total_tokens
-    x1 = swap(after(second, x0, fraction), "wide")
+    pull = (BALANCE * experts * fraction).reshape(experts, 1)
+    x1 = swap(after(second, x0, pull), "wide")
     act, up, out, back0, dots = expert(
         x0, grad_rows, gathered_in, gathered_bias, gathered_down, bias_down, 0
     )
@@ -1072,7 +1077,6 @@
     extras = jnp.transpose(back1[:, half:, :half], (1, 0, 2))
     dots1 = jnp.pad(extras, ((0, 0), (0, 0), (0, EXTRA))).reshape(EXTRA, experts * (half + EXTRA))
     dots0 = jnp.concatenate([extras[3:], extras[:3]], axis=0).reshape(EXTRA, experts * half)
-    pull = (BALANCE * experts * fraction).reshape(experts, 1)
     hid_grad, con_grad, sums, router_grad, prob_sums, *out_grad = combine(
         weight,
         place,

time: 467 us -> 479 us (1.026)
  starting transfers between devices: 65.9 us -> 75 us
    all_to_all x10, starting transfers between devices: 49.1 us -> 58.3 us  [swap(): return lax.all_to_all(blocks, axis, split_axis=0, concat_axis=0, tiled=True)]
  transfers between devices with their start and end apart: 34 -> 34, of which waited for: 20 -> 20; matrix products, arithmetic and copies ran while one was open for 4% -> 3% of each run, Pallas kernels for 51% -> 50%
where the time goes in v5:
time: 479 us; the launch traced here: 474 us
  Pallas kernels  239 us (50%)
  waiting for transfers between devices  118 us (25%)
  starting transfers between devices  75 us (16%)
  between operations  16.4 us (3%)
  local copies, waits for them, and re-layouts  12.7 us (3%)
  other arithmetic  6.71 us (1%)
  blocking collectives  5.61 us (1%)
    all_to_all x10, waiting for transfers between devices, swap(): return lax.all_to_all(blocks, axis, split_axis=0, concat_axis=0, tiled=True)  80.3 us
    pallas_call x2, Pallas kernels, expert(): pl.pallas_call(functools.partial(expert_kernel, parts, chunk), grid=(part...  66.1 us
    all_to_all x10, starting transfers between devices, swap(): return lax.all_to_all(blocks, axis, split_axis=0, concat_axis=0, tiled=True)  58.3 us
    ppermute x20, waiting for transfers between devices, trade(): lax.ppermute(value, axis, [(place, place ^ bit) for place in range(count)])  36.4 us
    pallas_call x2, Pallas kernels, attend_back(): pl.pallas_call(functools.partial(attend_back_kernel, block, shares), grid...  36.2 us
    pallas_call x1, Pallas kernels, weight_grads(): pl.pallas_call(functools.partial(weight_kernel, parts), grid=(parts, 2),...  33.6 us
    pallas_call x1, Pallas kernels, attend(): pl.pallas_call(functools.partial(attend_kernel, block), grid=(pairs,), in...  20.6 us
    pallas_call x1, Pallas kernels, combine(): pl.pallas_call(functools.partial(combine_kernel, shares), grid=(rows // t...  19.2 us
  transfers between devices with their start and end apart: 34, of which 20 were waited for; matrix products, arithmetic and copies ran while one was open for 3% of the time, Pallas kernels for 50%

profile of v5, /device:TPU:0, one launch (start us, length us, event | category | flops | bytes accessed | tf_op | source)
XLA Modules:
  0.0 473.7 jit_solution(12398294163669481265)
XLA Ops:
  7.9 6.8 %route.1 = (s32[1,1024]{1,0:T(1,128)}, s32[1024,2]{1,0:T(8,128)}, bf16[8,264,768]{2,1,0:T(8,128)(2,1)}) custom-call(s32[1,1024]{1,0:T(1,128)} %bitcast.54, bf16[1024,768]{1,0:T(8,128)(2,1)} %grad_ref.3), custom_call_target="tpu_custom_call" | custom-call | flops 3221225472 | bytes 4718592 | tf_op jit(solution)/shard_map/route/pallas_call | solution.py:292
  14.8 7.4 %all-to-all-start = ((bf16[8,264,768]{2,1,0:T(8,128)(2,1)}), bf16[8,264,768]{2,1,0:T(8,128)(2,1)S(1)}, u32[]{:S(2)}, u32[]{:S(2)}) async-start(bf16[8,264,768]{2,1,0:T(8,128)(2,1)} %get-tuple-element.106), calls=%async_computation | async-start | bytes 6488064 | tf_op jit(solution)/shard_map/all_to_all | solution.py:933
  27.9 8.2 %project.1 = (bf16[768,1024]{1,0:T(8,128)(2,1)}, bf16[1024,768]{1,0:T(8,128)(2,1)}, bf16[1024,768]{1,0:T(8,128)(2,1)}, bf16[1024,768]{1,0:T(8,128)(2,1)}) custom-call(bf16[1024,768]{1,0:T(8,128)(2,1)} %refs_6_.1, f32[1,768]{1,0:T(1,128)} %reshape.148.gain_ref.refs_8_, f32[1,768]{1,0:T(1,128)} %reshape.149.shift_ref, bf16[768,768]{1,0:T(8,128)(2,1)} %refs_9_.1, ...), custom_call_target="tpu_custom_call" | custom-call | flops 3623878656 | bytes 11403264 | tf_op jit(solution)/shard_map/project/pallas_call | solution.py:331
  36.1 20.6 %attend.1 = (bf16[1024,768]{1,0:T(8,128)(2,1)}, bf16[6,2,2560,256]{3,2,1,0:T(8,128)(2,1)}) custom-call(bf16[1024,768]{1,0:T(8,128)(2,1)} %get-tuple-element.98.q_ref, bf16[1024,768]{1,0:T(8,128)(2,1)} %get-tuple-element.99.k_ref, bf16[1024,768]{1,0:T(8,128)(2,1)} %get-tuple-element.100.v_ref), custom_call_target="tpu_custom_call" | custom-call | flops 6442450944 | bytes 6291456 | tf_op jit(solution)/shard_map/attend/pallas_call | solution.py:87
  56.7 7.2 %settle.1 = (f32[1024,768]{1,0:T(8,128)}, bf16[1024,768]{1,0:T(8,128)(2,1)}, f32[8,1024]{1,0:T(8,128)}) custom-call(bf16[1024,768]{1,0:T(8,128)(2,1)} %get-tuple-element.101.context_ref, bf16[1024,768]{1,0:T(8,128)(2,1)} %refs_6_.1, bf16[768,768]{1,0:T(8,128)(2,1)} %w_out_ref.3, f32[1,768]{1,0:T(1,128)} %reshape.152.bias_ref, f32[1,768]{1,0:T(1,128)} %reshape.153.gain_ref, ...), custom_call_target="tpu_custom_call" | custom-call | flops 1207959552 | bytes 9043968 | tf_op jit(solution)/shard_map/settle/pallas_call | solution.py:359
  63.9 8.5 %dispatch.1 = (bf16[8,128,768]{2,1,0:T(8,128)(2,1)}, bf16[8,136,768]{2,1,0:T(8,128)(2,1)}) custom-call(f32[1,1]{1,0:T(1,128)} %bitcast.2.weight_ref, s32[1,1024]{1,0:T(1,128)} %get-tuple-element.97.slots_ref, s32[1,1024]{1,0:T(1,128)} %bitcast.55, f32[8,1024]{1,0:T(8,128)} %get-tuple-element.102.logits_ref, bf16[1024,768]{1,0:T(8,128)(2,1)} %get-tuple-element.103.moe_ref), custom_call_target="tpu_custom_call" | custom-call | flops 3221225472 | bytes 4718592 | tf_op jit(solution)/shard_map/dispatch/pallas_call | solution.py:406
  72.4 22.6 %all-to-all-done.refs_1_.g_ref = bf16[8,264,768]{2,1,0:T(8,128)(2,1)S(1)} async-done(((bf16[8,264,768]{2,1,0:T(8,128)(2,1)}), bf16[8,264,768]{2,1,0:T(8,128)(2,1)S(1)}, u32[]{:S(2)}, u32[]{:S(2)}) %all-to-all-start) | async-done | bytes 3244064 | tf_op jit(solution)/shard_map/all_to_all | solution.py:933
  95.0 4.3 all-to-all-start.1
  99.4 1.1 collective-permute-done
  100.6 1.5 collective-permute-start.1
  102.1 2.0 collective-permute-done.1
  104.6 31.4 %all-to-all-done.1.refs_0_.x0_ref = bf16[8,128,768]{2,1,0:T(8,128)(2,1)} async-done(((bf16[8,128,768]{2,1,0:T(8,128)(2,1)}), bf16[8,128,768]{2,1,0:T(8,128)(2,1)}, u32[]{:S(2)}, u32[]{:S(2)}) %all-to-all-start.1) | async-done | bytes 1572896 | tf_op jit(solution)/shard_map/all_to_all | solution.py:933
  136.0 4.4 all-to-all-start.2
  140.4 5.6 %all-gather.1.refs_3_ = bf16[4,1,768]{2,1,0:T(2,128)(2,1)} all-gather(bf16[1,1,768]{2,1,0:T(2,128)(2,1)S(1)} %bitcast.58), channel_id=2, replica_groups=mesh['wide'=8,'narrow'=4] {'narrow'}, dimensions={0}, use_global_device_ids=true | all-gather | bytes 7680 | tf_op jit(solution)/shard_map/all_gather | solution.py:1056
  146.1 33.0 %expert.2 = (bf16[4,2,1024,768]{3,2,1,0:T(8,128)(2,1)}, bf16[4,2,1024,768]{3,2,1,0:T(8,128)(2,1)}, bf16[8,256,768]{2,1,0:T(8,128)(2,1)}, bf16[8,128,768]{2,1,0:T(8,128)(2,1)}, bf16[8,8,128]{2,1,0:T(8,128)(2,1)}) custom-call(bf16[8,128,768]{2,1,0:T(8,128)(2,1)} %all-to-all-done.1.refs_0_.x0_ref, bf16[8,264,768]{2,1,0:T(8,128)(2,1)} %copy-done.2, ...), custom_call_target="tpu_custom_call" | custom-call | flops 14495514624 | bytes 12582912 | tf_op jit(solution)/shard_map/expert/pallas_call | solution.py:519
  179.2 5.8 %all-to-all-start.3 = ((bf16[8,128,768]{2,1,0:T(8,128)(2,1)}), bf16[8,128,768]{2,1,0:T(8,128)(2,1)S(1)}, u32[]{:S(2)}, u32[]{:S(2)}) async-start(bf16[8,128,768]{2,1,0:T(8,128)(2,1)} %get-tuple-element.117), calls=%async_computation.3 | async-start | bytes 3145728 | tf_op jit(solution)/shard_map/all_to_all | solution.py:933
  184.9 33.2 %expert.3 = (bf16[4,2,1024,768]{3,2,1,0:T(8,128)(2,1)}, bf16[4,2,1024,768]{3,2,1,0:T(8,128)(2,1)}, bf16[8,256,768]{2,1,0:T(8,128)(2,1)}, bf16[8,136,768]{2,1,0:T(8,128)(2,1)}) custom-call(bf16[8,136,768]{2,1,0:T(8,128)(2,1)} %all-to-all-done.2.refs_0_.x1_ref, ...), custom_call_target="tpu_custom_call", output_to_operand_aliasing={{0}: (6, {}), {1}: (7, {}), {2}: (8, {})} | custom-call | flops 14495514624 | bytes 12582912 | tf_op jit(solution)/shard_map/expert/pallas_call | solution.py:519
  218.1 4.4 all-to-all-done.3
  222.4 1.1 copy-done.1
  223.6 12.9 %all-to-all-start.4 = ((bf16[8,136,768]{2,1,0:T(8,128)(2,1)}), bf16[8,136,768]{2,1,0:T(8,128)(2,1)S(1)}, u32[]{:S(2)}, u32[]{:S(2)}) async-start(bf16[8,136,768]{2,1,0:T(8,128)(2,1)} %get-tuple-element.118), calls=%async_computation.4 | async-start | bytes 3342336 | tf_op jit(solution)/shard_map/all_to_all | solution.py:933
  236.5 1.4 convert_reduce_fusion
  237.9 33.6 %weight_grads.1 = (bf16[4,776,768]{2,1,0:T(8,128)(2,1)}, bf16[4,768,768]{2,1,0:T(8,128)(2,1)}) custom-call(bf16[8,128,768]{2,1,0:T(8,128)(2,1)} %all-to-all-done.1.refs_0_.x0_ref, bf16[8,136,768]{2,1,0:T(8,128)(2,1)} %all-to-all-done.2.refs_0_.x1_ref, bf16[8,264,768]{2,1,0:T(8,128)(2,1)} %copy-done.2, bf16[4,2,1024,768]{3,2,1,0:T(8,128)(2,1)} %get-tuple-element.124.act_ref, ...), custom_call_target="tpu_custom_call" | custom-call | flops 28991029248 | bytes 25165824 | tf_op jit(solution)/shard_map/weight_grads/pallas_call | solution.py:614
  271.5 4.3 all-to-all-done.4
  275.8 4.5 all-to-all-start.5
  281.1 0.7 reshape.163.dots1_ref
  282.4 19.2 %combine.1 = (f32[1024,768]{1,0:T(8,128)}, bf16[1024,768]{1,0:T(8,128)(2,1)}, f32[8,768]{1,0:T(8,128)}, f32[8,768]{1,0:T(8,128)}, f32[8,1]{1,0:T(8,128)}, /*inde...) custom-call(f32[1,1]{1,0:T(1,128)} %bitcast.2.weight_ref, ...), custom_call_target="tpu_custom_call" | custom-call | flops 1024 | bytes 1024 | tf_op jit(solution)/shard_map/combine/pallas_call | solution.py:724
  301.7 1.7 collective-permute-start.3
  303.5 18.0 %attend_back.2 = (bf16[1024,384]{1,0:T(8,128)(2,1)}, bf16[1024,384]{1,0:T(8,128)(2,1)}, bf16[1024,384]{1,0:T(8,128)(2,1)}, f32[8,384]{1,0:T(8,128)}, bf16[192,11...) custom-call(s32[1,1]{1,0:T(1,128)} %bitcast.8.place_ref, ...), custom_call_target="tpu_custom_call" | custom-call | flops 1024 | bytes 1024 | tf_op jit(solution)/shard_map/attend_back/pallas_call | solution.py:162
  321.9 1.7 collective-permute-start.6
  323.6 18.2 %attend_back.3 = (bf16[1024,384]{1,0:T(8,128)(2,1)}, bf16[1024,384]{1,0:T(8,128)(2,1)}, bf16[1024,384]{1,0:T(8,128)(2,1)}, f32[8,384]{1,0:T(8,128)}, bf16[192,11...) custom-call(s32[1,1]{1,0:T(1,128)} %bitcast.8.place_ref, ...), custom_call_target="tpu_custom_call" | custom-call | flops 1024 | bytes 1024 | tf_op jit(solution)/shard_map/attend_back/pallas_call | solution.py:162
  342.0 1.7 collective-permute-done.6
  343.7 9.1 %collective-permute-done.7 = bf16[192,1152]{1,0:T(8,128)(2,1)S(1)} collective-permute-done((bf16[192,1152]{1,0:T(8,128)(2,1)}, bf16[192,1152]{1,0:T(8,128)(2,1)S(1)}, u32[]{:S(2)}, u32[]{:S(2)}) %collective-permute-start.7) | collective-permute-done | bytes 442400 | tf_op jit(solution)/shard_map/ppermute | solution.py:942
  353.0 0.9 pad_maximum_fusion
  354.2 0.8 copy-done.29
  355.3 1.1 collective-permute-start.15
  356.6 5.5 %all-to-all-start.6 = ((bf16[8,24,1920]{2,1,0:T(8,128)(2,1)}), bf16[8,24,1920]{2,1,0:T(8,128)(2,1)S(1)}, u32[]{:S(2)}, u32[]{:S(2)}) async-start(bf16[8,24,1920]{2,1,0:T(8,128)(2,1)} %bitcast.18), calls=%async_computation.6 | async-start | bytes 1474560 | tf_op jit(solution)/shard_map/all_to_all | solution.py:933
  362.2 10.8 %close.1 = (bf16[1024,768]{1,0:T(8,128)(2,1)}, f32[8,768]{1,0:T(8,128)}) custom-call(bf16[1024,384]{1,0:T(8,128)(2,1)} %get-tuple-element.130.refs_0_, bf16[1024,384]{1,0:T(8,128)(2,1)} %get-tuple-element.131.refs_1_, bf16[1024,384]{1,0:T(8,128)(2,1)} %get-tuple-element.132.refs_2_, bf16[1024,384]{1,0:T(8,128)(2,1)} %get-tuple-element.133.refs_3_, ...), custom_call_target="tpu_custom_call" | custom-call | flops 40000000000 | bytes 4096 | tf_op jit(solution)/shard_map/close/pallas_call | solution.py:807
  373.0 0.8 slice.56
  374.1 0.9 collective-permute-done.8
  375.1 1.1 collective-permute-start.9
  376.5 1.0 add_convert_fusion
  377.5 3.3 collective-permute-done.9
  380.8 1.4 all-to-all-done.6
  382.3 4.3 all-to-all-start.7
  386.6 2.0 collective-permute-start.10
  388.6 4.6 collective-permute-done.10
  393.2 2.1 collective-permute-start.11
  395.3 2.2 collective-permute-done.11
  397.5 1.8 collective-permute-start.12
  399.3 3.2 collective-permute-done.12
  402.6 0.9 broadcast_in_dim.8
  403.5 5.6 %all-to-all-start.8 = ((bf16[8,24,1920]{2,1,0:T(8,128)(2,1)}), bf16[8,24,1920]{2,1,0:T(8,128)(2,1)S(1)}, u32[]{:S(2)}, u32[]{:S(2)}) async-start(bf16[8,24,1920]{2,1,0:T(8,128)(2,1)} %broadcast_in_dim.8), calls=%async_computation.8 | async-start | bytes 1474560 | tf_op jit(solution)/shard_map/all_to_all | solution.py:933
  409.1 7.7 %block_output.1 = bf16[1024,768]{1,0:T(8,128)(2,1)} custom-call(bf16[2048,768]{1,0:T(8,128)(2,1)} %bitcast.7.back_ref, s32[1024,2]{1,0:T(8,128)} %get-tuple-element.120.columns_ref, s32[1,1024]{1,0:T(1,128)} %bitcast.57, f32[8,1024]{1,0:T(8,128)} %get-tuple-element.102.logits_ref, f32[1024,768]{1,0:T(8,128)} %get-tuple-element.121.hidden_ref), custom_call_target="tpu_custom_call" | custom-call | flops 40000000000 | bytes 4096 | tf_op jit(solution)/shard_map/block_output/pallas_call | solution.py:835
  416.8 8.5 %all-to-all-done.8 = bf16[8,24,1920]{2,1,0:T(8,128)(2,1)S(1)} async-done(((bf16[8,24,1920]{2,1,0:T(8,128)(2,1)}), bf16[8,24,1920]{2,1,0:T(8,128)(2,1)S(1)}, u32[]{:S(2)}, u32[]{:S(2)}) %all-to-all-start.8) | async-done | bytes 737312 | tf_op jit(solution)/shard_map/all_to_all | solution.py:933
  425.9 4.1 unpack_expert.1
  430.0 0.8 broadcast_in_dim.9
  430.8 3.6 all-to-all-start.9
  434.4 3.3 collective-permute-done.18
  438.3 7.6 %all-to-all-done.9 = bf16[8,24,1152]{2,1,0:T(8,128)(2,1)S(1)} async-done(((bf16[8,24,1152]{2,1,0:T(8,128)(2,1)}), bf16[8,24,1152]{2,1,0:T(8,128)(2,1)S(1)}, u32[]{:S(2)}, u32[]{:S(2)}) %all-to-all-start.9) | async-done | bytes 442400 | tf_op jit(solution)/shard_map/all_to_all | solution.py:933
  445.9 1.2 collective-permute-start.16
  449.6 4.5 collective-permute-done.16
  454.5 5.8 %unpack.2 = (f32[768,768]{1,0:T(8,128)}, f32[768,768]{1,0:T(8,128)}, f32[768,768]{1,0:T(8,128)}, f32[768,768]{1,0:T(8,128)}) custom-call(s32[1,1]{1,0:T(1,128)} %bitcast.17.upper_ref, bf16[384,1920]{1,0:T(8,128)(2,1)} %copy-done.3, bf16[384,1920]{1,0:T(8,128)(2,1)} %collective-permute-done.19.other_ref), custom_call_target="tpu_custom_call" | custom-call | flops 40000000000 | bytes 4096 | tf_op jit(solution)/shard_map/unpack/pallas_call | solution.py:917
  460.4 0.9 copy-done.27
  461.3 4.3 unpack.3
  (130 shorter events, 14.5 us)
Async XLA Ops:
  7.2 138.9 %all-gather.5.cloned.1.call-start = ((), (), s32[]{:S(2)}) async-start(), calls=%async_computation.12 | async-start | bytes 5898240 | tf_op jit(solution)/shard_map/all_gather | solution.py:1045
  14.7 8.3 %copy-start.12 = (f32[768]{0:T(1024)S(1)}, f32[768]{0:T(1024)}, u32[]{:S(2)}) copy-start(f32[768]{0:T(1024)} %param.26) | copy-start | bytes 9220
  14.7 8.9 %copy-start.13 = (f32[768]{0:T(1024)S(1)}, f32[768]{0:T(1024)}, u32[]{:S(2)}) copy-start(f32[768]{0:T(1024)} %param.27) | copy-start | bytes 9220
  14.7 9.4 %copy-start.14 = (f32[768]{0:T(1024)S(1)}, f32[768]{0:T(1024)}, u32[]{:S(2)}) copy-start(f32[768]{0:T(1024)} %param.29) | copy-start | bytes 9220
  14.7 10.0 %copy-start.15 = (f32[768]{0:T(1024)S(1)}, f32[768]{0:T(1024)}, u32[]{:S(2)}) copy-start(f32[768]{0:T(1024)} %param.32) | copy-start | bytes 9220
  14.7 10.6 %copy-start.16 = (f32[768]{0:T(1024)S(1)}, f32[768]{0:T(1024)}, u32[]{:S(2)}) copy-start(f32[768]{0:T(1024)} %param.35) | copy-start | bytes 9220
  14.7 11.2 %copy-start.17 = (f32[768]{0:T(1024)S(1)}, f32[768]{0:T(1024)}, u32[]{:S(2)}) copy-start(f32[768]{0:T(1024)} %param.34) | copy-start | bytes 9220
  14.8 11.7 %copy-start.18 = (f32[768]{0:T(1024)S(1)}, f32[768]{0:T(1024)}, u32[]{:S(2)}) copy-start(f32[768]{0:T(1024)} %param.36) | copy-start | bytes 9220
  14.8 12.3 %copy-start.21 = (s32[8]{0:T(128)S(1)}, s32[8]{0:T(128)}, u32[]{:S(2)}) copy-start(s32[8]{0:T(128)} %param.24) | copy-start | bytes 100
  14.8 12.5 %copy-start.22 = (s32[8]{0:T(128)S(1)}, s32[8]{0:T(128)}, u32[]{:S(2)}) copy-start(s32[8]{0:T(128)} %param.25) | copy-start | bytes 100
  14.8 80.2 %all-to-all-start = ((bf16[8,264,768]{2,1,0:T(8,128)(2,1)}), bf16[8,264,768]{2,1,0:T(8,128)(2,1)S(1)}, u32[]{:S(2)}, u32[]{:S(2)}) async-start(bf16[8,264,768]{2,1,0:T(8,128)(2,1)} %get-tuple-element.106), calls=%async_computation | async-start | bytes 6488064 | tf_op jit(solution)/shard_map/all_to_all | solution.py:933
  22.2 123.8 %all-gather.7.cloned.1.call-start = ((), (), s32[]{:S(2)}) async-start(), calls=%async_computation.13 | async-start | bytes 5898240 | tf_op jit(solution)/shard_map/all_gather | solution.py:1046
  95.0 41.0 %copy-start.2 = (bf16[8,264,768]{2,1,0:T(8,128)(2,1)}, bf16[8,264,768]{2,1,0:T(8,128)(2,1)S(1)}, u32[]{:S(2)}) copy-start(bf16[8,264,768]{2,1,0:T(8,128)(2,1)S(1)} %all-to-all-done.refs_1_.g_ref) | copy-start | bytes 9732100
  95.0 40.9 %all-to-all-start.1 = ((bf16[8,128,768]{2,1,0:T(8,128)(2,1)}), bf16[8,128,768]{2,1,0:T(8,128)(2,1)}, u32[]{:S(2)}, u32[]{:S(2)}) async-start(bf16[8,128,768]{2,1,0:T(8,128)(2,1)} %get-tuple-element.107), calls=%async_computation.1 | async-start | bytes 3145728 | tf_op jit(solution)/shard_map/all_to_all | solution.py:933
  99.4 1.2 collective-permute-start
  100.6 35.4 %copy-start.23 = (f32[8]{0:T(128)}, f32[8]{0:T(128)S(1)}, u32[]{:S(2)}) copy-start(f32[8]{0:T(128)S(1)} %add.70) | copy-start | bytes 100
  100.6 3.5 collective-permute-start.1
  104.1 0.5 copy-start.25
  136.0 4.4 copy-start.20
  136.0 43.2 %all-to-all-start.2 = ((bf16[8,136,768]{2,1,0:T(8,128)(2,1)}), bf16[8,136,768]{2,1,0:T(8,128)(2,1)}, u32[]{:S(2)}, u32[]{:S(2)}) async-start(bf16[8,136,768]{2,1,0:T(8,128)(2,1)} %get-tuple-element.108), calls=%async_computation.2 | async-start | bytes 3342336 | tf_op jit(solution)/shard_map/all_to_all | solution.py:933
  179.2 43.3 %all-to-all-start.3 = ((bf16[8,128,768]{2,1,0:T(8,128)(2,1)}), bf16[8,128,768]{2,1,0:T(8,128)(2,1)S(1)}, u32[]{:S(2)}, u32[]{:S(2)}) async-start(bf16[8,128,768]{2,1,0:T(8,128)(2,1)} %get-tuple-element.117), calls=%async_computation.3 | async-start | bytes 3145728 | tf_op jit(solution)/shard_map/all_to_all | solution.py:933
  222.4 1.1 copy-start.1
  223.6 52.2 %all-to-all-start.4 = ((bf16[8,136,768]{2,1,0:T(8,128)(2,1)}), bf16[8,136,768]{2,1,0:T(8,128)(2,1)S(1)}, u32[]{:S(2)}, u32[]{:S(2)}) async-start(bf16[8,136,768]{2,1,0:T(8,128)(2,1)} %get-tuple-element.118), calls=%async_computation.4 | async-start | bytes 3342336 | tf_op jit(solution)/shard_map/all_to_all | solution.py:933
  236.5 117.5 %reduce-scatter.3.cloned.1.call-start = ((), (), s32[]{:S(2)}) async-start(), calls=%async_computation.14 | async-start | bytes 5898240 | tf_op jit(solution)/shard_map/reduce_scatter | solution.py:1073
  275.8 5.3 %copy-start = (bf16[8,136,768]{2,1,0:T(8,128)(2,1)}, bf16[8,136,768]{2,1,0:T(8,128)(2,1)S(1)}, u32[]{:S(2)}) copy-start(bf16[8,136,768]{2,1,0:T(8,128)(2,1)S(1)} %all-to-all-done.4) | copy-start | bytes 5013508
  275.8 80.8 %all-to-all-start.5 = ((bf16[8,256,768]{2,1,0:T(8,128)(2,1)}), bf16[8,256,768]{2,1,0:T(8,128)(2,1)}, u32[]{:S(2)}, u32[]{:S(2)}) async-start(bf16[8,256,768]{2,1,0:T(8,128)(2,1)} %get-tuple-element.119), calls=%async_computation.5 | async-start | bytes 6291456 | tf_op jit(solution)/shard_map/all_to_all | solution.py:933
  280.3 145.6 %reduce-scatter.5.cloned.1.call-start = ((), (), s32[]{:S(2)}) async-start(), calls=%async_computation.15 | async-start | bytes 5959680 | tf_op jit(solution)/shard_map/reduce_scatter | solution.py:1122
  301.6 22.0 %collective-permute-start.2 = (bf16[192,768]{1,0:T(8,128)(2,1)}, bf16[192,768]{1,0:T(8,128)(2,1)S(1)}, u32[]{:S(2)}, u32[]{:S(2)}) collective-permute-start(bf16[192,768]{1,0:T(8,128)(2,1)} %get-tuple-element.138), channel_id=1, source_target_pairs={{0,1},{1,0},{2,3},{3,2},{4,5},{5,4},{6,7},{7,6},{8,9},{9,8},{10,11... | collective-permute-start | bytes 884744 | tf_op jit(solution)/shard_map/ppermute | solution.py:942
  301.7 40.1 %collective-permute-start.3 = (bf16[192,768]{1,0:T(8,128)(2,1)}, bf16[192,768]{1,0:T(8,128)(2,1)S(1)}, u32[]{:S(2)}, u32[]{:S(2)}) collective-permute-start(bf16[192,768]{1,0:T(8,128)(2,1)} %get-tuple-element.139), channel_id=1, source_target_pairs={{0,2},{1,3},{2,0},{3,1},{4,6},{5,7},{6,4},{7,5},{8,10},{9,11},{10,... | collective-permute-start | bytes 884744 | tf_op jit(solution)/shard_map/ppermute | solution.py:942
  303.4 38.4 %collective-permute-start.4 = (bf16[192,768]{1,0:T(8,128)(2,1)}, bf16[192,768]{1,0:T(8,128)(2,1)S(1)}, u32[]{:S(2)}, u32[]{:S(2)}) collective-permute-start(bf16[192,768]{1,0:T(8,128)(2,1)} %get-tuple-element.140), channel_id=1, source_target_pairs={{0,3},{1,2},{2,1},{3,0},{4,7},{5,6},{6,5},{7,4},{8,11},{9,10},{10,... | collective-permute-start | bytes 884744 | tf_op jit(solution)/shard_map/ppermute | solution.py:942
  321.6 20.4 %collective-permute-start.5 = (bf16[192,1152]{1,0:T(8,128)(2,1)}, bf16[192,1152]{1,0:T(8,128)(2,1)S(1)}, u32[]{:S(2)}, u32[]{:S(2)}) collective-permute-start(bf16[192,1152]{1,0:T(8,128)(2,1)} %get-tuple-element.142), channel_id=1, source_target_pairs={{0,1},{1,0},{2,3},{3,2},{4,5},{5,4},{6,7},{7,6},{8,9},{9,8},{10,11... | collective-permute-start | bytes 1327112 | tf_op jit(solution)/shard_map/ppermute | solution.py:942
  321.9 21.7 %collective-permute-start.6 = (bf16[192,1152]{1,0:T(8,128)(2,1)}, bf16[192,1152]{1,0:T(8,128)(2,1)S(1)}, u32[]{:S(2)}, u32[]{:S(2)}) collective-permute-start(bf16[192,1152]{1,0:T(8,128)(2,1)} %get-tuple-element.143), channel_id=1, source_target_pairs={{0,2},{1,3},{2,0},{3,1},{4,6},{5,7},{6,4},{7,5},{8,10},{9,11},{10,... | collective-permute-start | bytes 1327112 | tf_op jit(solution)/shard_map/ppermute | solution.py:942
  323.6 18.2 %copy-start.7 = (bf16[192,768]{1,0:T(8,128)(2,1)S(1)}, bf16[192,768]{1,0:T(8,128)(2,1)}, u32[]{:S(2)}) copy-start(bf16[192,768]{1,0:T(8,128)(2,1)} %get-tuple-element.137) | copy-start | bytes 884740
  323.6 29.2 %collective-permute-start.7 = (bf16[192,1152]{1,0:T(8,128)(2,1)}, bf16[192,1152]{1,0:T(8,128)(2,1)S(1)}, u32[]{:S(2)}, u32[]{:S(2)}) collective-permute-start(bf16[192,1152]{1,0:T(8,128)(2,1)} %get-tuple-element.144), channel_id=1, source_target_pairs={{0,3},{1,2},{2,1},{3,0},{4,7},{5,6},{6,5},{7,4},{8,11},{9,10},{10,... | collective-permute-start | bytes 1327112 | tf_op jit(solution)/shard_map/ppermute | solution.py:942
  341.8 11.0 %copy-start.6 = (bf16[192,1152]{1,0:T(8,128)(2,1)S(1)}, bf16[192,1152]{1,0:T(8,128)(2,1)}, u32[]{:S(2)}) copy-start(bf16[192,1152]{1,0:T(8,128)(2,1)} %get-tuple-element.141) | copy-start | bytes 1327108
  354.0 1.0 copy-start.29
  354.0 1.3 copy-start.28
  354.0 2.5 copy-start.11
  354.0 2.5 copy-start.19
  354.0 2.6 copy-start.9
  354.0 2.6 copy-start.10
  354.0 22.1 %collective-permute-start.13 = (bf16[192,1152]{1,0:T(8,128)(2,1)}, bf16[192,1152]{1,0:T(8,128)(2,1)S(1)}, u32[]{:S(2)}, u32[]{:S(2)}) collective-permute-start(bf16[192,1152]{1,0:T(8,128)(2,1)} %get-tuple-element.154), channel_id=1, source_target_pairs={{0,1},{1,0},{2,3},{3,2},{4,5},{5,4},{6,7},{7,6},{8,9},{9,8},{10,11... | collective-permute-start | bytes 1327112 | tf_op jit(solution)/shard_map/ppermute | solution.py:942
  355.0 21.2 %collective-permute-start.14 = (bf16[192,1152]{1,0:T(8,128)(2,1)S(1)}, bf16[192,1152]{1,0:T(8,128)(2,1)S(1)}, u32[]{:S(2)}, u32[]{:S(2)}) collective-permute-start(bf16[192,1152]{1,0:T(8,128)(2,1)S(1)} %copy-done.29), channel_id=1, source_target_pairs={{0,2},{1,3},{2,0},{3,1},{4,6},{5,7},{6,4},{7,5},{8,10},{9,11},{10,... | collective-permute-start | bytes 1327112 | tf_op jit(solution)/shard_map/ppermute | solution.py:942
  355.3 21.2 %collective-permute-start.15 = (bf16[192,1152]{1,0:T(8,128)(2,1)S(1)}, bf16[192,1152]{1,0:T(8,128)(2,1)S(1)}, u32[]{:S(2)}, u32[]{:S(2)}) collective-permute-start(bf16[192,1152]{1,0:T(8,128)(2,1)S(1)} %copy-done.28), channel_id=1, source_target_pairs={{0,3},{1,2},{2,1},{3,0},{4,7},{5,6},{6,5},{7,4},{8,11},{9,10},{10,... | collective-permute-start | bytes 1327112 | tf_op jit(solution)/shard_map/ppermute | solution.py:942
  356.6 25.5 %all-to-all-start.6 = ((bf16[8,24,1920]{2,1,0:T(8,128)(2,1)}), bf16[8,24,1920]{2,1,0:T(8,128)(2,1)S(1)}, u32[]{:S(2)}, u32[]{:S(2)}) async-start(bf16[8,24,1920]{2,1,0:T(8,128)(2,1)} %bitcast.18), calls=%async_computation.6 | async-start | bytes 1474560 | tf_op jit(solution)/shard_map/all_to_all | solution.py:933
  362.1 11.6 %copy-start.8 = (f32[8,768]{1,0:T(8,128)S(1)}, f32[8,768]{1,0:T(8,128)}, u32[]{:S(2)}) copy-start(f32[8,768]{1,0:T(8,128)} %get-tuple-element.151) | copy-start | bytes 73732
  362.2 14.4 %copy-start.5 = (bf16[192,1152]{1,0:T(8,128)(2,1)S(1)}, bf16[192,1152]{1,0:T(8,128)(2,1)}, u32[]{:S(2)}) copy-start(bf16[192,1152]{1,0:T(8,128)(2,1)} %get-tuple-element.153) | copy-start | bytes 1327108
  373.8 1.3 collective-permute-start.8
  375.1 5.7 %collective-permute-start.9 = (f32[16,768]{1,0:T(8,128)S(1)}, f32[16,768]{1,0:T(8,128)S(1)}, u32[]{:S(2)}, u32[]{:S(2)}) collective-permute-start(f32[16,768]{1,0:T(8,128)S(1)} %add.78), channel_id=1, source_target_pairs={{0,2},{1,3},{2,0},{3,1},{4,6},{5,7},{6,4},{7,5},{8,10},{9,11},{10,... | collective-permute-start | bytes 147464 | tf_op jit(solution)/shard_map/ppermute | solution.py:942
  382.3 20.3 %all-to-all-start.7 = ((bf16[8,24,1152]{2,1,0:T(8,128)(2,1)}), bf16[8,24,1152]{2,1,0:T(8,128)(2,1)S(1)}, u32[]{:S(2)}, u32[]{:S(2)}) async-start(bf16[8,24,1152]{2,1,0:T(8,128)(2,1)} %bitcast.19), calls=%async_computation.7 | async-start | bytes 884736 | tf_op jit(solution)/shard_map/all_to_all | solution.py:933
  386.6 6.6 %collective-permute-start.10 = (f32[16,768]{1,0:T(8,128)S(1)}, f32[16,768]{1,0:T(8,128)S(1)}, u32[]{:S(2)}, u32[]{:S(2)}) collective-permute-start(f32[16,768]{1,0:T(8,128)S(1)} %add.79), channel_id=1, source_target_pairs={{0,4},{4,0},{8,12},{12,8},{16,20},{20,16},{24,28},{28,24},{1,5},{5... | collective-permute-start | bytes 147464 | tf_op jit(solution)/shard_map/ppermute | solution.py:942
  393.2 4.3 collective-permute-start.11
  397.5 5.0 %collective-permute-start.12 = (f32[16,768]{1,0:T(8,128)S(1)}, f32[16,768]{1,0:T(8,128)S(1)}, u32[]{:S(2)}, u32[]{:S(2)}) collective-permute-start(f32[16,768]{1,0:T(8,128)S(1)} %add.81), channel_id=1, source_target_pairs={{0,16},{4,20},{8,24},{12,28},{16,0},{20,4},{24,8},{28,12},{1,17},{... | collective-permute-start | bytes 147464 | tf_op jit(solution)/shard_map/ppermute | solution.py:942
  403.5 21.8 %all-to-all-start.8 = ((bf16[8,24,1920]{2,1,0:T(8,128)(2,1)}), bf16[8,24,1920]{2,1,0:T(8,128)(2,1)S(1)}, u32[]{:S(2)}, u32[]{:S(2)}) async-start(bf16[8,24,1920]{2,1,0:T(8,128)(2,1)} %broadcast_in_dim.8), calls=%async_computation.8 | async-start | bytes 1474560 | tf_op jit(solution)/shard_map/all_to_all | solution.py:933
  425.3 12.5 %collective-permute-start.18 = (bf16[192,1920]{1,0:T(8,128)(2,1)S(1)}, bf16[192,1920]{1,0:T(8,128)(2,1)S(1)}, u32[]{:S(2)}, u32[]{:S(2)}) collective-permute-start(bf16[192,1920]{1,0:T(8,128)(2,1)S(1)} %bitcast.47), channel_id=1, source_target_pairs={{0,2},{1,3},{2,0},{3,1},{4,6},{5,7},{6,4},{7,5},{8,10},{9,11},{10,... | collective-permute-start | bytes 2211848 | tf_op jit(solution)/shard_map/ppermute | solution.py:942
  430.8 15.0 %all-to-all-start.9 = ((bf16[8,24,1152]{2,1,0:T(8,128)(2,1)}), bf16[8,24,1152]{2,1,0:T(8,128)(2,1)S(1)}, u32[]{:S(2)}, u32[]{:S(2)}) async-start(bf16[8,24,1152]{2,1,0:T(8,128)(2,1)} %broadcast_in_dim.9), calls=%async_computation.11 | async-start | bytes 884736 | tf_op jit(solution)/shard_map/all_to_all | solution.py:933
  434.4 12.7 %copy-start.24 = (f32[8]{0:T(128)S(1)}, f32[8]{0:T(128)}, u32[]{:S(2)}) copy-start(f32[8]{0:T(128)} %copy-done.23) | copy-start | bytes 100
  434.4 12.7 %copy-start.26 = (f32[8]{0:T(128)S(1)}, f32[8]{0:T(128)}, u32[]{:S(2)}) copy-start(f32[8]{0:T(128)} %copy-done.25) | copy-start | bytes 100
  438.2 16.4 %copy-start.3 = (bf16[384,1920]{1,0:T(8,128)(2,1)}, bf16[384,1920]{1,0:T(8,128)(2,1)S(1)}, u32[]{:S(2)}) copy-start(bf16[384,1920]{1,0:T(8,128)(2,1)S(1)} %maximum_select_fusion.own_ref) | copy-start | bytes 4423684
  438.2 16.4 %collective-permute-start.19 = (bf16[384,1920]{1,0:T(8,128)(2,1)S(1)}, bf16[384,1920]{1,0:T(8,128)(2,1)}, u32[]{:S(2)}, u32[]{:S(2)}) collective-permute-start(bf16[384,1920]{1,0:T(8,128)(2,1)S(1)} %maximum_select_fusion.own_ref), channel_id=1, source_target_pairs={{0,1},{1,0},{2,3},{3,2},{4,5},{5,4},{6,7},{7,6},{8,9},{9,8},{10,11... | collective-permute-start | bytes 4423688 | tf_op jit(solution)/shard_map/ppermute | solution.py:942
  445.9 8.3 %collective-permute-start.16 = (bf16[192,1152]{1,0:T(8,128)(2,1)S(1)}, bf16[192,1152]{1,0:T(8,128)(2,1)S(1)}, u32[]{:S(2)}, u32[]{:S(2)}) collective-permute-start(bf16[192,1152]{1,0:T(8,128)(2,1)S(1)} %bitcast.49), channel_id=1, source_target_pairs={{0,2},{1,3},{2,0},{3,1},{4,6},{5,7},{6,4},{7,5},{8,10},{9,11},{10,... | collective-permute-start | bytes 1327112 | tf_op jit(solution)/shard_map/ppermute | solution.py:942
  454.4 6.0 %copy-start.4 = (bf16[384,1152]{1,0:T(8,128)(2,1)}, bf16[384,1152]{1,0:T(8,128)(2,1)S(1)}, u32[]{:S(2)}) copy-start(bf16[384,1152]{1,0:T(8,128)(2,1)S(1)} %maximum_select_fusion.1.own_ref) | copy-start | bytes 2654212
  454.4 5.9 %collective-permute-start.17 = (bf16[384,1152]{1,0:T(8,128)(2,1)S(1)}, bf16[384,1152]{1,0:T(8,128)(2,1)S(1)}, u32[]{:S(2)}, u32[]{:S(2)}) collective-permute-start(bf16[384,1152]{1,0:T(8,128)(2,1)S(1)} %maximum_select_fusion.1.own_ref), channel_id=1, source_target_pairs={{0,1},{1,0},{2,3},{3,2},{4,5},{5,4},{6,7},{7,6},{8,9},{9,8},{10,11... | collective-permute-start | bytes 2654216 | tf_op jit(solution)/shard_map/ppermute | solution.py:942
  460.4 0.9 copy-start.27
Sparse Core Ops, SparseCore 0:
  9.6 40.1 all-gather.4
  51.3 37.4 all-gather.6
  276.0 63.3 reduce-scatter.2
  354.1 50.5 reduce-scatter.4
